TPU v7x, 32 devices: a whole 2x2x4 slice. The times are simulated.
32 devices in a mesh: dp: 4 (over y, core), fsdp: 8 (over z, x).
Axes of the slice: x: 2, y: 2, z: 4, core: 2. Of those that a mesh axis runs over, the one named last changes fastest.
Arguments:
- block_in: bfloat16 [160, 197, 768], P(('dp', 'fsdp')), may hold values from -6 to 6
- cotangent: bfloat16 [160, 197, 768], P(('dp', 'fsdp')), may hold values from -6 to 6
- image_live: int32 [160], P(('dp', 'fsdp')), may hold values from 0 to 1, as said below
- image_set: int32 [160], P(('dp', 'fsdp')), may hold values from 0 to 7
- expert_routes: int32 [160, 197, 2], P(('dp', 'fsdp')), may hold values from 0 to 7, as said below
- expert_slots: int32 [160, 197, 2], P(('dp', 'fsdp')), may hold values from -1 to 383, as said below
- gain_attn: bfloat16 [768], P(('dp', 'fsdp')), may hold values from 0.099609375 to 1.8984375
- gain_moe: bfloat16 [768], P(('dp', 'fsdp')), may hold values from 0.099609375 to 1.8984375
- w_qkv: bfloat16 [768, 2304], P(('dp', 'fsdp')), may hold values from -0.21875 to 0.21875
- w_out: bfloat16 [768, 768], P(('dp', 'fsdp')), may hold values from -0.875 to 0.875
- w_router: bfloat16 [768, 8], P(('dp', 'fsdp')), may hold values from -0.109375 to 0.109375
- w_up: bfloat16 [8, 768, 3072], P(None, None, ('dp', 'fsdp')), may hold values from -0.21875 to 0.21875
- w_down: bfloat16 [8, 768, 3072], P(None, None, ('dp', 'fsdp')), may hold values from -0.875 to 0.875
- qkv_adapter_first: bfloat16 [768, 128], P(('dp', 'fsdp')), may hold values from -0.21875 to 0.21875
- qkv_adapter_second: bfloat16 [128, 2304], P(None, ('dp', 'fsdp')), may hold values from -2 to 2
- output_adapter_first: bfloat16 [768, 128], P(('dp', 'fsdp')), may hold values from -0.875 to 0.875
- output_adapter_second: bfloat16 [128, 768], P(None, ('dp', 'fsdp')), may hold values from -2 to 2
- router_adapter_first: bfloat16 [768, 128], P(('dp', 'fsdp')), may hold values from -0.21875 to 0.21875
- router_adapter_second: bfloat16 [1024], P(('dp', 'fsdp')), may hold values from -1 to 1
- up_adapter_first: bfloat16 [8, 768, 128], P(None, ('dp', 'fsdp')), may hold values from -0.21875 to 0.21875
- up_adapter_second: bfloat16 [8, 128, 3072], P(None, None, ('dp', 'fsdp')), may hold values from -2 to 2
- down_adapter_first: bfloat16 [8, 128, 3072], P(None, None, ('dp', 'fsdp')), may hold values from -0.109375 to 0.109375
- down_adapter_second: bfloat16 [8, 128, 768], P(None, None, ('dp', 'fsdp')), may hold values from -6 to 6
Outputs:
- block_out: bfloat16 [160, 197, 768], P(('dp', 'fsdp'))
- input_grad: bfloat16 [160, 197, 768], P(('dp', 'fsdp'))
- grad_qkv_down: float32 [768, 128], P(('dp', 'fsdp'))
- grad_qkv_up: float32 [128, 2304], P(None, ('dp', 'fsdp'))
- grad_out_down: float32 [768, 128], P(('dp', 'fsdp'))
- grad_out_up: float32 [128, 768], P(None, ('dp', 'fsdp'))
- grad_router_down: float32 [768, 128], P(('dp', 'fsdp'))
- router_second_gradient: float32 [1024], P(('dp', 'fsdp'))
- grad_up_down: float32 [8, 768, 128], P(None, ('dp', 'fsdp'))
- grad_up_up: float32 [8, 128, 3072], P(None, None, ('dp', 'fsdp'))
- grad_down_down: float32 [8, 128, 3072], P(None, None, ('dp', 'fsdp'))
- grad_down_up: float32 [8, 128, 768], P(None, None, ('dp', 'fsdp'))
Inputs may be any that keep to these rules, and one draw needn't show every extreme that they name: `expert_routes`: A token's two experts differ. In each device's block of 985 tokens some expert is named by 384 or more of them. `expert_slots`: within each device's block of 985 tokens, taken token by token and, inside a token, choice by choice, the choices that name one expert get slots 0, 1, 2, ... in turn; a choice past slot 383 gets -1. Each (expert, slot) pair is used at most once in a block, and slot 383 is used in every block. `image_live`: in each device's block of 5 image slots the live ones come first and at least one is live; some block is all live.
All inputs are finite; a program needn't handle non-finite values.
Results may differ from a plain program's by a relative error of at most 0.018.
Values may be sent and summed in bfloat16 or wider, within the bound.
No kernel may reach another device: no remote copies, remote signals or barrier semaphores. Data moves between devices by JAX's collectives and lax.ppermute only.
A program may use at most 448 MiB of HBM per device.

v0:
```python
import math

import jax
import jax.numpy as jnp
from jax import lax
from jax.sharding import PartitionSpec as P

MODEL_WIDTH = 768
HEADS = 12
HEAD = 64
EXPERT_COUNT = 8
LENGTH = 197
ADAPTER_SETS = 8
ADAPTER_RANK = 16
CAP = 384


EPS = 1e-06


def product_plain(first_mat, second_mat):
    return jnp.dot(first_mat, second_mat, preferred_element_type=jnp.float32)


def product_right(first_mat, second_mat):
    return lax.dot_general(
        first_mat, second_mat, (((1,), (1,)), ((), ())), preferred_element_type=jnp.float32
    )


def product_left(first_mat, second_mat):
    return lax.dot_general(
        first_mat, second_mat, (((0,), (0,)), ((), ())), preferred_element_type=jnp.float32
    )


def norm_forward(values, gain_vec):
    mean_val = jnp.mean(values, axis=-1, keepdims=True)
    centered = values - mean_val
    variance = jnp.mean(centered * centered, axis=-1, keepdims=True)
    inverse = lax.rsqrt(variance + EPS)
    unit_rows = centered * inverse
    return (unit_rows * gain_vec.astype(jnp.float32), unit_rows, inverse)


def norm_backward(grad_rows, unit_rows, inverse, gain_vec):
    scaled = grad_rows * gain_vec.astype(jnp.float32)
    return inverse * (
        scaled
        - jnp.mean(scaled, axis=-1, keepdims=True)
        - unit_rows * jnp.mean(scaled * unit_rows, axis=-1, keepdims=True)
    )


def on_device(
    block_in,
    cotangent,
    image_live,
    image_set,
    expert_routes,
    expert_slots,
    gain_attn,
    gain_moe,
    w_qkv,
    w_out,
    w_router,
    w_up,
    w_down,
    qkv_adapter_first,
    qkv_adapter_second,
    output_adapter_first,
    output_adapter_second,
    router_adapter_first,
    router_adapter_second,
    up_adapter_first,
    up_adapter_second,
    down_adapter_first,
    down_adapter_second,
):
    single_float = jnp.float32
    brain_float_half = jnp.bfloat16
    images = block_in.shape[0]
    tok_count = images * LENGTH
    adapter_column_ids = ADAPTER_SETS * ADAPTER_RANK
    slot_total = EXPERT_COUNT * CAP
    front = (
        lax.all_gather(gain_attn, ("dp", "fsdp"), axis=0, tiled=True),
        lax.all_gather(gain_moe, ("dp", "fsdp"), axis=0, tiled=True),
        lax.all_gather(w_qkv, ("dp", "fsdp"), axis=0, tiled=True),
        lax.all_gather(w_out, ("dp", "fsdp"), axis=0, tiled=True),
        lax.all_gather(w_router, ("dp", "fsdp"), axis=0, tiled=True),
        lax.all_gather(qkv_adapter_first, ("dp", "fsdp"), axis=0, tiled=True),
        lax.all_gather(qkv_adapter_second, ("dp", "fsdp"), axis=1, tiled=True),
        lax.all_gather(output_adapter_first, ("dp", "fsdp"), axis=0, tiled=True),
        lax.all_gather(output_adapter_second, ("dp", "fsdp"), axis=1, tiled=True),
        lax.all_gather(router_adapter_first, ("dp", "fsdp"), axis=0, tiled=True),
        lax.all_gather(router_adapter_second, ("dp", "fsdp"), axis=0, tiled=True),
        lax.all_gather(up_adapter_first, ("dp", "fsdp"), axis=1, tiled=True),
        lax.all_gather(down_adapter_second, ("dp", "fsdp"), axis=2, tiled=True),
    )
    (
        gain_one,
        gain_two,
        qkv_full,
        outw_full,
        router_full,
        qkv_first_whole,
        qkvu_full,
        output_first_whole,
        outu_full,
        router_first_whole,
        router_second_whole,
        upd_full,
        downu_full,
    ) = front
    hidden = block_in.reshape(tok_count, MODEL_WIDTH).astype(single_float)
    token_adapter_set = jnp.repeat(image_set, LENGTH)
    column_indices = jnp.arange(adapter_column_ids, dtype=jnp.int32) // ADAPTER_RANK
    adapter_column_mask = (token_adapter_set[:, None] == column_indices[None, :]).astype(
        single_float
    )
    live_tok = jnp.repeat(image_live, LENGTH).astype(single_float)[:, None]
    normed_one, unit_one, inverse_one = norm_forward(hidden, gain_one)
    first_input = normed_one.astype(brain_float_half)
    qkv_adapter_delta = (adapter_column_mask * product_plain(first_input, qkv_first_whole)).astype(
        brain_float_half
    )
    qkv = (
        product_plain(first_input, qkv_full) + product_plain(qkv_adapter_delta, qkvu_full)
    ).astype(brain_float_half)
    qkv_heads = qkv.reshape(images, LENGTH, 3, HEADS, HEAD)
    queries = qkv_heads[:, :, 0]
    key_rows = qkv_heads[:, :, 1]
    values = qkv_heads[:, :, 2]
    score_scale = 1.0 / math.sqrt(HEAD)
    scores = score_scale * jnp.einsum(
        "bqhd,bkhd->bhqk", queries, key_rows, preferred_element_type=single_float
    )
    log_total = jax.nn.logsumexp(scores, axis=-1, keepdims=True)
    attn_probs = jnp.exp(scores - log_total)
    attention_output = (
        jnp.einsum(
            "bhqk,bkhd->bqhd",
            attn_probs.astype(brain_float_half),
            values,
            preferred_element_type=single_float,
        )
        .reshape(tok_count, MODEL_WIDTH)
        .astype(brain_float_half)
    )
    output_adapter_delta = (
        adapter_column_mask * product_plain(attention_output, output_first_whole)
    ).astype(brain_float_half)
    middle = (
        hidden
        + product_plain(attention_output, outw_full)
        + product_plain(output_adapter_delta, outu_full)
    )
    normed_two, unit_two, inverse_two = norm_forward(middle, gain_two)
    second_input = normed_two.astype(brain_float_half)
    router_adapter_delta = (
        adapter_column_mask * product_plain(second_input, router_first_whole)
    ).astype(brain_float_half)
    router_matrix = router_second_whole.reshape(adapter_column_ids, EXPERT_COUNT)
    logits = product_plain(second_input, router_full) + product_plain(
        router_adapter_delta, router_matrix
    )
    router_probs = jax.nn.softmax(logits, axis=-1)
    route_tok = expert_routes.reshape(tok_count, 2)
    slot_tok = expert_slots.reshape(tok_count, 2)
    is_kept = (slot_tok >= 0).astype(single_float)
    target = jnp.where(slot_tok >= 0, route_tok * CAP + slot_tok, slot_total)
    choose = (route_tok[:, :, None] == jnp.arange(EXPERT_COUNT, dtype=jnp.int32)).astype(
        single_float
    )
    gate_values = jnp.sum(choose * router_probs[:, None, :], axis=2) * is_kept
    token_ids = jnp.repeat(jnp.arange(tok_count, dtype=jnp.int32), 2)
    slot_owner = (
        jnp.full((slot_total + 1,), tok_count, jnp.int32)
        .at[target.reshape(-1)]
        .set(token_ids)[:slot_total]
    )
    expert_in = jnp.concatenate(
        [second_input, jnp.zeros((1, MODEL_WIDTH), brain_float_half)], axis=0
    )[slot_owner].reshape(EXPERT_COUNT, CAP, MODEL_WIDTH)
    row_set = jnp.concatenate([token_adapter_set, jnp.full((1,), -1, jnp.int32)], axis=0)[
        slot_owner
    ].reshape(EXPERT_COUNT, CAP)
    row_mask = (row_set[..., None] == column_indices).astype(single_float)
    adapt_u = (
        row_mask
        * jnp.einsum("ecd,edr->ecr", expert_in, upd_full, preferred_element_type=single_float)
    ).astype(brain_float_half)
    up_piece = lax.all_gather(w_up, ("dp", "fsdp"), axis=2, tiled=True)
    upa_piece = lax.all_gather(up_adapter_second, ("dp", "fsdp"), axis=2, tiled=True)
    down_piece = lax.all_gather(w_down, ("dp", "fsdp"), axis=2, tiled=True)
    downa_piece = lax.all_gather(down_adapter_first, ("dp", "fsdp"), axis=2, tiled=True)
    pre_gelu = jnp.einsum(
        "ecd,edf->ecf", expert_in, up_piece, preferred_element_type=single_float
    ) + jnp.einsum("ecr,erf->ecf", adapt_u, upa_piece, preferred_element_type=single_float)
    active = jax.nn.gelu(pre_gelu).astype(brain_float_half)
    summed = jnp.einsum("ecf,edf->ecd", active, down_piece, preferred_element_type=single_float)
    adapt_sum = jnp.einsum("ecf,erf->ecr", active, downa_piece, preferred_element_type=single_float)
    summed, adapt_sum = (summed, adapt_sum)
    adapt_d = (row_mask * adapt_sum).astype(brain_float_half)
    expert_out = summed + jnp.einsum(
        "ecr,erd->ecd", adapt_d, downu_full, preferred_element_type=single_float
    )
    flat_out = jnp.concatenate(
        [expert_out.reshape(slot_total, MODEL_WIDTH), jnp.zeros((1, MODEL_WIDTH), single_float)],
        axis=0,
    )
    picked = flat_out[target]
    block_sum = (middle + jnp.sum(gate_values[..., None] * picked, axis=1)) * live_tok
    block_out = block_sum.astype(brain_float_half).reshape(images, LENGTH, MODEL_WIDTH)
    back = (
        lax.all_gather(gain_attn, ("dp", "fsdp"), axis=0, tiled=True),
        lax.all_gather(gain_moe, ("dp", "fsdp"), axis=0, tiled=True),
        lax.all_gather(w_qkv, ("dp", "fsdp"), axis=0, tiled=True),
        lax.all_gather(w_out, ("dp", "fsdp"), axis=0, tiled=True),
        lax.all_gather(w_router, ("dp", "fsdp"), axis=0, tiled=True),
        lax.all_gather(qkv_adapter_first, ("dp", "fsdp"), axis=0, tiled=True),
        lax.all_gather(qkv_adapter_second, ("dp", "fsdp"), axis=1, tiled=True),
        lax.all_gather(output_adapter_first, ("dp", "fsdp"), axis=0, tiled=True),
        lax.all_gather(output_adapter_second, ("dp", "fsdp"), axis=1, tiled=True),
        lax.all_gather(router_adapter_first, ("dp", "fsdp"), axis=0, tiled=True),
        lax.all_gather(router_adapter_second, ("dp", "fsdp"), axis=0, tiled=True),
        lax.all_gather(up_adapter_first, ("dp", "fsdp"), axis=1, tiled=True),
        lax.all_gather(down_adapter_second, ("dp", "fsdp"), axis=2, tiled=True),
    )
    (
        gain_one_bk,
        gain_two_bk,
        qkv_bk,
        outw_bk,
        router_bk,
        qkvd_bk,
        qkv_second_backward,
        outd_bk,
        output_second_backward,
        routerd_bk,
        router_second_backward,
        upd_bk,
        downu_bk,
    ) = back
    router_matrix_backward = router_second_backward.reshape(adapter_column_ids, EXPERT_COUNT)
    grad_final = cotangent.reshape(tok_count, MODEL_WIDTH).astype(single_float) * live_tok
    grad_gate = jnp.sum(grad_final[:, None, :] * picked, axis=2) * is_kept
    grad_probs = jnp.sum(grad_gate[..., None] * choose, axis=1)
    logits_gradient = (
        router_probs * (grad_probs - jnp.sum(grad_probs * router_probs, axis=-1, keepdims=True))
    ).astype(brain_float_half)
    slot_gate = (
        jnp.zeros((slot_total + 1,), single_float)
        .at[target.reshape(-1)]
        .set(gate_values.reshape(-1))[:slot_total]
    )
    grad_rows_pad = jnp.concatenate([grad_final, jnp.zeros((1, MODEL_WIDTH), single_float)], axis=0)
    grad_expert = (
        (slot_gate[:, None] * grad_rows_pad[slot_owner])
        .reshape(EXPERT_COUNT, CAP, MODEL_WIDTH)
        .astype(brain_float_half)
    )
    grad_down_up = jnp.einsum(
        "ecr,ecd->erd", adapt_d, grad_expert, preferred_element_type=single_float
    )
    grad_adapt_d = (
        row_mask
        * jnp.einsum("ecd,erd->ecr", grad_expert, downu_bk, preferred_element_type=single_float)
    ).astype(brain_float_half)
    up_piece = lax.all_gather(w_up, ("dp", "fsdp"), axis=2, tiled=True)
    upa_piece = lax.all_gather(up_adapter_second, ("dp", "fsdp"), axis=2, tiled=True)
    down_piece = lax.all_gather(w_down, ("dp", "fsdp"), axis=2, tiled=True)
    downa_piece = lax.all_gather(down_adapter_first, ("dp", "fsdp"), axis=2, tiled=True)
    pre_gelu = jnp.einsum(
        "ecd,edf->ecf", expert_in, up_piece, preferred_element_type=single_float
    ) + jnp.einsum("ecr,erf->ecf", adapt_u, upa_piece, preferred_element_type=single_float)
    active, gelu_back = jax.vjp(jax.nn.gelu, pre_gelu)
    active_low = active.astype(brain_float_half)
    grad_active = jnp.einsum(
        "ecd,edf->ecf", grad_expert, down_piece, preferred_element_type=single_float
    ) + jnp.einsum("ecr,erf->ecf", grad_adapt_d, downa_piece, preferred_element_type=single_float)
    grad_pre = gelu_back(grad_active)[0].astype(brain_float_half)
    piece_downa = jnp.einsum(
        "ecr,ecf->erf", grad_adapt_d, active_low, preferred_element_type=single_float
    )
    piece_upa = jnp.einsum("ecr,ecf->erf", adapt_u, grad_pre, preferred_element_type=single_float)
    grad_in = jnp.einsum("ecf,edf->ecd", grad_pre, up_piece, preferred_element_type=single_float)
    grad_adapt = jnp.einsum(
        "ecf,erf->ecr", grad_pre, upa_piece, preferred_element_type=single_float
    )
    expert_grads = (grad_in, grad_adapt, piece_downa, piece_upa)
    grad_in, grad_adapt, grad_down_down, grad_up_up = expert_grads
    grad_adapt_u = (row_mask * grad_adapt).astype(brain_float_half)
    grad_in = grad_in + jnp.einsum(
        "ecr,edr->ecd", grad_adapt_u, upd_bk, preferred_element_type=single_float
    )
    grad_up_down = jnp.einsum(
        "ecd,ecr->edr", expert_in, grad_adapt_u, preferred_element_type=single_float
    )
    grad_two = (
        jnp.zeros((tok_count + 1, MODEL_WIDTH), single_float)
        .at[slot_owner]
        .add(grad_in.reshape(slot_total, MODEL_WIDTH))[:tok_count]
    )
    router_adapter_gradient = (
        adapter_column_mask * product_right(logits_gradient, router_matrix_backward)
    ).astype(brain_float_half)
    router_second_gradient = product_left(router_adapter_delta, logits_gradient).reshape(
        adapter_column_ids * EXPERT_COUNT
    )
    grad_router_down = product_left(second_input, router_adapter_gradient)
    grad_two = (
        grad_two
        + product_right(logits_gradient, router_bk)
        + product_right(router_adapter_gradient, routerd_bk)
    )
    grad_middle = grad_final + norm_backward(grad_two, unit_two, inverse_two, gain_two_bk)
    branch_gradient = grad_middle.astype(brain_float_half)
    grad_out_up = product_left(output_adapter_delta, branch_gradient)
    output_adapter_gradient = (
        adapter_column_mask * product_right(branch_gradient, output_second_backward)
    ).astype(brain_float_half)
    grad_out_down = product_left(attention_output, output_adapter_gradient)
    grad_attended = (
        (product_right(branch_gradient, outw_bk) + product_right(output_adapter_gradient, outd_bk))
        .astype(brain_float_half)
        .reshape(images, LENGTH, HEADS, HEAD)
    )
    scores_again = score_scale * jnp.einsum(
        "bqhd,bkhd->bhqk", queries, key_rows, preferred_element_type=single_float
    )
    probs_again = jnp.exp(scores_again - log_total)
    grad_attn = jnp.einsum(
        "bqhd,bkhd->bhqk", grad_attended, values, preferred_element_type=single_float
    )
    grad_values = jnp.einsum(
        "bhqk,bqhd->bkhd",
        probs_again.astype(brain_float_half),
        grad_attended,
        preferred_element_type=single_float,
    )
    grad_scores = (
        probs_again * (grad_attn - jnp.sum(grad_attn * probs_again, axis=-1, keepdims=True))
    ).astype(brain_float_half)
    grad_queries = score_scale * jnp.einsum(
        "bhqk,bkhd->bqhd", grad_scores, key_rows, preferred_element_type=single_float
    )
    grad_keys = score_scale * jnp.einsum(
        "bhqk,bqhd->bkhd", grad_scores, queries, preferred_element_type=single_float
    )
    qkv_gradient = (
        jnp.stack([grad_queries, grad_keys, grad_values], axis=2)
        .reshape(tok_count, 3 * MODEL_WIDTH)
        .astype(brain_float_half)
    )
    grad_qkv_up = product_left(qkv_adapter_delta, qkv_gradient)
    qkv_adapter_gradient = (
        adapter_column_mask * product_right(qkv_gradient, qkv_second_backward)
    ).astype(brain_float_half)
    grad_qkv_down = product_left(first_input, qkv_adapter_gradient)
    grad_one = product_right(qkv_gradient, qkv_bk) + product_right(qkv_adapter_gradient, qkvd_bk)
    grad_hidden = grad_middle + norm_backward(grad_one, unit_one, inverse_one, gain_one_bk)
    input_grad = grad_hidden.astype(brain_float_half).reshape(images, LENGTH, MODEL_WIDTH)
    shards = (
        lax.psum_scatter(grad_qkv_down, ("dp", "fsdp"), scatter_dimension=0, tiled=True),
        lax.psum_scatter(grad_qkv_up, ("dp", "fsdp"), scatter_dimension=1, tiled=True),
        lax.psum_scatter(grad_out_down, ("dp", "fsdp"), scatter_dimension=0, tiled=True),
        lax.psum_scatter(grad_out_up, ("dp", "fsdp"), scatter_dimension=1, tiled=True),
        lax.psum_scatter(grad_router_down, ("dp", "fsdp"), scatter_dimension=0, tiled=True),
        lax.psum_scatter(router_second_gradient, ("dp", "fsdp"), scatter_dimension=0, tiled=True),
        lax.psum_scatter(grad_up_down, ("dp", "fsdp"), scatter_dimension=1, tiled=True),
        lax.psum_scatter(grad_up_up, ("dp", "fsdp"), scatter_dimension=2, tiled=True),
        lax.psum_scatter(grad_down_down, ("dp", "fsdp"), scatter_dimension=2, tiled=True),
        lax.psum_scatter(grad_down_up, ("dp", "fsdp"), scatter_dimension=2, tiled=True),
    )
    return (
        block_out,
        input_grad,
        shards[0],
        shards[1],
        shards[2],
        shards[3],
        shards[4],
        shards[5],
        shards[6],
        shards[7],
        shards[8],
        shards[9],
    )


def solution(mesh):
    return jax.shard_map(
        on_device,
        mesh=mesh,
        in_specs=(
            P(("dp", "fsdp"), None, None),
            P(("dp", "fsdp"), None, None),
            P(("dp", "fsdp")),
            P(("dp", "fsdp")),
            P(("dp", "fsdp"), None, None),
            P(("dp", "fsdp"), None, None),
            P(("dp", "fsdp")),
            P(("dp", "fsdp")),
            P(("dp", "fsdp"), None),
            P(("dp", "fsdp"), None),
            P(("dp", "fsdp"), None),
            P(None, None, ("dp", "fsdp")),
            P(None, None, ("dp", "fsdp")),
            P(("dp", "fsdp"), None),
            P(None, ("dp", "fsdp")),
            P(("dp", "fsdp"), None),
            P(None, ("dp", "fsdp")),
            P(("dp", "fsdp"), None),
            P(("dp", "fsdp")),
            P(None, ("dp", "fsdp"), None),
            P(None, None, ("dp", "fsdp")),
            P(None, None, ("dp", "fsdp")),
            P(None, None, ("dp", "fsdp")),
        ),
        out_specs=(
            P(("dp", "fsdp"), None, None),
            P(("dp", "fsdp"), None, None),
            P(("dp", "fsdp"), None),
            P(None, ("dp", "fsdp")),
            P(("dp", "fsdp"), None),
            P(None, ("dp", "fsdp")),
            P(("dp", "fsdp"), None),
            P(("dp", "fsdp")),
            P(None, ("dp", "fsdp"), None),
            P(None, None, ("dp", "fsdp")),
            P(None, None, ("dp", "fsdp")),
            P(None, None, ("dp", "fsdp")),
        ),
        check_vma=False,
    )
```

profile of v0, /device:TPU:0, one launch (start us, length us, event | category | flops | bytes accessed | tf_op | source)
XLA Modules:
  0.0 2137.9 jit_solution(7674811183276227096)
XLA Ops:
  16.2 42.1 %all-reduce.12 = (bf16[768]{0:T(1024)(128)(2,1)S(1)}, bf16[768]{0:T(1024)(128)(2,1)S(1)}, bf16[1024]{0:T(1024)(128)(2,1)S(1)}) all-reduce(bf16[768]{0:T(1024)(128)(2,1)S(1)} %dynamic-update-slice, bf16[768]{0:T(1024)(128)(2,1)S(1)} %dynamic-update-slice.1, ...), channel_id=1, replica_groups=mesh['dp'=4,'fsdp'=8] {'dp','fsdp'}, use_global_device_ids=true, to_apply=%add.3 | all-reduce | flops 2560 | bytes 10240
  64.6 66.2 %all-gather = bf16[32,24,8]{1,2,0:T(8,128)(2,1)S(1)} all-gather(bf16[1,24,8]{1,2,0:T(8,128)(2,1)S(1)} %bitcast.152), channel_id=1, replica_groups=mesh['dp'=4,'fsdp'=8] {'dp','fsdp'}, dimensions={0}, use_global_device_ids=true | all-gather | bytes 12672 | tf_op jit(solution)/shard_map/all_gather | solution.py:91
  149.8 13.8 gather_fusion.3
  189.7 65.5 %all_gather.70 = bf16[768,128]{1,0:T(8,128)(2,1)S(1)} all-gather(bf16[24,128]{1,0:T(8,128)(2,1)} %param.36), channel_id=1, replica_groups=mesh['dp'=4,'fsdp'=8] {'dp','fsdp'}, dimensions={0}, use_global_device_ids=true | all-gather | bytes 202752 | tf_op jit(solution)/shard_map/all_gather | solution.py:92
  255.1 72.6 %all_gather.73 = bf16[768,128]{1,0:T(8,128)(2,1)} all-gather(bf16[24,128]{1,0:T(8,128)(2,1)} %param.38), channel_id=1, replica_groups=mesh['dp'=4,'fsdp'=8] {'dp','fsdp'}, dimensions={0}, use_global_device_ids=true | all-gather | bytes 202752 | tf_op jit(solution)/shard_map/all_gather | solution.py:94
  327.7 65.8 %all_gather.74 = bf16[128,768]{0,1:T(8,128)(2,1)S(1)} all-gather(bf16[128,24]{0,1:T(8,128)(2,1)} %param.39), channel_id=1, replica_groups=mesh['dp'=4,'fsdp'=8] {'dp','fsdp'}, dimensions={1}, use_global_device_ids=true | all-gather | bytes 202752 | tf_op jit(solution)/shard_map/all_gather | solution.py:95
  393.5 74.6 %all_gather.77 = bf16[768,128]{1,0:T(8,128)(2,1)} all-gather(bf16[24,128]{1,0:T(8,128)(2,1)} %param.40), channel_id=1, replica_groups=mesh['dp'=4,'fsdp'=8] {'dp','fsdp'}, dimensions={0}, use_global_device_ids=true | all-gather | bytes 202752 | tf_op jit(solution)/shard_map/all_gather | solution.py:96
  472.2 78.0 %all_gather.71 = bf16[128,2304]{0,1:T(8,128)(2,1)} all-gather(bf16[128,72]{0,1:T(8,128)(2,1)S(1)} %copy-done.71), channel_id=1, replica_groups=mesh['dp'=4,'fsdp'=8] {'dp','fsdp'}, dimensions={1}, use_global_device_ids=true | all-gather | bytes 608256 | tf_op jit(solution)/shard_map/all_gather | solution.py:93
  560.0 14.6 reshape.412
  617.7 16.4 convert_element_type.137
  654.7 13.6 gather_fusion
  685.2 18.0 fusion.62
  703.2 19.8 fusion.64
  722.9 48.7 %multiply_convert_fusion = (bf16[8,384,3072]{2,1,0:T(8,128)(2,1)}, f32[8,384,3072]{2,1,0:T(8,128)}) fusion(f32[8,384,3072]{2,1,0:T(8,128)} %fusion.62, bf16[8,384,768]{2,1,0:T(8,128)(2,1)} %bitcast.147, bf16[8,768,3072]{1,2,0:T(8,128)(2,1)} %all-gather.14.cloned.1.call-done), kind=kOutput, calls=%fused_computation.16 | convolution fusion | flops 14589886464 | bytes 136839168 | tf_op jit(solution)/shard_map/ecd,edf->ecf/dot_general | solution.py:198
  782.8 47.2 %all-gather.20.cloned.1.call-done = bf16[8,768,3072]{1,2,0:T(8,128)(2,1)} async-done(((bf16[8,768,96]{1,2,0:T(8,128)(2,1)}), bf16[8,768,3072]{1,2,0:T(8,128)(2,1)}) %all-gather.20.cloned.1.call-update) | async-done | bytes 37748752 | tf_op jit(solution)/shard_map/all_gather | solution.py:196
  830.0 26.6 %fusion.63 = f32[8,384,768]{2,1,0:T(8,128)} fusion(bf16[8,384,3072]{2,1,0:T(8,128)(2,1)} %get-tuple-element.34, bf16[8,768,3072]{1,2,0:T(8,128)(2,1)} %all-gather.20.cloned.1.call-done), kind=kOutput, calls=%fused_computation.140 | convolution fusion | flops 14495514624 | bytes 66060288 | tf_op jit(solution)/shard_map/ecf,edf->ecd/dot_general | solution.py:202
  865.9 14.4 gather_fusion.2
  888.4 16.7 multiply_reduce_fusion.2
  914.3 58.6 %fusion.6 = bf16[8,384,3072]{2,1,0:T(8,128)(2,1)} fusion(f32[8,384,3072]{2,1,0:T(8,128)} %fusion.64, f32[8,384,3072]{2,1,0:T(8,128)} %get-tuple-element.35, f32[8,384,3072]{2,1,0:T(8,128)} %fusion.62, bf16[8,384,768]{1,2,0:T(8,128)(2,1)} %multiply_convert_fusion.2, bf16[8,768,3072]{1,2,0:T(8,128)(2,1)} %all-gather.20.cloned.1.call-done), kind=kOutput, calls=%fused_computation.15 | convolution fusion | flops 14703132672 | bytes 174587904 | tf_op jit(solution)/shard_map/ecd,edf->ecf/dot_general | solution.py:280
  972.9 27.0 %fusion.65 = f32[8,384,768]{2,1,0:T(8,128)} fusion(bf16[8,384,3072]{2,1,0:T(8,128)(2,1)} %fusion.6, bf16[8,768,3072]{1,2,0:T(8,128)(2,1)} %all-gather.14.cloned.1.call-done), kind=kOutput, calls=%fused_computation.142 | convolution fusion | flops 14495514624 | bytes 66060288 | tf_op jit(solution)/shard_map/ecf,edf->ecd/dot_general | solution.py:288
  1016.3 23.6 %scatter_custom_fusion.2 = f32[986,768]{1,0:T(8,128)} fusion(s32[3072]{0:T(1024)} %get-tuple-element.26, f32[3072,768]{1,0:T(8,128)} %bitcast.149, f32[]{:T(128)} %constant.66.clone.1), kind=kCustom, calls=%fused_computation.71 | custom fusion | flops 2359296 | bytes 3029504 | tf_op jit(solution)/shard_map/scatter-add | solution.py:304
  1065.4 13.3 multiply_reduce_fusion
  1118.7 13.8 convert_element_type.160
  1201.3 38.4 %all-reduce.11 = f32[1024]{0:T(1024)S(1)} all-reduce(f32[1024]{0:T(1024)S(1)} %reshape.340), channel_id=7, replica_groups=mesh['dp'=4,'fsdp'=8] {'dp','fsdp'}, use_global_device_ids=true, to_apply=%region_26.27.clone | all-reduce | flops 1024 | bytes 8192
  1240.3 53.6 %reduce-scatter.32.cloned.1.call-done = f32[24,128]{1,0:T(8,128)} async-done(((f32[768,128]{1,0:T(8,128)}), f32[24,128]{1,0:T(8,128)}) %reduce-scatter.32.cloned.1.call-update) | async-done | bytes 12304
  1293.9 99.5 %reduce-scatter.28.cloned.1.call-done = f32[24,128]{1,0:T(8,128)} async-done(((f32[768,128]{1,0:T(8,128)}), f32[24,128]{1,0:T(8,128)}) %reduce-scatter.28.cloned.1.call-update) | async-done | bytes 12304
  1393.4 100.1 %reduce-scatter.36.cloned.1.call-done = f32[24,128]{1,0:T(8,128)} async-done(((f32[768,128]{1,0:T(8,128)}), f32[24,128]{1,0:T(8,128)}) %reduce-scatter.36.cloned.1.call-update) | async-done | bytes 12304
  1493.5 101.0 %reduce-scatter.30.cloned.1.call-done = f32[128,72]{0,1:T(8,128)} async-done(((f32[128,2304]{0,1:T(8,128)}), f32[128,72]{0,1:T(8,128)}) %reduce-scatter.30.cloned.1.call-update) | async-done | bytes 36880
  1594.5 106.5 %reduce-scatter.26.cloned.1.call-done = f32[8,128,24]{1,2,0:T(8,128)} async-done(((f32[8,128,768]{1,2,0:T(8,128)}), f32[8,128,24]{1,2,0:T(8,128)}) %reduce-scatter.26.cloned.1.call-update) | async-done | bytes 98320 | tf_op jit(solution)/shard_map/reduce_scatter | solution.py:375
  1701.0 106.4 %reduce-scatter.20.cloned.1.call-done = f32[8,24,128]{2,1,0:T(8,128)} async-done(((f32[8,768,128]{2,1,0:T(8,128)}), f32[8,24,128]{2,1,0:T(8,128)}) %reduce-scatter.20.cloned.1.call-update) | async-done | bytes 98320 | tf_op jit(solution)/shard_map/reduce_scatter | solution.py:372
  1807.5 161.2 %reduce-scatter.24.cloned.1.call-done = f32[8,128,96]{1,2,0:T(8,128)} async-done(((f32[8,128,3072]{1,2,0:T(8,128)}), f32[8,128,96]{1,2,0:T(8,128)}) %reduce-scatter.24.cloned.1.call-update) | async-done | bytes 393232 | tf_op jit(solution)/shard_map/reduce_scatter | solution.py:374
  1968.6 162.3 %reduce-scatter.22.cloned.1.call-done = f32[8,128,96]{1,2,0:T(8,128)} async-done(((f32[8,128,3072]{1,2,0:T(8,128)}), f32[8,128,96]{1,2,0:T(8,128)}) %reduce-scatter.22.cloned.1.call-update) | async-done | bytes 393232 | tf_op jit(solution)/shard_map/reduce_scatter | solution.py:373
  (355 shorter events, 342.3 us)
Async XLA Ops:
  7.2 51.7 %copy-start.15 = (bf16[5,197,768]{2,1,0:T(8,128)(2,1)S(1)}, bf16[5,197,768]{2,1,0:T(8,128)(2,1)}, u32[]{:S(2)}) copy-start(bf16[5,197,768]{2,1,0:T(8,128)(2,1)} %param.23) | copy-start | bytes 4538884
  7.2 543.1 %all-gather.10.cloned.1.call-start = ((), (), s32[]{:S(2)}) async-start(), calls=%async_computation.9 | async-start | bytes 3649536 | tf_op jit(solution)/shard_map/all_gather | solution.py:89
  8.0 628.3 %all-gather.12.cloned.1.call-start = ((), (), s32[]{:S(2)}) async-start(), calls=%async_computation.10 | async-start | bytes 1216512 | tf_op jit(solution)/shard_map/all_gather | solution.py:90
  8.7 667.3 %all-gather.24.cloned.1.call-start = ((), (), s32[]{:S(2)}) async-start(), calls=%async_computation.16 | async-start | bytes 1622016 | tf_op jit(solution)/shard_map/all_gather | solution.py:99
  9.4 671.2 %all-gather.16.cloned.1.call-start = ((), (), s32[]{:S(2)}) async-start(), calls=%async_computation.12 | async-start | bytes 1622016 | tf_op jit(solution)/shard_map/all_gather | solution.py:98
  10.0 675.1 %all-gather.18.cloned.1.call-start = ((), (), s32[]{:S(2)}) async-start(), calls=%async_computation.13 | async-start | bytes 6488064 | tf_op jit(solution)/shard_map/all_gather | solution.py:195
  10.6 692.6 %all-gather.22.cloned.1.call-start = ((), (), s32[]{:S(2)}) async-start(), calls=%async_computation.15 | async-start | bytes 6488064 | tf_op jit(solution)/shard_map/all_gather | solution.py:197
  11.2 711.7 %all-gather.14.cloned.1.call-start = ((), (), s32[]{:S(2)}) async-start(), calls=%async_computation.11 | async-start | bytes 38928384 | tf_op jit(solution)/shard_map/all_gather | solution.py:194
  11.9 818.0 %all-gather.20.cloned.1.call-start = ((), (), s32[]{:S(2)}) async-start(), calls=%async_computation.14 | async-start | bytes 38928384 | tf_op jit(solution)/shard_map/all_gather | solution.py:196
  12.7 1227.6 %reduce-scatter.34.cloned.1.call-start = ((), (), s32[]{:S(2)}) async-start(), calls=%async_computation.24 | async-start | bytes 405504
  62.5 72.9 %copy-start.83 = (s32[5]{0:T(128)S(1)}, s32[5]{0:T(128)}, u32[]{:S(2)}) copy-start(s32[5]{0:T(128)} %param.25) | copy-start | bytes 64
  63.3 109.9 %copy-start.63 = (s32[985]{0:T(1024)}, s32[985]{0:T(1024)S(1)}, u32[]{:S(2)}) copy-start(s32[985]{0:T(1024)S(1)} %eq.45) | copy-start | bytes 11824
  173.3 296.1 %copy-start.4 = (f32[985,768]{1,0:T(8,128)S(1)}, f32[985,768]{1,0:T(8,128)}, u32[]{:S(2)}) copy-start(f32[985,768]{1,0:T(8,128)} %reshape.341) | copy-start | bytes 9077764
  189.7 282.0 %copy-start.64 = (s32[985]{0:T(1024)S(1)}, s32[985]{0:T(1024)}, u32[]{:S(2)}) copy-start(s32[985]{0:T(1024)} %copy-done.63) | copy-start | bytes 11824
  255.1 217.1 %copy-start.43 = (bf16[768,128]{1,0:T(8,128)(2,1)}, bf16[768,128]{1,0:T(8,128)(2,1)S(1)}, u32[]{:S(2)}) copy-start(bf16[768,128]{1,0:T(8,128)(2,1)S(1)} %all_gather.70) | copy-start | bytes 589828
  393.5 246.0 %copy-start.29 = (bf16[128,768]{0,1:T(8,128)(2,1)}, bf16[128,768]{0,1:T(8,128)(2,1)S(1)}, u32[]{:S(2)}) copy-start(bf16[128,768]{0,1:T(8,128)(2,1)S(1)} %all_gather.74) | copy-start | bytes 589828
  393.5 78.7 %copy-start.71 = (bf16[128,72]{0,1:T(8,128)(2,1)S(1)}, bf16[128,72]{0,1:T(8,128)(2,1)}, u32[]{:S(2)}) copy-start(bf16[128,72]{0,1:T(8,128)(2,1)} %param.37) | copy-start | bytes 55300
  468.1 303.6 %copy-start.77 = (s32[128]{0:T(128)}, s32[128]{0:T(128)S(1)}, u32[]{:S(2)}) copy-start(s32[128]{0:T(128)S(1)} %and_select_fusion) | copy-start | bytes 1540
  472.2 84.3 %copy-start.36 = (bf16[985,128]{1,0:T(8,128)(2,1)}, bf16[985,128]{1,0:T(8,128)(2,1)S(1)}, u32[]{:S(2)}) copy-start(bf16[985,128]{1,0:T(8,128)(2,1)S(1)} %fusion.34) | copy-start | bytes 756484
  782.8 73.8 %copy-start.23 = (bf16[8,384,128]{2,1,0:T(8,128)(2,1)}, bf16[8,384,128]{2,1,0:T(8,128)(2,1)S(1)}, u32[]{:S(2)}) copy-start(bf16[8,384,128]{2,1,0:T(8,128)(2,1)S(1)} %fusion.28) | copy-start | bytes 2359300
  782.8 73.8 %copy-start.32 = (bf16[8,128,768]{1,2,0:T(8,128)(2,1)S(1)}, bf16[8,128,768]{1,2,0:T(8,128)(2,1)}, u32[]{:S(2)}) copy-start(bf16[8,128,768]{1,2,0:T(8,128)(2,1)} %all-gather.24.cloned.1.call-done) | copy-start | bytes 4718596
  909.3 130.6 %copy-start.48 = (bf16[985,8]{0,1:T(8,128)(2,1)}, bf16[985,8]{0,1:T(8,128)(2,1)S(1)}, u32[]{:S(2)}) copy-start(bf16[985,8]{0,1:T(8,128)(2,1)S(1)} %multiply_convert_fusion.8) | copy-start | bytes 47284
  1011.2 28.7 %copy-start.61 = (f32[985]{0:T(1024)S(1)}, f32[985]{0:T(1024)}, u32[]{:S(2)}) copy-start(f32[985]{0:T(1024)} %copy-done.60) | copy-start | bytes 11824
  1011.2 28.7 %copy-start.70 = (f32[768]{0:T(1024)S(1)}, f32[768]{0:T(1024)}, u32[]{:S(2)}) copy-start(f32[768]{0:T(1024)} %convert_element_type.139) | copy-start | bytes 9220
  1100.6 193.3 %reduce-scatter.32.cloned.1.call-start = ((), (), s32[]{:S(2)}) async-start(), calls=%async_computation.23 | async-start | bytes 405504
  1135.3 258.2 %reduce-scatter.28.cloned.1.call-start = ((), (), s32[]{:S(2)}) async-start(), calls=%async_computation.21 | async-start | bytes 405504
  1141.0 352.5 %reduce-scatter.36.cloned.1.call-start = ((), (), s32[]{:S(2)}) async-start(), calls=%async_computation.25 | async-start | bytes 405504
  1143.9 450.6 %reduce-scatter.30.cloned.1.call-start = ((), (), s32[]{:S(2)}) async-start(), calls=%async_computation.22 | async-start | bytes 1216512
  1148.7 552.3 %reduce-scatter.26.cloned.1.call-start = ((), (), s32[]{:S(2)}) async-start(), calls=%async_computation.20 | async-start | bytes 3244032 | tf_op jit(solution)/shard_map/reduce_scatter | solution.py:375
  1154.4 653.0 %reduce-scatter.20.cloned.1.call-start = ((), (), s32[]{:S(2)}) async-start(), calls=%async_computation.17 | async-start | bytes 3244032 | tf_op jit(solution)/shard_map/reduce_scatter | solution.py:372
  1160.2 808.4 %reduce-scatter.24.cloned.1.call-start = ((), (), s32[]{:S(2)}) async-start(), calls=%async_computation.19 | async-start | bytes 12976128 | tf_op jit(solution)/shard_map/reduce_scatter | solution.py:374
  1172.6 958.3 %reduce-scatter.22.cloned.1.call-start = ((), (), s32[]{:S(2)}) async-start(), calls=%async_computation.18 | async-start | bytes 12976128 | tf_op jit(solution)/shard_map/reduce_scatter | solution.py:373
  (72 other events, 554.0 us)
Sparse Core Ops, SparseCore 0:
  11.0 63.0 all-gather.9
  77.1 52.9 all-gather.11
  132.9 51.7 all-gather.23
  187.4 52.3 all-gather.15
  242.5 70.2 all-gather.17
  315.5 69.1 all-gather.21
  387.8 225.6 all-gather.13
  616.6 213.3 all-gather.19
  1100.7 93.0 reduce-scatter.33
  1199.9 93.9 reduce-scatter.31
  1299.4 93.9 reduce-scatter.27
  1399.6 93.8 reduce-scatter.35
  1499.2 95.3 reduce-scatter.29
  1600.4 100.6 reduce-scatter.25
  1706.9 100.5 reduce-scatter.19
  1813.9 154.6 reduce-scatter.23
  1976.1 154.7 reduce-scatter.21
where the time goes:
time: 2150 us; the launch traced here: 2140 us
  waiting for transfers between devices  943 us (44%)
  blocking collectives  503 us (23%)
  matrix products  364 us (17%)
  local copies, waits for them, and re-layouts  228 us (11%)
  other arithmetic  82.7 us (4%)
    unnamed x22, waiting for transfers between devices  359 us
    reduce_scatter x1, waiting for transfers between devices, on_device(): lax.psum_scatter(grad_up_up, ('dp', 'fsdp'), scatter_dimension=2, tiled=T...  162 us
    reduce_scatter x1, waiting for transfers between devices, on_device(): lax.psum_scatter(grad_down_down, ('dp', 'fsdp'), scatter_dimension=2, til...  161 us
    reduce_scatter x1, waiting for transfers between devices, on_device(): lax.psum_scatter(grad_down_up, ('dp', 'fsdp'), scatter_dimension=2, tiled...  107 us
    reduce_scatter x1, waiting for transfers between devices, on_device(): lax.psum_scatter(grad_up_down, ('dp', 'fsdp'), scatter_dimension=1, tiled...  106 us
    unnamed x2, blocking collectives  80.6 us
    all_gather x1, blocking collectives, on_device(): lax.all_gather(qkv_adapter_second, ('dp', 'fsdp'), axis=1, tiled=True)  78 us
    all_gather x1, blocking collectives, on_device(): lax.all_gather(router_adapter_first, ('dp', 'fsdp'), axis=0, tiled=True)  74.6 us
  transfers between devices with their start and end apart: 17, of which 9 were waited for; matrix products, arithmetic and copies ran while one was open for 19% of the time, Pallas kernels for 0%

commit v1 on v0

v1 whole, which is shorter than its diff:
```python
import functools
import math

import jax
import jax.numpy as jnp
from jax import lax
from jax.experimental import pallas as pl
from jax.experimental.pallas import tpu as pltpu
from jax.sharding import PartitionSpec as P

D = 768
HEADS = 12
HEAD = 64
NE = 8
LEN = 197
LP = 208
SL = 256
AC = 128
RANK = 16
CAP = 384
IMG = 5
GRP = 4
EL = NE // GRP
ROWS = GRP * CAP
RT = 256
DW = D + AC
EPS = 1e-06
F32 = jnp.float32
BF = jnp.bfloat16
AXES = ("dp", "fsdp")
VMEM = 60 * 1000 * 1024


def nn(a, b):
    return lax.dot_general(a, b, (((1,), (0,)), ((), ())), preferred_element_type=F32)


def nt(a, b):
    return lax.dot_general(a, b, (((1,), (1,)), ((), ())), preferred_element_type=F32)


def adapter_mask(rows, which):
    lane = lax.broadcasted_iota(jnp.int32, (rows, AC), 1)
    return jnp.where(lane // RANK == which, 1.0, 0.0).astype(F32)


def norm_parts(v):
    mean = jnp.mean(v, axis=-1, keepdims=True)
    cen = v - mean
    var = jnp.mean(cen * cen, axis=-1, keepdims=True)
    inv = lax.rsqrt(var + EPS)
    return cen * inv, inv


def norm_back(g, unit, inv, gain):
    s = g * gain
    return inv * (
        s
        - jnp.mean(s, axis=-1, keepdims=True)
        - unit * jnp.mean(s * unit, axis=-1, keepdims=True)
    )


def params(n):
    return pltpu.CompilerParams(dimension_semantics=("arbitrary",) * n, vmem_limit_bytes=VMEM)


def whole(shape):
    zeros = (0,) * len(shape)
    return pl.BlockSpec(shape, lambda *_: zeros, pipeline_mode=pl.Buffered(1))


def per_image(shape):
    rest = (0,) * (len(shape) - 1)
    return pl.BlockSpec(shape, lambda i, *_: (i,) + rest)


def fwd_kernel(sets, x_ref, g_ref, wq, wk, wv, wo, b4, a2t, rm, qkv_ref, att_ref, mid_ref, x2_ref, ad_ref, pr_ref, hid):
    mask = adapter_mask(LP, sets[pl.program_id(0)])
    hid[...] = jnp.zeros((LP, D), F32)
    hid[0:LEN, :] = x_ref[0].astype(F32)
    hidden = hid[...]
    unit, _ = norm_parts(hidden)
    x1 = (unit * g_ref[0:1, :]).astype(BF)
    aq = (mask * nn(x1, b4[:, 0:AC])).astype(BF)
    ad_ref[0, :, 0:AC] = aq
    for j, w in enumerate((wq, wk, wv)):
        part = nn(x1, w[...]) + nt(aq, a2t[j * D:(j + 1) * D, :])
        qkv_ref[0, :, j * D:(j + 1) * D] = part.astype(BF)
    lane = lax.broadcasted_iota(jnp.int32, (LP, 2 * HEAD), 1)
    keyok = lax.broadcasted_iota(jnp.int32, (LP, LP), 1) < LEN
    scale = 1.0 / math.sqrt(HEAD)
    for h in range(HEADS // 2):
        at = h * 2 * HEAD
        q = qkv_ref[0, :, at:at + 2 * HEAD]
        k = qkv_ref[0, :, D + at:D + at + 2 * HEAD]
        v = qkv_ref[0, :, 2 * D + at:2 * D + at + 2 * HEAD]
        outs = []
        for half in range(2):
            mine = (lane >= HEAD) if half else (lane < HEAD)
            s = nt(jnp.where(mine, q, jnp.zeros_like(q)), k) * scale
            s = jnp.where(keyok, s, -1e30)
            e = jnp.exp(s - jnp.max(s, axis=-1, keepdims=True))
            p = e * (1.0 / jnp.sum(e, axis=-1, keepdims=True))
            outs.append(nn(p.astype(BF), v))
        att_ref[0, :, at:at + 2 * HEAD] = jnp.where(lane < HEAD, outs[0], outs[1]).astype(BF)
    att = att_ref[0]
    ao = (mask * nn(att, b4[:, AC:2 * AC])).astype(BF)
    ad_ref[0, :, AC:2 * AC] = ao
    middle = hidden + nn(att, wo[...]) + nt(ao, b4[:, 3 * AC:4 * AC])
    mid_ref[0] = middle
    unit2, _ = norm_parts(middle)
    x2 = (unit2 * g_ref[1:2, :]).astype(BF)
    x2_ref[0] = x2
    ar = (mask * nn(x2, b4[:, 2 * AC:3 * AC])).astype(BF)
    ad_ref[0, :, 2 * AC:3 * AC] = ar
    logits = nn(x2, b4[:, 4 * AC:5 * AC]) + nn(ar, rm[...])
    elane = lax.broadcasted_iota(jnp.int32, (LP, AC), 1)
    logits = jnp.where(elane < NE, logits, -1e30)
    e = jnp.exp(logits - jnp.max(logits, axis=-1, keepdims=True))
    probs = e * (1.0 / jnp.sum(e, axis=-1, keepdims=True))
    padded = jnp.concatenate([probs, jnp.zeros((SL - LP, AC), F32)], axis=0)
    pr_ref[0] = jnp.transpose(padded)[0:NE, :]


def attention_forward(block_in, sets, gains, wq, wk, wv, wo, b4, a2t, rm):
    n = block_in.shape[0]
    sq = whole((D, D))
    return pl.pallas_call(
        fwd_kernel,
        grid_spec=pltpu.PrefetchScalarGridSpec(
            num_scalar_prefetch=1,
            grid=(n,),
            in_specs=[per_image((1, LEN, D)), whole((8, D)), sq, sq, sq, sq, sq, whole((3 * D, AC)), whole((AC, AC))],
            out_specs=[
                per_image((1, LP, 3 * D)),
                per_image((1, LP, D)),
                per_image((1, LP, D)),
                per_image((1, LP, D)),
                per_image((1, LP, 3 * AC)),
                per_image((1, NE, SL)),
            ],
            scratch_shapes=[pltpu.VMEM((LP, D), F32)],
        ),
        out_shape=[
            jax.ShapeDtypeStruct((n, LP, 3 * D), BF),
            jax.ShapeDtypeStruct((n, LP, D), BF),
            jax.ShapeDtypeStruct((n, LP, D), F32),
            jax.ShapeDtypeStruct((n, LP, D), BF),
            jax.ShapeDtypeStruct((n, LP, 3 * AC), BF),
            jax.ShapeDtypeStruct((n, NE, SL), F32),
        ],
        compiler_params=params(1),
        name="attention_forward",
    )(sets, block_in, gains, wq, wk, wv, wo, b4, a2t, rm)


def dispatch_kernel(offs, sets, slot_ref, gate_ref, x2_ref, cot_ref, u1_ref, d2_ref, xa_ref, ga_ref, mk_ref, acc, cpad):
    e = pl.program_id(0)
    b = pl.program_id(1)

    @pl.when(b == 0)
    def _():
        xa_ref[...] = jnp.zeros_like(xa_ref)
        ga_ref[...] = jnp.zeros_like(ga_ref)
        mk_ref[...] = jnp.zeros_like(mk_ref)

    acc[...] = jnp.zeros_like(acc)
    cpad[...] = jnp.zeros_like(cpad)
    gcol = jnp.transpose(gate_ref[0, 0])
    rows = lax.broadcasted_iota(jnp.int32, (CAP, LP), 0)
    for i in range(IMG):
        pick = jnp.where(rows == slot_ref[0, 0, i:i + 1, 0:LP], 1.0, 0.0).astype(BF)
        cpad[0:LEN, :] = cot_ref[0, i].astype(F32)
        gg = (cpad[...] * gcol[0:LP, i:i + 1]).astype(BF)
        acc[:, 0:D] += nn(pick, x2_ref[0, i])
        acc[:, D:2 * D] += nn(pick, gg)
        acc[:, 2 * D:] += nn(pick, adapter_mask(LP, sets[b * IMG + i]).astype(BF))
    mk = acc[:, 2 * D:]
    xs = acc[:, 0:D].astype(BF)
    gs = acc[:, D:2 * D].astype(BF)
    at = pl.multiple_of(offs[e * (GRP + 1) + b], 16)
    here = pl.ds(at, CAP)
    xa_ref[0, here, 0:D] = xs
    xa_ref[0, here, D:DW] = (mk * nn(xs, u1_ref[0])).astype(BF)
    ga_ref[0, here, 0:D] = gs
    ga_ref[0, here, D:DW] = (mk * nn(gs, d2_ref[0])).astype(BF)
    mk_ref[0, here, :] = mk.astype(BF)


def dispatch(offs, sets, slots, gates, x2, cot, u1, d2):
    return pl.pallas_call(
        dispatch_kernel,
        grid_spec=pltpu.PrefetchScalarGridSpec(
            num_scalar_prefetch=2,
            grid=(EL, GRP),
            in_specs=[
                pl.BlockSpec((1, 1, 8, SL), lambda e, b, *_: (b, e, 0, 0)),
                pl.BlockSpec((1, 1, 8, SL), lambda e, b, *_: (b, e, 0, 0)),
                pl.BlockSpec((1, IMG, LP, D), lambda e, b, *_: (b, 0, 0, 0)),
                pl.BlockSpec((1, IMG, LEN, D), lambda e, b, *_: (b, 0, 0, 0)),
                pl.BlockSpec((1, D, AC), lambda e, b, *_: (e, 0, 0)),
                pl.BlockSpec((1, D, AC), lambda e, b, *_: (e, 0, 0)),
            ],
            out_specs=[
                pl.BlockSpec((1, ROWS, DW), lambda e, b, *_: (e, 0, 0)),
                pl.BlockSpec((1, ROWS, DW), lambda e, b, *_: (e, 0, 0)),
                pl.BlockSpec((1, ROWS, AC), lambda e, b, *_: (e, 0, 0)),
            ],
            scratch_shapes=[pltpu.VMEM((CAP, 2 * D + AC), F32), pltpu.VMEM((LP, D), F32)],
        ),
        out_shape=[
            jax.ShapeDtypeStruct((EL, ROWS, DW), BF),
            jax.ShapeDtypeStruct((EL, ROWS, DW), BF),
            jax.ShapeDtypeStruct((EL, ROWS, AC), BF),
        ],
        compiler_params=params(2),
        name="dispatch",
    )(offs, sets, slots, gates, x2, cot, u1, d2)


def expert_kernel(first, e, offs, xa_ref, ga_ref, w_ref, *refs):
    if first:
        a1, a2, gu_ref, gd_ref, at_ref = refs
    else:
        p1, p2, a1, a2, gu_ref, gd_ref, at_ref = refs
    total = offs[e * (GRP + 1) + GRP]
    tiles = (total + (RT - 1)) // RT

    @pl.when(pl.program_id(0) == 0)
    def _():
        if first:
            a1[...] = jnp.zeros_like(a1)
            a2[...] = jnp.zeros_like(a2)
        else:
            a1[...] = p1[...]
            a2[...] = p2[...]
        at_ref[0] = jnp.transpose(xa_ref[0, :, D:DW].astype(F32)).astype(BF)
        at_ref[1] = jnp.transpose(ga_ref[0, :, D:DW].astype(F32)).astype(BF)

    wu = w_ref[0, :, 0:DW]
    wd = w_ref[0, :, DW:2 * DW]
    hb = w_ref.shape[1]
    c0 = math.sqrt(2.0 / math.pi)

    def step(t, carry):
        gu, gd = carry
        here = pl.ds(pl.multiple_of(t * RT, RT), RT)
        x = xa_ref[0, here, :]
        g = ga_ref[0, here, :]
        pre = nt(x, wu)
        gact = nt(g, wd)
        sq = pre * pre
        th = jnp.tanh(c0 * pre * (1.0 + 0.044715 * sq))
        half = 0.5 * (1.0 + th)
        act = (pre * half).astype(BF)
        slope = half + 0.5 * pre * (1.0 - th * th) * (c0 * (1.0 + 3 * 0.044715 * sq))
        gp = (slope * gact).astype(BF)
        a1[here, :] += nn(act, wd)
        a2[here, :] += nn(gp, wu)
        gu = gu + nn(at_ref[0, :, here], gp)
        gd = gd + nn(at_ref[1, :, here], act)
        return gu, gd

    zero = jnp.zeros((AC, hb), F32)
    gu, gd = lax.fori_loop(0, tiles, step, (zero, zero))
    gu_ref[0] = gu.astype(BF)
    gd_ref[0] = gd.astype(BF)


def expert_part(e, offs, xa, ga, w, prev):
    n, hb, _ = w.shape
    first = prev is None
    acc = whole((ROWS, DW))
    rows = pl.BlockSpec((1, ROWS, DW), lambda i, *_: (e, 0, 0))
    in_specs = [rows, rows, pl.BlockSpec((1, hb, 2 * DW), lambda i, *_: (i, 0, 0))]
    args = [xa, ga, w]
    alias = {}
    if not first:
        in_specs += [acc, acc]
        args += list(prev)
        alias = {4: 0, 5: 1}
    gspec = pl.BlockSpec((1, AC, hb), lambda i, *_: (i, 0, 0))
    return pl.pallas_call(
        functools.partial(expert_kernel, first, e),
        grid_spec=pltpu.PrefetchScalarGridSpec(
            num_scalar_prefetch=1,
            grid=(n,),
            in_specs=in_specs,
            out_specs=[acc, acc, gspec, gspec],
            scratch_shapes=[pltpu.VMEM((2, AC, ROWS), BF)],
        ),
        out_shape=[
            jax.ShapeDtypeStruct((ROWS, DW), F32),
            jax.ShapeDtypeStruct((ROWS, DW), F32),
            jax.ShapeDtypeStruct((n, AC, hb), BF),
            jax.ShapeDtypeStruct((n, AC, hb), BF),
        ],
        input_output_aliases=alias,
        compiler_params=params(1),
        name="expert_part",
    )(offs, *args)


def combine_kernel(offs, first_expert, a10, a20, a11, a21, xa_ref, ga_ref, mk_ref, u1_ref, d2_ref, slot_ref, gate_ref, cot_ref,
                   y_ref, g_ref, dot_ref, gud_ref, gdu_ref, ob, gb):
    b = pl.program_id(0)

    @pl.when(b == 0)
    def _():
        ob[...] = jnp.zeros_like(ob)
        gb[...] = jnp.zeros_like(gb)
        for e, (a1, a2) in enumerate(((a10, a20), (a11, a21))):
            total = offs[e * (GRP + 1) + GRP]
            tiles = (total + (RT - 1)) // RT

            def step(t, carry):
                gud, gdu = carry
                here = pl.ds(pl.multiple_of(t * RT, RT), RT)
                mk = mk_ref[e, here, :].astype(F32)
                adt = (mk * a1[here, D:DW]).astype(BF)
                aut = (mk * a2[here, D:DW]).astype(BF)
                ob[e, here, :] = (a1[here, 0:D] + nt(adt, d2_ref[e])).astype(BF)
                gb[e, here, :] = (a2[here, 0:D] + nt(aut, u1_ref[e])).astype(BF)
                autt = jnp.transpose(aut.astype(F32)).astype(BF)
                adtt = jnp.transpose(adt.astype(F32)).astype(BF)
                gud = gud + nn(autt, xa_ref[e, here, 0:D])
                gdu = gdu + nn(adtt, ga_ref[e, here, 0:D])
                return gud, gdu

            zero = jnp.zeros((AC, D), F32)
            gud, gdu = lax.fori_loop(0, tiles, step, (zero, zero))
            gud_ref[e] = jnp.transpose(gud).astype(BF)
            gdu_ref[e] = jnp.transpose(gdu).astype(BF)

    lanes = lax.broadcasted_iota(jnp.int32, (LP, CAP), 1).astype(F32)
    dlane = lax.broadcasted_iota(jnp.int32, (LP, AC), 1)
    scol = [jnp.transpose(slot_ref[0, e].astype(F32)) for e in range(EL)]
    gcol = [jnp.transpose(gate_ref[0, e]) for e in range(EL)]
    for i in range(IMG):
        y = jnp.zeros((LP, D), F32)
        g = jnp.zeros((LP, D), F32)
        dots = jnp.zeros((LP, AC), F32)
        cot = jnp.concatenate([cot_ref[0, i].astype(F32), jnp.zeros((LP - LEN, D), F32)], axis=0)
        for e in range(EL):
            at = pl.multiple_of(offs[e * (GRP + 1) + b], 16)
            here = pl.ds(at, CAP)
            pick = jnp.where(scol[e][0:LP, i:i + 1] == lanes, 1.0, 0.0).astype(BF)
            ye = nn(pick, ob[e, here, :])
            g = g + nn(pick, gb[e, here, :])
            y = y + gcol[e][0:LP, i:i + 1] * ye
            dot = jnp.sum(ye * cot, axis=-1, keepdims=True)
            dots = dots + jnp.where(dlane == first_expert[0] + e, dot, 0.0)
        y_ref[0, i] = y.astype(BF)
        g_ref[0, i] = g.astype(BF)
        full = jnp.concatenate([dots, jnp.zeros((SL - LP, AC), F32)], axis=0)
        dot_ref[0, i] = jnp.transpose(full)[0:NE, :]


def combine(offs, first_expert, accs, xa, ga, mk, u1, d2, slots, gates, cot):
    acc = whole((ROWS, DW))
    rows = whole((EL, ROWS, DW))
    block = lambda *shape: pl.BlockSpec((1,) + shape, lambda b, *_: (b,) + (0,) * len(shape))
    return pl.pallas_call(
        combine_kernel,
        grid_spec=pltpu.PrefetchScalarGridSpec(
            num_scalar_prefetch=2,
            grid=(GRP,),
            in_specs=[acc, acc, acc, acc, rows, rows, whole((EL, ROWS, AC)), whole((EL, D, AC)), whole((EL, D, AC)),
                      block(EL, 8, SL), block(EL, 8, SL), block(IMG, LEN, D)],
            out_specs=[block(IMG, LP, D), block(IMG, LP, D), block(IMG, NE, SL), whole((EL, D, AC)), whole((EL, D, AC))],
            scratch_shapes=[pltpu.VMEM((EL, ROWS, D), BF), pltpu.VMEM((EL, ROWS, D), BF)],
        ),
        out_shape=[
            jax.ShapeDtypeStruct((GRP, IMG, LP, D), BF),
            jax.ShapeDtypeStruct((GRP, IMG, LP, D), BF),
            jax.ShapeDtypeStruct((GRP, IMG, NE, SL), F32),
            jax.ShapeDtypeStruct((EL, D, AC), BF),
            jax.ShapeDtypeStruct((EL, D, AC), BF),
        ],
        compiler_params=params(1),
        name="combine",
    )(offs, first_expert, accs[0][0], accs[0][1], accs[1][0], accs[1][1], xa, ga, mk, u1, d2, slots, gates, cot)


def bwd_kernel(sets, live, x_ref, cot_ref, gin_ref, dot_ref, pr_ref, mid_ref, y_ref, qkv_ref, att_ref, x2_ref, ad_ref, g_ref,
               wq, wk, wv, wo, b4, a2t, rm, out_ref, ig_ref, acc_ref, hid, gq, acc):
    i = pl.program_id(0)
    mask = adapter_mask(LP, sets[i])
    alive = live[i].astype(F32)
    aq = ad_ref[0, :, 0:AC]
    ao = ad_ref[0, :, AC:2 * AC]
    ar = ad_ref[0, :, 2 * AC:3 * AC]

    @pl.when(i == 0)
    def _():
        acc[...] = jnp.zeros_like(acc)

    def tr(v):
        return jnp.transpose(v.astype(F32)).astype(BF)

    hid[...] = jnp.zeros((LP, D), F32)
    hid[0:LEN, :] = cot_ref[0].astype(F32) * alive
    gfin = hid[...]
    elane = lax.broadcasted_iota(jnp.int32, (LP, AC), 1)
    zrow = jnp.zeros((AC - NE, SL), F32)
    probs = jnp.transpose(jnp.concatenate([pr_ref[0], zrow], axis=0))[0:LP, :]
    gprobs = jnp.transpose(jnp.concatenate([dot_ref[0], zrow], axis=0))[0:LP, :]
    gl = probs * (gprobs - jnp.sum(gprobs * probs, axis=-1, keepdims=True))
    gl = jnp.where(elane < NE, gl, 0.0).astype(BF)
    gar = (mask * nt(gl, rm[...])).astype(BF)
    gtwo = gin_ref[0] + nt(gl, b4[:, 4 * AC:5 * AC]) + nt(gar, b4[:, 2 * AC:3 * AC])
    middle = mid_ref[0]
    out_ref[0] = ((middle + y_ref[0].astype(F32)) * alive)[0:LEN, :].astype(BF)
    unit2, inv2 = norm_parts(middle)
    gmid = gfin + norm_back(gtwo, unit2, inv2, g_ref[1:2, :])
    gbr = gmid.astype(BF)
    gao = (mask * nn(gbr, b4[:, 3 * AC:4 * AC])).astype(BF)
    gatt = (nt(gbr, wo[...]) + nt(gao, b4[:, AC:2 * AC])).astype(BF)
    gart = tr(gar)
    acc[:, 4 * D:5 * D] += nn(tr(gao), att_ref[0])
    acc[:, 5 * D:6 * D] += nn(tr(ao), gbr)
    acc[:, 6 * D:7 * D] += nn(gart, x2_ref[0])
    acc[:, 7 * D:] += nn(tr(ar), gl)

    lane = lax.broadcasted_iota(jnp.int32, (LP, 2 * HEAD), 1)
    keyok = lax.broadcasted_iota(jnp.int32, (LP, LP), 0) < LEN
    drow = lax.broadcasted_iota(jnp.int32, (2 * HEAD, LP), 0)
    scale = 1.0 / math.sqrt(HEAD)
    for h in range(HEADS // 2):
        at = h * 2 * HEAD
        q = qkv_ref[0, :, at:at + 2 * HEAD]
        k = qkv_ref[0, :, D + at:D + at + 2 * HEAD]
        v = qkv_ref[0, :, 2 * D + at:2 * D + at + 2 * HEAD]
        go = gatt[:, at:at + 2 * HEAD]
        kt = tr(k)
        dq, dk, dv = [], [], []
        for half in range(2):
            mine = (lane >= HEAD) if half else (lane < HEAD)
            s = nt(k, jnp.where(mine, q, jnp.zeros_like(q))) * scale
            s = jnp.where(keyok, s, -1e30)
            ex = jnp.exp(s - jnp.max(s, axis=0, keepdims=True))
            p = ex * (1.0 / jnp.sum(ex, axis=0, keepdims=True))
            dv.append(nn(p.astype(BF), go))
            dp = nt(v, jnp.where(mine, go, jnp.zeros_like(go)))
            gs = (p * (dp - jnp.sum(dp * p, axis=0, keepdims=True))).astype(BF)
            dk.append(nn(gs, q))
            dq.append(nn(kt, gs))
        dqt = jnp.where(drow < HEAD, dq[0], dq[1]) * scale
        gq[:, at:at + 2 * HEAD] = jnp.transpose(dqt).astype(BF)
        gq[:, D + at:D + at + 2 * HEAD] = (jnp.where(lane < HEAD, dk[0], dk[1]) * scale).astype(BF)
        gq[:, 2 * D + at:2 * D + at + 2 * HEAD] = jnp.where(lane < HEAD, dv[0], dv[1]).astype(BF)
    gqkv = gq[...]
    gaq = (mask * nn(gqkv, a2t[...])).astype(BF)
    hid[...] = jnp.zeros((LP, D), F32)
    hid[0:LEN, :] = x_ref[0].astype(F32)
    unit1, inv1 = norm_parts(hid[...])
    x1 = (unit1 * g_ref[0:1, :]).astype(BF)
    acc[:, 0:D] += nn(tr(gaq), x1)
    acc[:, D:4 * D] += nn(tr(aq), gqkv)
    gone = nt(gaq, b4[:, 0:AC])
    for j, w in enumerate((wq, wk, wv)):
        gone = gone + nt(gqkv[:, j * D:(j + 1) * D], w[...])
    ig = gmid + norm_back(gone, unit1, inv1, g_ref[0:1, :])
    ig_ref[0] = ig[0:LEN, :].astype(BF)

    @pl.when(i == pl.num_programs(0) - 1)
    def _():
        for c in range(acc.shape[1] // AC):
            acc_ref[c * AC:(c + 1) * AC, :] = jnp.transpose(acc[:, c * AC:(c + 1) * AC])


def backward(sets, live, block_in, cot, gin, dots, probs, mid, y, qkv, att, x2, ad, gains, wq, wk, wv, wo, b4, a2t, rm):
    n = block_in.shape[0]
    sq = whole((D, D))
    na = 7 * D + AC
    return pl.pallas_call(
        bwd_kernel,
        grid_spec=pltpu.PrefetchScalarGridSpec(
            num_scalar_prefetch=2,
            grid=(n,),
            in_specs=[
                per_image((1, LEN, D)), per_image((1, LEN, D)), per_image((1, LP, D)), per_image((1, NE, SL)), per_image((1, NE, SL)),
                per_image((1, LP, D)), per_image((1, LP, D)), per_image((1, LP, 3 * D)), per_image((1, LP, D)), per_image((1, LP, D)),
                per_image((1, LP, 3 * AC)), whole((8, D)), sq, sq, sq, sq, sq, whole((3 * D, AC)), whole((AC, AC)),
            ],
            out_specs=[per_image((1, LEN, D)), per_image((1, LEN, D)), whole((na, AC))],
            scratch_shapes=[pltpu.VMEM((LP, D), F32), pltpu.VMEM((LP, 3 * D), BF), pltpu.VMEM((AC, na), F32)],
        ),
        out_shape=[
            jax.ShapeDtypeStruct((n, LEN, D), BF),
            jax.ShapeDtypeStruct((n, LEN, D), BF),
            jax.ShapeDtypeStruct((na, AC), F32),
        ],
        compiler_params=params(1),
        name="backward",
    )(sets, live, block_in, cot, gin, dots, probs, mid, y, qkv, att, x2, ad, gains, wq, wk, wv, wo, b4, a2t, rm)


def on_device(dpn, fsn, block_in, cotangent, image_live, image_set, expert_routes, expert_slots, gain_attn, gain_moe, w_qkv, w_out,
              w_router, w_up, w_down, qkv_first, qkv_second, out_first, out_second, router_first, router_second, up_first,
              up_second, down_first, down_second):
    ndev = dpn * fsn
    nx = 1 << ((fsn.bit_length() - 1) // 2)
    nz = fsn // nx
    ng = dpn // GRP
    r = D // ndev
    hs = w_up.shape[2]
    d = lax.axis_index("dp")
    q = d % GRP
    rings = [
        (nz, "fsdp", [(f, ((f // nx + 1) % nz) * nx + f % nx) for f in range(fsn)]),
        (nx, "fsdp", [(f, (f // nx) * nx + (f % nx + 1) % nx) for f in range(fsn)]),
        (ng, "dp", [(a, (a + GRP) % dpn) for a in range(dpn)]),
    ]

    def swap(v, bit):
        return lax.ppermute(v, "dp", [(a, a ^ bit) for a in range(dpn)])

    rel = [0, 2, 1, 3]

    tr = jnp.transpose
    small = jnp.concatenate(
        [
            qkv_first, out_first, router_first, tr(out_second),
            jnp.concatenate([w_router, gain_attn[:, None], gain_moe[:, None], jnp.zeros((r, AC - NE - 2), BF)], axis=1),
            jnp.zeros((r, AC), BF).at[0, 0:router_second.shape[0]].set(router_second),
        ],
        axis=1,
    )
    a2s = tr(qkv_second).reshape(3, r, AC)
    second = jnp.concatenate([a2s[0], a2s[1], a2s[2], jnp.zeros((r, 3 * AC), BF)], axis=1)
    front = jnp.stack([w_qkv[:, 0:D], w_qkv[:, D:2 * D], w_qkv[:, 2 * D:], w_out, small, second])
    front = lax.all_gather(front.reshape(6 * r, D), AXES, axis=0, tiled=True).reshape(ndev, 6, r, D)
    wq, wk, wv, wo, b4 = (front[:, j].reshape(D, D) for j in range(5))
    a2t = tr(front[:, 5, :, 0:3 * AC].reshape(ndev, r, 3, AC), (0, 2, 1, 3)).reshape(3 * D, AC)
    gains = jnp.concatenate(
        [b4[:, 4 * AC + NE].reshape(1, D), b4[:, 4 * AC + NE + 1].reshape(1, D), jnp.zeros((6, D), BF)], axis=0
    ).astype(F32)
    rm = front[:, 4, 0, 5 * AC:5 * AC + router_second.shape[0]].reshape(AC, NE)
    rm = jnp.pad(rm, ((0, 0), (0, AC - NE)))

    wpk = jnp.concatenate([tr(w_up, (0, 2, 1)), tr(up_second, (0, 2, 1)), tr(w_down, (0, 2, 1)), tr(down_first, (0, 2, 1))], axis=2)
    wpk = wpk.reshape(GRP, EL, hs, 2 * DW)
    own = [lax.dynamic_index_in_dim(wpk, q ^ j, 0, keepdims=False) for j in range(GRP)]
    got = swap(jnp.stack([own[2], own[3]]), 2)
    mine = jnp.stack([own[0], got[0]])
    sib = swap(jnp.stack([own[1], got[1]]), 1)
    mine = jnp.concatenate([mine, sib], axis=0)
    units = [mine[:, e].reshape(GRP * hs, 2 * DW) for e in range(EL)]
    parts = []
    for e in range(EL):
        held = [units[e]]
        for n, axis, perm in rings:
            rows = [held]
            for _ in range(n - 1):
                rows.append([lax.ppermute(v, axis, perm) for v in rows[-1]])
            held = [v for row in rows for v in row]
        parts.append(held)

    route = expert_routes.reshape(IMG, LEN, 2)
    slot = expert_slots.reshape(IMG, LEN, 2)
    ids = jnp.arange(NE, dtype=jnp.int32)[None, :, None, None]
    ok = (route[:, None] == ids) & (slot[:, None] >= 0) & (image_live[:, None, None, None] > 0)
    mine_slots = jnp.max(jnp.where(ok, slot[:, None], -1), axis=-1)
    mine_slots = jnp.pad(mine_slots, ((0, 8 - IMG), (0, 0), (0, SL - LEN)), constant_values=-1)
    mine_slots = tr(mine_slots, (1, 0, 2))

    def group(v):
        two = jnp.stack([v, swap(v, 2)])
        return jnp.concatenate([two, swap(two, 1)], axis=0)

    all_slots = lax.dynamic_slice_in_dim(group(mine_slots), q * EL, EL, axis=1)
    counts = jnp.max(all_slots, axis=(2, 3)) + 1
    steps = (counts + 15) // 16 * 16
    offs = jnp.concatenate([jnp.zeros((1, EL), jnp.int32), jnp.cumsum(steps, axis=0)], axis=0)
    offs = tr(offs).reshape(-1).astype(jnp.int32)
    all_sets = group(image_set).reshape(-1)
    cots = group(cotangent)

    ef = jnp.concatenate([up_first, tr(down_second, (0, 2, 1))], axis=2)
    ef = lax.all_gather(ef, AXES, axis=0, tiled=False)
    ef = lax.dynamic_slice_in_dim(ef, q * EL, EL, axis=1)
    ef = tr(ef, (1, 0, 2, 3)).reshape(EL, D, 2 * AC)
    u1, d2 = ef[:, :, 0:AC], ef[:, :, AC:]

    qkv, att, mid, x2, ad, probs = attention_forward(block_in, image_set, gains, wq, wk, wv, wo, b4, a2t, rm)
    x2s = group(x2)
    gates = lax.dynamic_slice_in_dim(tr(group(jnp.pad(probs, ((0, 8 - IMG), (0, 0), (0, 0)))), (0, 2, 1, 3)), q * EL, EL, axis=1)

    xa, ga, mk = dispatch(offs, all_sets, all_slots, gates, x2s, cots, u1, d2)

    accs, gus, gds = [], [], []
    for e in range(EL):
        w = jnp.stack(parts[e])
        a1, a2, gu, gd = expert_part(e, offs, xa, ga, w.reshape(-1, 2 * CAP, 2 * DW), None)
        accs.append((a1, a2))
        shape = (AC, w.shape[0], GRP, hs)
        unroll = lambda v: tr(v, (1, 0, 2)).reshape(shape)
        gus.append(unroll(gu))
        gds.append(unroll(gd))

    ysum, gsum, dots, gud, gdu = combine(offs, (q * EL).reshape(1), accs, xa, ga, mk, u1, d2, all_slots, gates, cots)

    def home(v, dt):
        half = v[0:2].astype(F32) + swap(v[2:4], 1).astype(F32)
        return half[0] + swap(half[1].astype(dt), 2).astype(F32)

    gin = home(gsum, BF)
    dots = home(dots, F32)
    ymine = home(ysum, BF).astype(BF)

    block_out, input_grad, acc = backward(image_set, image_live, block_in, cotangent, gin, dots, probs, mid, ymine, qkv, att, x2, ad,
                                          gains, wq, wk, wv, wo, b4, a2t, rm)

    eg = jnp.stack([jnp.stack(gus), jnp.stack(gds)])
    pieces = [eg[:, :, :, j] for j in range(eg.shape[3])]
    for n, axis, perm in reversed(rings):
        back = [(b, a) for a, b in perm]
        cut = len(pieces) // n
        rows = [pieces[k * cut:(k + 1) * cut] for k in range(n)]
        total = rows[n - 1]
        for k in range(n - 2, -1, -1):
            total = [(lax.ppermute(v, axis, back).astype(F32) + u.astype(F32)).astype(BF) for v, u in zip(total, rows[k])]
        pieces = total
    piece = pieces[0]

    def owners(v):
        sib = swap(v[2:4], 1)
        near = jnp.stack([v[0], sib[0]])
        far = swap(jnp.stack([v[1], sib[1]]), 2)
        got = jnp.concatenate([near, far], axis=0)
        order = [0, 1, 2, 3]
        at = jnp.stack([q ^ j for j in order])
        place = jnp.argsort(at)
        return jnp.take(got, place, axis=0)

    eg = owners(tr(piece, (3, 0, 1, 2, 4)))
    eg = tr(eg, (1, 0, 2, 3, 4)).reshape(2, NE, AC, hs).astype(F32)

    ff = jnp.stack([gud, gdu])
    ff = ff.reshape(2, EL, ng, GRP, fsn, r, AC)
    ff = jnp.moveaxis(ff, 3, 0)
    ff = jnp.stack([lax.dynamic_index_in_dim(ff, q ^ j, 0, keepdims=False) for j in rel])
    ff = lax.psum_scatter(ff, "fsdp", scatter_dimension=4, tiled=False)
    held = ff
    for _ in range(ng - 1):
        held = lax.ppermute(held, "dp", rings[2][2])
        ff = ff + held
    ff = lax.dynamic_index_in_dim(ff, d // GRP, 3, keepdims=False)
    ff = owners(ff)
    ff = tr(ff, (1, 0, 2, 3, 4)).reshape(2, NE, r, AC).astype(F32)

    per = lambda v, k: v.reshape(ndev, k * r, AC)
    nrs = router_second.shape[0]
    rs = tr(acc[7 * D:7 * D + NE, :]).reshape(ndev, nrs)
    rs = jnp.pad(rs, ((0, 0), (0, AC - nrs)))[:, None]
    sm = jnp.concatenate([per(acc[0:D], 1), per(acc[D:4 * D], 3), per(acc[4 * D:5 * D], 1), per(acc[5 * D:6 * D], 1),
                          per(acc[6 * D:7 * D], 1), rs, jnp.zeros((ndev, 7, AC), F32)], axis=1)
    sm = lax.psum_scatter(sm.astype(BF), AXES, scatter_dimension=0, tiled=False).astype(F32)
    return (
        block_out,
        input_grad,
        sm[0:r],
        tr(sm[r:4 * r]),
        sm[4 * r:5 * r],
        tr(sm[5 * r:6 * r]),
        sm[6 * r:7 * r],
        sm[7 * r, 0:nrs],
        ff[0],
        eg[0],
        eg[1],
        tr(ff[1], (0, 2, 1)),
    )


def solution(mesh):
    dpn, fsn = mesh.shape["dp"], mesh.shape["fsdp"]
    both = ("dp", "fsdp")
    return jax.shard_map(
        functools.partial(on_device, dpn, fsn),
        mesh=mesh,
        in_specs=(
            P(both, None, None),
            P(both, None, None),
            P(both),
            P(both),
            P(both, None, None),
            P(both, None, None),
            P(both),
            P(both),
            P(both, None),
            P(both, None),
            P(both, None),
            P(None, None, both),
            P(None, None, both),
            P(both, None),
            P(None, both),
            P(both, None),
            P(None, both),
            P(both, None),
            P(both),
            P(None, both, None),
            P(None, None, both),
            P(None, None, both),
            P(None, None, both),
        ),
        out_specs=(
            P(both, None, None),
            P(both, None, None),
            P(both, None),
            P(None, both),
            P(both, None),
            P(None, both),
            P(both, None),
            P(both),
            P(None, both, None),
            P(None, None, both),
            P(None, None, both),
            P(None, None, both),
        ),
        check_vma=False,
    )
```

time: 2150 us -> 922 us (0.43)
  blocking collectives: 503 us -> 0 us
  waiting for transfers between devices: 943 us -> 487 us
  matrix products: 364 us -> 0 us
  Pallas kernels: 0 us -> 220 us
  local copies, waits for them, and re-layouts: 228 us -> 99.8 us
  starting transfers between devices: 1.14 us -> 45.9 us
  other arithmetic: 82.7 us -> 43.2 us
    all_gather x6 -> x0, blocking collectives: 423 us -> none  [the longest x1 78 us: on_device(): lax.all_gather(qkv_adapter_second, ('dp', 'fsdp'), axis=1, tiled=True)]
    reduce_scatter x4 -> x2, waiting for transfers between devices: 536 us -> 118 us  [the longest x1 118 us: on_device(): lax.psum_scatter(sm.astype(BF), AXES, scatter_dimension=0, tiled=False)]
    ppermute x0 -> x43, waiting for transfers between devices: none -> 369 us  [the longest x14 196 us: on_device(): rows.append([lax.ppermute(v, axis, perm) for v in rows[-1]])]
    dot_general x46 -> x0, matrix products: 364 us -> none  [the longest x1 58.6 us: on_device(): jnp.einsum('ecd,edf->ecf', grad_expert, down_piece, preferred_element_typ...]
    unnamed x22 -> x4, waiting for transfers between devices: 359 us -> 0.07 us
    pallas_call x0 -> x6, Pallas kernels: none -> 220 us  [the longest x2 75.9 us: expert_part(): pl.pallas_call(functools.partial(expert_kernel, first, e), grid_spec=pltp...]
    unnamed x2 -> x0, blocking collectives: 80.6 us -> none
    gather x6 -> x2, local copies, waits for them, and re-layouts: 72.2 us -> 1.19 us  [owners(): return jnp.take(got, place, axis=0)]
  transfers between devices with their start and end apart: 17 -> 47, of which waited for: 9 -> 17; matrix products, arithmetic and copies ran while one was open for 19% -> 14% of each run, Pallas kernels for 0% -> 9%
where the time goes in v1:
time: 922 us; the launch traced here: 911 us
  waiting for transfers between devices  487 us (53%)
  Pallas kernels  220 us (24%)
  local copies, waits for them, and re-layouts  99.8 us (11%)
  starting transfers between devices  45.9 us (5%)
  other arithmetic  43.2 us (5%)
  between operations  15 us (2%)
    ppermute x14, waiting for transfers between devices, on_device(): rows.append([lax.ppermute(v, axis, perm) for v in rows[-1]])  196 us
    ppermute x22, waiting for transfers between devices, swap(): return lax.ppermute(v, 'dp', [(a, a ^ bit) for a in range(dpn)])  164 us
    reduce_scatter x1, waiting for transfers between devices, on_device(): lax.psum_scatter(sm.astype(BF), AXES, scatter_dimension=0, tiled=False)  118 us
    pallas_call x2, Pallas kernels, expert_part(): pl.pallas_call(functools.partial(expert_kernel, first, e), grid_spec=pltp...  75.9 us
    pallas_call x1, Pallas kernels, backward(): pl.pallas_call(bwd_kernel, grid_spec=pltpu.PrefetchScalarGridSpec(num_sca...  52.6 us
    unnamed x79, local copies, waits for them, and re-layouts  37.7 us
    pallas_call x1, Pallas kernels, combine(): pl.pallas_call(combine_kernel, grid_spec=pltpu.PrefetchScalarGridSpec(num...  35.2 us
    pallas_call x1, Pallas kernels, dispatch(): pl.pallas_call(dispatch_kernel, grid_spec=pltpu.PrefetchScalarGridSpec(nu...  28.7 us
  transfers between devices with their start and end apart: 47, of which 17 were waited for; matrix products, arithmetic and copies ran while one was open for 14% of the time, Pallas kernels for 9%

profile of v1, /device:TPU:0, one launch (start us, length us, event | category | flops | bytes accessed | tf_op | source)
XLA Modules:
  0.0 910.8 jit_solution(1178027286705127373)
XLA Ops:
  19.5 3.0 collective-permute-start.10
  23.4 32.2 %collective-permute-done.10 = bf16[2,2,96,1792]{3,2,1,0:T(8,128)(2,1)S(1)} collective-permute-done((bf16[2,2,96,1792]{3,2,1,0:T(8,128)(2,1)S(1)}, bf16[2,2,96,1792]{3,2,1,0:T(8,128)(2,1)S(1)}, u32[]{:S(2)}, u32[]{:S(2)}) %collective-permute-start.10) | collective-permute-done | bytes 1376288 | tf_op jit(solution)/shard_map/ppermute | solution.py:518
  58.1 37.4 %collective-permute-done.8 = bf16[5,197,768]{2,1,0:T(8,128)(2,1)S(1)} collective-permute-done((bf16[5,197,768]{2,1,0:T(8,128)(2,1)S(1)}, bf16[5,197,768]{2,1,0:T(8,128)(2,1)S(1)}, u32[]{:S(2)}, u32[]{:S(2)}) %collective-permute-start.8) | collective-permute-done | bytes 1512992 | tf_op jit(solution)/shard_map/ppermute | solution.py:518
  95.9 3.9 copy.118
  119.0 35.2 %collective-permute-done.12 = bf16[384,1792]{1,0:T(8,128)(2,1)} collective-permute-done((bf16[384,1792]{1,0:T(8,128)(2,1)}, bf16[384,1792]{1,0:T(8,128)(2,1)}, u32[]{:S(2)}, u32[]{:S(2)}) %collective-permute-start.12) | collective-permute-done | bytes 1376288 | tf_op jit(solution)/shard_map/ppermute | solution.py:557
  155.6 39.4 %collective-permute-done.19 = bf16[384,1792]{1,0:T(8,128)(2,1)} collective-permute-done((bf16[384,1792]{1,0:T(8,128)(2,1)}, bf16[384,1792]{1,0:T(8,128)(2,1)}, u32[]{:S(2)}, u32[]{:S(2)}) %collective-permute-start.19) | collective-permute-done | bytes 1376288 | tf_op jit(solution)/shard_map/ppermute | solution.py:557
  203.9 3.2 pad_maximum_fusion.1.cot_ref
  207.2 17.3 %collective-permute-done.13 = bf16[384,1792]{1,0:T(8,128)(2,1)} collective-permute-done((bf16[384,1792]{1,0:T(8,128)(2,1)}, bf16[384,1792]{1,0:T(8,128)(2,1)}, u32[]{:S(2)}, u32[]{:S(2)}) %collective-permute-start.13) | collective-permute-done | bytes 1376288 | tf_op jit(solution)/shard_map/ppermute | solution.py:557
  228.7 25.0 %collective-permute-done.20 = bf16[384,1792]{1,0:T(8,128)(2,1)S(1)} collective-permute-done((bf16[384,1792]{1,0:T(8,128)(2,1)}, bf16[384,1792]{1,0:T(8,128)(2,1)S(1)}, u32[]{:S(2)}, u32[]{:S(2)}) %collective-permute-start.20) | collective-permute-done | bytes 1376288 | tf_op jit(solution)/shard_map/ppermute | solution.py:557
  261.0 4.9 fusion.43
  268.1 27.5 %attention_forward.1 = (bf16[5,208,2304]{2,1,0:T(8,128)(2,1)}, bf16[5,208,768]{2,1,0:T(8,128)(2,1)}, f32[5,208,768]{2,1,0:T(8,128)}, bf16[5,208,768]{2,1,0:T(8,1...) custom-call(s32[5]{0:T(128)} %sets.3, bf16[5,197,768]{2,1,0:T(8,128)(2,1)} %x_ref.3, ...), custom_call_target="tpu_custom_call" | custom-call | tf_op jit(solution)/shard_map/attention_forward/pallas_call | solution.py:129
  310.0 22.6 %collective-permute-done.6 = bf16[5,208,768]{2,1,0:T(8,128)(2,1)S(1)} collective-permute-done((bf16[5,208,768]{2,1,0:T(8,128)(2,1)}, bf16[5,208,768]{2,1,0:T(8,128)(2,1)S(1)}, u32[]{:S(2)}, u32[]{:S(2)}) %collective-permute-start.6) | collective-permute-done | bytes 1597472 | tf_op jit(solution)/shard_map/ppermute | solution.py:518
  340.0 25.7 %collective-permute-done.24 = bf16[384,1792]{1,0:T(8,128)(2,1)S(1)} collective-permute-done((bf16[384,1792]{1,0:T(8,128)(2,1)S(1)}, bf16[384,1792]{1,0:T(8,128)(2,1)S(1)}, u32[]{:S(2)}, u32[]{:S(2)}) %collective-permute-start.24) | collective-permute-done | bytes 1376288 | tf_op jit(solution)/shard_map/ppermute | solution.py:557
  367.6 27.7 %collective-permute-done.18 = bf16[384,1792]{1,0:T(8,128)(2,1)S(1)} collective-permute-done((bf16[384,1792]{1,0:T(8,128)(2,1)}, bf16[384,1792]{1,0:T(8,128)(2,1)S(1)}, u32[]{:S(2)}, u32[]{:S(2)}) %collective-permute-start.18) | collective-permute-done | bytes 1376288 | tf_op jit(solution)/shard_map/ppermute | solution.py:557
  396.6 26.1 %collective-permute-done.25 = bf16[384,1792]{1,0:T(8,128)(2,1)S(1)} collective-permute-done((bf16[384,1792]{1,0:T(8,128)(2,1)S(1)}, bf16[384,1792]{1,0:T(8,128)(2,1)S(1)}, u32[]{:S(2)}, u32[]{:S(2)}) %collective-permute-start.25) | collective-permute-done | bytes 1376288 | tf_op jit(solution)/shard_map/ppermute | solution.py:557
  424.5 3.5 pad_maximum_fusion.x2_ref
  428.1 28.7 %dispatch.1 = (bf16[2,1536,896]{2,1,0:T(8,128)(2,1)}, bf16[2,1536,896]{2,1,0:T(8,128)(2,1)}, bf16[2,1536,128]{2,1,0:T(8,128)(2,1)}) custom-call(s32[10]{0:T(128)} %reshape.167.offs, s32[20]{0:T(128)} %reshape.169.sets, s32[4,2,8,256]{3,2,1,0:T(8,128)} %get-tuple-element.79.slot_ref, f32[4,2,8,256]{3,2,1,0:T(8,128)} %fusion.34.gate_ref, ...), custom_call_target="tpu_custom_call" | custom-call | tf_op jit(solution)/shard_map/dispatch/pallas_call | solution.py:192
  456.7 37.9 %expert_part.3 = (f32[1536,896]{1,0:T(8,128)}, f32[1536,896]{1,0:T(8,128)}, bf16[4,128,768]{2,1,0:T(8,128)(2,1)}, bf16[4,128,768]{2,1,0:T(8,128)(2,1)}) custom-call(s32[10]{0:T(128)} %reshape.167.offs, bf16[2,1536,896]{2,1,0:T(8,128)(2,1)} %get-tuple-element.52.xa_ref, bf16[2,1536,896]{2,1,0:T(8,128)(2,1)} %get-tuple-element.53.ga_ref, ...), custom_call_target="tpu_custom_call" | custom-call | tf_op jit(solution)/shard_map/expert_part/pallas_call | solution.py:284
  494.7 37.9 %expert_part.2 = (f32[1536,896]{1,0:T(8,128)}, f32[1536,896]{1,0:T(8,128)}, bf16[4,128,768]{2,1,0:T(8,128)(2,1)}, bf16[4,128,768]{2,1,0:T(8,128)(2,1)}) custom-call(s32[10]{0:T(128)} %reshape.167.offs, bf16[2,1536,896]{2,1,0:T(8,128)(2,1)} %get-tuple-element.52.xa_ref, bf16[2,1536,896]{2,1,0:T(8,128)(2,1)} %get-tuple-element.53.ga_ref, ...), custom_call_target="tpu_custom_call" | custom-call | tf_op jit(solution)/shard_map/expert_part/pallas_call | solution.py:284
  532.6 35.2 %combine.1 = (bf16[4,5,208,768]{3,2,1,0:T(8,128)(2,1)}, bf16[4,5,208,768]{3,2,1,0:T(8,128)(2,1)}, f32[4,5,8,256]{3,2,1,0:T(8,128)}, bf16[2,768,128]{2,1,0:T(8,128)(2,1)}, bf16[2,768,128]{2,1,0:T(8,128)(2,1)}) custom-call(s32[10]{0:T(128)} %reshape.167.offs, s32[1]{0:T(128)} %bitcast.5.first_expert, f32[1536,896]{1,0:T(8,128)} %get-tuple-element.54.a10, ...), custom_call_target="tpu_custom_call" | custom-call | tf_op jit(solution)/shard_map/combine/pallas_call | solution.py:364
  567.8 3.9 slice.286
  586.7 8.5 collective-permute-done.34
  595.4 12.6 %collective-permute-start.35 = (bf16[2,2,128,4,96]{2,4,1,0,3:T(8,128)(2,1)S(1)}, bf16[2,2,128,4,96]{2,4,1,0,3:T(8,128)(2,1)S(1)}, u32[]{:S(2)}, u32[]{:S(2)}) collective-permute-start(bf16[2,2,128,4,96]{2,4,1,0,3:T(8,128)(2,1)S(1)} %fusion.8), channel_id=1, source_target_pairs={{2,0},{3,1},{4,2},{5,3},{6,4},{7,5},{0,6},{1,7},{10,8},{11,9},{12,... | collective-permute-start | bytes 1179656 | tf_op jit(solution)/shard_map/ppermute | solution.py:624
  612.2 4.0 convert_add_fusion.1
  622.7 59.4 %collective-permute-done.29 = f32[5,8,256]{2,1,0:T(8,128)} collective-permute-done((f32[5,8,256]{2,1,0:T(8,128)}, f32[5,8,256]{2,1,0:T(8,128)}, u32[]{:S(2)}, u32[]{:S(2)}) %collective-permute-start.29) | collective-permute-done | bytes 40992 | tf_op jit(solution)/shard_map/ppermute | solution.py:518
  688.0 3.9 fusion.1.y_ref
  691.9 4.4 fusion.2.gin_ref
  696.4 52.6 %backward.1 = (bf16[5,197,768]{2,1,0:T(8,128)(2,1)}, bf16[5,197,768]{2,1,0:T(8,128)(2,1)}, f32[5504,128]{1,0:T(8,128)}) custom-call(s32[5]{0:T(128)} %sets.3, s32[5]{0:T(128)} %live.1, bf16[5,197,768]{2,1,0:T(8,128)(2,1)} %x_ref.3, bf16[5,197,768]{2,1,0:T(8,128)(2,1)} %cot_ref.1, f32[5,208,768]{2,1,0:T(8,128)} %fusion.2.gin_ref, ...), custom_call_target="tpu_custom_call" | custom-call | tf_op jit(solution)/shard_map/backward/pallas_call | solution.py:477
  756.9 9.8 %concatenate.66 = bf16[32,176,128]{2,1,0:T(8,128)(2,1)} concatenate(bf16[32,24,128]{2,1,0:T(8,128)(2,1)} %bitcast.264, bf16[32,72,128]{2,1,0:T(8,128)(2,1)} %bitcast.258, bf16[32,24,128]{2,1,0:T(8,128)(2,1)} %bitcast.263, bf16[32,24,128]{2,1,0:T(8,128)(2,1)S(1)} %bitcast.262, bf16[32,24,128]{2,1,0:T(8,128)(2,1)S(1)} %bitcast.261, bf16[32,1,128]{2,1,0:T(2,128)(2,1)S(1)} %copy.122, ...), dimensions={1} | concatenate | bytes 2883584 | tf_op jit(solution)/shard_map/concatenate | solution.py:658
  770.3 3.5 collective-permute-done.33
  775.6 5.9 collective-permute-done.42
  783.2 118.1 %reduce-scatter.3.cloned.1.call-done = bf16[1,176,128]{2,1,0:T(8,128)(2,1)} async-done(((bf16[32,176,128]{2,1,0:T(8,128)(2,1)}), bf16[1,176,128]{2,1,0:T(8,128)(2,1)}) %reduce-scatter.3.cloned.1.call-update) | async-done | bytes 45072 | tf_op jit(solution)/shard_map/reduce_scatter | solution.py:660
  (273 shorter events, 134.8 us)
Async XLA Ops:
  7.2 248.8 %all-gather.6.cloned.1.call-start = ((), (), s32[]{:S(2)}) async-start(), calls=%async_computation.5 | async-start | bytes 3244032 | tf_op jit(solution)/shard_map/all_gather | solution.py:582
  8.7 249.5 %all-gather.4.cloned.1.call-start = ((), (), s32[]{:S(2)}) async-start(), calls=%async_computation.2 | async-start | bytes 7299072 | tf_op jit(solution)/shard_map/all_gather | solution.py:534
  17.1 750.3 %reduce-scatter.5.cloned.1.call-start = ((), (), s32[]{:S(2)}) async-start(), calls=%async_computation.4 | async-start | bytes 884736 | tf_op jit(solution)/shard_map/reduce_scatter | solution.py:645
  19.5 36.1 %collective-permute-start.10 = (bf16[2,2,96,1792]{3,2,1,0:T(8,128)(2,1)S(1)}, bf16[2,2,96,1792]{3,2,1,0:T(8,128)(2,1)S(1)}, u32[]{:S(2)}, u32[]{:S(2)}) collective-permute-start(bf16[2,2,96,1792]{3,2,1,0:T(8,128)(2,1)S(1)} %pad_maximum_fusion.6), channel_id=1, source_target_pairs={{0,16},{8,24},{16,0},{24,8},{1,17},{9,25},{17,1},{25,9},{2,18},{10... | collective-permute-start | bytes 4128776 | tf_op jit(solution)/shard_map/ppermute | solution.py:518
  22.5 73.1 %collective-permute-start.8 = (bf16[5,197,768]{2,1,0:T(8,128)(2,1)S(1)}, bf16[5,197,768]{2,1,0:T(8,128)(2,1)S(1)}, u32[]{:S(2)}, u32[]{:S(2)}) collective-permute-start(bf16[5,197,768]{2,1,0:T(8,128)(2,1)S(1)} %copy-done.3), channel_id=1, source_target_pairs={{0,16},{8,24},{16,0},{24,8},{1,17},{9,25},{17,1},{25,9},{2,18},{10... | collective-permute-start | bytes 4538888 | tf_op jit(solution)/shard_map/ppermute | solution.py:518
  55.8 44.0 %collective-permute-start.11 = (bf16[2,2,96,1792]{3,2,1,0:T(8,128)(2,1)S(1)}, bf16[2,2,96,1792]{3,2,1,0:T(8,128)(2,1)S(1)}, u32[]{:S(2)}, u32[]{:S(2)}) collective-permute-start(bf16[2,2,96,1792]{3,2,1,0:T(8,128)(2,1)S(1)} %pad_maximum_fusion.7), channel_id=1, source_target_pairs={{0,8},{8,0},{16,24},{24,16},{1,9},{9,1},{17,25},{25,17},{2,10},{10... | collective-permute-start | bytes 4128776 | tf_op jit(solution)/shard_map/ppermute | solution.py:518
  56.1 50.7 %collective-permute-start = (s32[8,8,256]{2,1,0:T(8,128)S(1)}, s32[8,8,256]{2,1,0:T(8,128)S(1)}, u32[]{:S(2)}, u32[]{:S(2)}) collective-permute-start(s32[8,8,256]{2,1,0:T(8,128)S(1)} %get-tuple-element.124), channel_id=1, source_target_pairs={{0,16},{8,24},{16,0},{24,8},{1,17},{9,25},{17,1},{25,9},{2,18},{10... | collective-permute-start | bytes 196616 | tf_op jit(solution)/shard_map/ppermute | solution.py:518
  99.8 100.3 %collective-permute-start.9 = (bf16[2,5,197,768]{3,0,2,1:T(2,128)(2,1)}, bf16[2,5,197,768]{3,0,2,1:T(2,128)(2,1)}, u32[]{:S(2)}, u32[]{:S(2)}) collective-permute-start(bf16[2,5,197,768]{3,0,2,1:T(2,128)(2,1)} %copy.118), channel_id=1, source_target_pairs={{0,8},{8,0},{16,24},{24,16},{1,9},{9,1},{17,25},{25,17},{2,10},{10... | collective-permute-start | bytes 9077768 | tf_op jit(solution)/shard_map/ppermute | solution.py:518
  101.8 52.4 %collective-permute-start.12 = (bf16[384,1792]{1,0:T(8,128)(2,1)}, bf16[384,1792]{1,0:T(8,128)(2,1)}, u32[]{:S(2)}, u32[]{:S(2)}) collective-permute-start(bf16[384,1792]{1,0:T(8,128)(2,1)} %bitcast.46), channel_id=1, source_target_pairs={{0,2},{1,3},{2,4},{3,5},{4,6},{5,7},{6,0},{7,1},{8,10},{9,11},{10,... | collective-permute-start | bytes 4128776 | tf_op jit(solution)/shard_map/ppermute | solution.py:557
  103.6 91.4 %collective-permute-start.19 = (bf16[384,1792]{1,0:T(8,128)(2,1)}, bf16[384,1792]{1,0:T(8,128)(2,1)}, u32[]{:S(2)}, u32[]{:S(2)}) collective-permute-start(bf16[384,1792]{1,0:T(8,128)(2,1)} %bitcast.56), channel_id=1, source_target_pairs={{0,2},{1,3},{2,4},{3,5},{4,6},{5,7},{6,0},{7,1},{8,10},{9,11},{10,... | collective-permute-start | bytes 4128776 | tf_op jit(solution)/shard_map/ppermute | solution.py:557
  111.9 187.8 %collective-permute-start.15 = (bf16[384,1792]{1,0:T(8,128)(2,1)}, bf16[384,1792]{1,0:T(8,128)(2,1)}, u32[]{:S(2)}, u32[]{:S(2)}) collective-permute-start(bf16[384,1792]{1,0:T(8,128)(2,1)} %bitcast.46), channel_id=1, source_target_pairs={{0,1},{1,0},{2,3},{3,2},{4,5},{5,4},{6,7},{7,6},{8,9},{9,8},{10,11... | collective-permute-start | bytes 4128776 | tf_op jit(solution)/shard_map/ppermute | solution.py:557
  113.4 222.2 %collective-permute-start.22 = (bf16[384,1792]{1,0:T(8,128)(2,1)}, bf16[384,1792]{1,0:T(8,128)(2,1)}, u32[]{:S(2)}, u32[]{:S(2)}) collective-permute-start(bf16[384,1792]{1,0:T(8,128)(2,1)} %bitcast.56), channel_id=1, source_target_pairs={{0,1},{1,0},{2,3},{3,2},{4,5},{5,4},{6,7},{7,6},{8,9},{9,8},{10,11... | collective-permute-start | bytes 4128776 | tf_op jit(solution)/shard_map/ppermute | solution.py:557
  154.2 70.3 %collective-permute-start.13 = (bf16[384,1792]{1,0:T(8,128)(2,1)}, bf16[384,1792]{1,0:T(8,128)(2,1)}, u32[]{:S(2)}, u32[]{:S(2)}) collective-permute-start(bf16[384,1792]{1,0:T(8,128)(2,1)} %collective-permute-done.12), channel_id=1, source_target_pairs={{0,2},{1,3},{2,4},{3,5},{4,6},{5,7},{6,0},{7,1},{8,10},{9,11},{10,... | collective-permute-start | bytes 4128776 | tf_op jit(solution)/shard_map/ppermute | solution.py:557
  195.0 58.7 %collective-permute-start.20 = (bf16[384,1792]{1,0:T(8,128)(2,1)}, bf16[384,1792]{1,0:T(8,128)(2,1)S(1)}, u32[]{:S(2)}, u32[]{:S(2)}) collective-permute-start(bf16[384,1792]{1,0:T(8,128)(2,1)} %collective-permute-done.19), channel_id=1, source_target_pairs={{0,2},{1,3},{2,4},{3,5},{4,6},{5,7},{6,0},{7,1},{8,10},{9,11},{10,... | collective-permute-start | bytes 4128776 | tf_op jit(solution)/shard_map/ppermute | solution.py:557
  200.1 102.9 %collective-permute-start.16 = (bf16[384,1792]{1,0:T(8,128)(2,1)}, bf16[384,1792]{1,0:T(8,128)(2,1)}, u32[]{:S(2)}, u32[]{:S(2)}) collective-permute-start(bf16[384,1792]{1,0:T(8,128)(2,1)} %collective-permute-done.12), channel_id=1, source_target_pairs={{0,1},{1,0},{2,3},{3,2},{4,5},{5,4},{6,7},{7,6},{8,9},{9,8},{10,11... | collective-permute-start | bytes 4128776 | tf_op jit(solution)/shard_map/ppermute | solution.py:557
  224.5 82.5 %collective-permute-start.17 = (bf16[384,1792]{1,0:T(8,128)(2,1)}, bf16[384,1792]{1,0:T(8,128)(2,1)}, u32[]{:S(2)}, u32[]{:S(2)}) collective-permute-start(bf16[384,1792]{1,0:T(8,128)(2,1)} %collective-permute-done.13), channel_id=1, source_target_pairs={{0,1},{1,0},{2,3},{3,2},{4,5},{5,4},{6,7},{7,6},{8,9},{9,8},{10,11... | collective-permute-start | bytes 4128776 | tf_op jit(solution)/shard_map/ppermute | solution.py:557
  253.7 41.9 %collective-permute-start.14 = (bf16[384,1792]{1,0:T(8,128)(2,1)}, bf16[384,1792]{1,0:T(8,128)(2,1)}, u32[]{:S(2)}, u32[]{:S(2)}) collective-permute-start(bf16[384,1792]{1,0:T(8,128)(2,1)} %collective-permute-done.13), channel_id=1, source_target_pairs={{0,2},{1,3},{2,4},{3,5},{4,6},{5,7},{6,0},{7,1},{8,10},{9,11},{10,... | collective-permute-start | bytes 4128776 | tf_op jit(solution)/shard_map/ppermute | solution.py:557
  295.6 37.0 %collective-permute-start.6 = (bf16[5,208,768]{2,1,0:T(8,128)(2,1)}, bf16[5,208,768]{2,1,0:T(8,128)(2,1)S(1)}, u32[]{:S(2)}, u32[]{:S(2)}) collective-permute-start(bf16[5,208,768]{2,1,0:T(8,128)(2,1)} %get-tuple-element.51.x2_ref), channel_id=1, source_target_pairs={{0,16},{8,24},{16,0},{24,8},{1,17},{9,25},{17,1},{25,9},{2,18},{10... | collective-permute-start | bytes 4792328 | tf_op jit(solution)/shard_map/ppermute | solution.py:518
  302.9 36.0 %collective-permute-start.23 = (bf16[384,1792]{1,0:T(8,128)(2,1)}, bf16[384,1792]{1,0:T(8,128)(2,1)S(1)}, u32[]{:S(2)}, u32[]{:S(2)}) collective-permute-start(bf16[384,1792]{1,0:T(8,128)(2,1)} %collective-permute-done.19), channel_id=1, source_target_pairs={{0,1},{1,0},{2,3},{3,2},{4,5},{5,4},{6,7},{7,6},{8,9},{9,8},{10,11... | collective-permute-start | bytes 4128776 | tf_op jit(solution)/shard_map/ppermute | solution.py:557
  306.9 58.8 %collective-permute-start.24 = (bf16[384,1792]{1,0:T(8,128)(2,1)S(1)}, bf16[384,1792]{1,0:T(8,128)(2,1)S(1)}, u32[]{:S(2)}, u32[]{:S(2)}) collective-permute-start(bf16[384,1792]{1,0:T(8,128)(2,1)S(1)} %copy-done.8), channel_id=1, source_target_pairs={{0,1},{1,0},{2,3},{3,2},{4,5},{5,4},{6,7},{7,6},{8,9},{9,8},{10,11... | collective-permute-start | bytes 4128776 | tf_op jit(solution)/shard_map/ppermute | solution.py:557
  332.7 62.6 %collective-permute-start.18 = (bf16[384,1792]{1,0:T(8,128)(2,1)}, bf16[384,1792]{1,0:T(8,128)(2,1)S(1)}, u32[]{:S(2)}, u32[]{:S(2)}) collective-permute-start(bf16[384,1792]{1,0:T(8,128)(2,1)} %collective-permute-done.14), channel_id=1, source_target_pairs={{0,1},{1,0},{2,3},{3,2},{4,5},{5,4},{6,7},{7,6},{8,9},{9,8},{10,11... | collective-permute-start | bytes 4128776 | tf_op jit(solution)/shard_map/ppermute | solution.py:557
  334.3 90.2 %collective-permute-start.7 = (bf16[2,5,208,768]{3,2,1,0:T(8,128)(2,1)S(1)}, bf16[2,5,208,768]{3,2,1,0:T(8,128)(2,1)S(1)}, u32[]{:S(2)}, u32[]{:S(2)}) collective-permute-start(bf16[2,5,208,768]{3,2,1,0:T(8,128)(2,1)S(1)} %pad_maximum_fusion.2), channel_id=1, source_target_pairs={{0,8},{8,0},{16,24},{24,16},{1,9},{9,1},{17,25},{25,17},{2,10},{10... | collective-permute-start | bytes 9584648 | tf_op jit(solution)/shard_map/ppermute | solution.py:518
  335.7 87.0 %collective-permute-start.25 = (bf16[384,1792]{1,0:T(8,128)(2,1)S(1)}, bf16[384,1792]{1,0:T(8,128)(2,1)S(1)}, u32[]{:S(2)}, u32[]{:S(2)}) collective-permute-start(bf16[384,1792]{1,0:T(8,128)(2,1)S(1)} %collective-permute-done.21), channel_id=1, source_target_pairs={{0,1},{1,0},{2,3},{3,2},{4,5},{5,4},{6,7},{7,6},{8,9},{9,8},{10,11... | collective-permute-start | bytes 4128776 | tf_op jit(solution)/shard_map/ppermute | solution.py:557
  574.5 37.7 %collective-permute-start.26 = (bf16[2,5,208,768]{3,2,1,0:T(8,128)(2,1)}, bf16[2,5,208,768]{3,2,1,0:T(8,128)(2,1)}, u32[]{:S(2)}, u32[]{:S(2)}) collective-permute-start(bf16[2,5,208,768]{3,2,1,0:T(8,128)(2,1)} %slice.278), channel_id=1, source_target_pairs={{0,8},{8,0},{16,24},{24,16},{1,9},{9,1},{17,25},{25,17},{2,10},{10... | collective-permute-start | bytes 9584648 | tf_op jit(solution)/shard_map/ppermute | solution.py:518
  595.2 88.9 %collective-permute-start.38 = (bf16[2,2,128,4,96]{2,4,1,0,3:T(8,128)(2,1)S(1)}, bf16[2,2,128,4,96]{2,4,1,0,3:T(8,128)(2,1)}, u32[]{:S(2)}, u32[]{:S(2)}) collective-permute-start(bf16[2,2,128,4,96]{2,4,1,0,3:T(8,128)(2,1)S(1)} %get-tuple-element.88), channel_id=1, source_target_pairs={{1,0},{0,1},{3,2},{2,3},{5,4},{4,5},{7,6},{6,7},{9,8},{8,9},{11,10... | collective-permute-start | bytes 1179656 | tf_op jit(solution)/shard_map/ppermute | solution.py:624
  612.2 75.8 %collective-permute-start.31 = (bf16[5,208,768]{2,1,0:T(8,128)(2,1)}, bf16[5,208,768]{2,1,0:T(8,128)(2,1)}, u32[]{:S(2)}, u32[]{:S(2)}) collective-permute-start(bf16[5,208,768]{2,1,0:T(8,128)(2,1)} %fusion.4), channel_id=1, source_target_pairs={{0,16},{8,24},{16,0},{24,8},{1,17},{9,25},{17,1},{25,9},{2,18},{10... | collective-permute-start | bytes 4792328 | tf_op jit(solution)/shard_map/ppermute | solution.py:518
  617.7 74.2 %collective-permute-start.27 = (bf16[5,208,768]{2,1,0:T(8,128)(2,1)}, bf16[5,208,768]{2,1,0:T(8,128)(2,1)}, u32[]{:S(2)}, u32[]{:S(2)}) collective-permute-start(bf16[5,208,768]{2,1,0:T(8,128)(2,1)} %fusion.3), channel_id=1, source_target_pairs={{0,16},{8,24},{16,0},{24,8},{1,17},{9,25},{17,1},{25,9},{2,18},{10... | collective-permute-start | bytes 4792328 | tf_op jit(solution)/shard_map/ppermute | solution.py:518
  619.6 64.5 %collective-permute-start.37 = (bf16[2,2,128,4,96]{2,4,1,0,3:T(8,128)(2,1)}, bf16[2,2,128,4,96]{2,4,1,0,3:T(8,128)(2,1)}, u32[]{:S(2)}, u32[]{:S(2)}) collective-permute-start(bf16[2,2,128,4,96]{2,4,1,0,3:T(8,128)(2,1)} %add_convert_fusion.2), channel_id=1, source_target_pairs={{2,0},{3,1},{4,2},{5,3},{6,4},{7,5},{0,6},{1,7},{10,8},{11,9},{12,... | collective-permute-start | bytes 1179656 | tf_op jit(solution)/shard_map/ppermute | solution.py:624
  620.4 61.7 %collective-permute-start.29 = (f32[5,8,256]{2,1,0:T(8,128)}, f32[5,8,256]{2,1,0:T(8,128)}, u32[]{:S(2)}, u32[]{:S(2)}) collective-permute-start(f32[5,8,256]{2,1,0:T(8,128)} %slice_bitcast_fusion.3), channel_id=1, source_target_pairs={{0,16},{8,24},{16,0},{24,8},{1,17},{9,25},{17,1},{25,9},{2,18},{10... | collective-permute-start | bytes 122888 | tf_op jit(solution)/shard_map/ppermute | solution.py:518
  622.6 278.7 %reduce-scatter.3.cloned.1.call-start = ((), (), s32[]{:S(2)}) async-start(), calls=%async_computation.3 | async-start | bytes 1486848 | tf_op jit(solution)/shard_map/reduce_scatter | solution.py:660
  682.1 86.2 %collective-permute-start.40 = (bf16[2,2,128,4,96]{2,4,1,0,3:T(8,128)(2,1)}, bf16[2,2,128,4,96]{2,4,1,0,3:T(8,128)(2,1)}, u32[]{:S(2)}, u32[]{:S(2)}) collective-permute-start(bf16[2,2,128,4,96]{2,4,1,0,3:T(8,128)(2,1)} %get-tuple-element.85), channel_id=1, source_target_pairs={{1,0},{0,1},{3,2},{2,3},{5,4},{4,5},{7,6},{6,7},{9,8},{8,9},{11,10... | collective-permute-start | bytes 1179656 | tf_op jit(solution)/shard_map/ppermute | solution.py:624
  686.1 82.1 %collective-permute-start.39 = (bf16[2,2,128,4,96]{2,4,1,0,3:T(8,128)(2,1)}, bf16[2,2,128,4,96]{2,4,1,0,3:T(8,128)(2,1)}, u32[]{:S(2)}, u32[]{:S(2)}) collective-permute-start(bf16[2,2,128,4,96]{2,4,1,0,3:T(8,128)(2,1)} %add_convert_fusion.1), channel_id=1, source_target_pairs={{2,0},{3,1},{4,2},{5,3},{6,4},{7,5},{0,6},{1,7},{10,8},{11,9},{12,... | collective-permute-start | bytes 1179656 | tf_op jit(solution)/shard_map/ppermute | solution.py:624
  (44 other events, 595.2 us)
Sparse Core Ops, SparseCore 0:
  11.6 67.0 all-gather.5
  81.7 100.1 all-gather.3
  622.7 61.2 reduce-scatter.4
  766.8 134.4 reduce-scatter.2

commit v2 on v1

v2 whole, which is shorter than its diff:
```python
import functools
import math

import jax
import jax.numpy as jnp
from jax import lax
from jax.experimental import pallas as pl
from jax.experimental.pallas import tpu as pltpu
from jax.sharding import PartitionSpec as P

D = 768
HEADS = 12
HEAD = 64
NE = 8
LEN = 197
LP = 208
SL = 256
AC = 128
RANK = 16
CAP = 384
IMG = 5
GRP = 4
EL = NE // GRP
ROWS = GRP * CAP
RT = 256
DW = D + AC
WIN = 256
LG = LP + 16
EPS = 1e-06
F32 = jnp.float32
BF = jnp.bfloat16
AXES = ("dp", "fsdp")
VMEM = 60 * 1000 * 1024


def nn(a, b):
    return lax.dot_general(a, b, (((1,), (0,)), ((), ())), preferred_element_type=F32)


def nt(a, b):
    return lax.dot_general(a, b, (((1,), (1,)), ((), ())), preferred_element_type=F32)


def adapter_mask(rows, which):
    lane = lax.broadcasted_iota(jnp.int32, (rows, AC), 1)
    return jnp.where(lane // RANK == which, 1.0, 0.0).astype(F32)


def norm_parts(v):
    mean = jnp.mean(v, axis=-1, keepdims=True)
    cen = v - mean
    var = jnp.mean(cen * cen, axis=-1, keepdims=True)
    inv = lax.rsqrt(var + EPS)
    return cen * inv, inv


def norm_back(g, unit, inv, gain):
    s = g * gain
    return inv * (
        s
        - jnp.mean(s, axis=-1, keepdims=True)
        - unit * jnp.mean(s * unit, axis=-1, keepdims=True)
    )


def params(n):
    return pltpu.CompilerParams(dimension_semantics=("arbitrary",) * n, vmem_limit_bytes=VMEM)


def cost(us):
    return pl.CostEstimate(flops=int(us * 1.15e9), transcendentals=0, bytes_accessed=0)


def whole(shape):
    zeros = (0,) * len(shape)
    return pl.BlockSpec(shape, lambda *_: zeros, pipeline_mode=pl.Buffered(1))


def per_image(shape):
    rest = (0,) * (len(shape) - 1)
    return pl.BlockSpec(shape, lambda i, *_: (i,) + rest)


def fwd_kernel(sets, x_ref, g_ref, wq, wk, wv, wo, b4, a2t, rm, qkv_ref, att_ref, mid_ref, x2_ref, ad_ref, pr_ref, hid):
    mask = adapter_mask(LP, sets[pl.program_id(0)])
    hid[...] = jnp.zeros((LP, D), F32)
    hid[0:LEN, :] = x_ref[0].astype(F32)
    hidden = hid[...]
    unit, _ = norm_parts(hidden)
    x1 = (unit * g_ref[0:1, :]).astype(BF)
    aq = (mask * nn(x1, b4[:, 0:AC])).astype(BF)
    ad_ref[0, :, 0:AC] = aq
    for j, w in enumerate((wq, wk, wv)):
        part = nn(x1, w[...]) + nt(aq, a2t[j * D:(j + 1) * D, :])
        qkv_ref[0, :, j * D:(j + 1) * D] = part.astype(BF)
    lane = lax.broadcasted_iota(jnp.int32, (LP, 2 * HEAD), 1)
    keyok = lax.broadcasted_iota(jnp.int32, (LP, LP), 1) < LEN
    scale = 1.0 / math.sqrt(HEAD)
    for h in range(HEADS // 2):
        at = h * 2 * HEAD
        q = qkv_ref[0, :, at:at + 2 * HEAD]
        k = qkv_ref[0, :, D + at:D + at + 2 * HEAD]
        v = qkv_ref[0, :, 2 * D + at:2 * D + at + 2 * HEAD]
        outs = []
        for half in range(2):
            mine = (lane >= HEAD) if half else (lane < HEAD)
            s = nt(jnp.where(mine, q, jnp.zeros_like(q)), k) * scale
            s = jnp.where(keyok, s, -1e30)
            e = jnp.exp(s - jnp.max(s, axis=-1, keepdims=True))
            p = e * (1.0 / jnp.sum(e, axis=-1, keepdims=True))
            outs.append(nn(p.astype(BF), v))
        att_ref[0, :, at:at + 2 * HEAD] = jnp.where(lane < HEAD, outs[0], outs[1]).astype(BF)
    att = att_ref[0]
    ao = (mask * nn(att, b4[:, AC:2 * AC])).astype(BF)
    ad_ref[0, :, AC:2 * AC] = ao
    middle = hidden + nn(att, wo[...]) + nt(ao, b4[:, 3 * AC:4 * AC])
    mid_ref[0] = middle
    unit2, _ = norm_parts(middle)
    x2 = (unit2 * g_ref[1:2, :]).astype(BF)
    x2_ref[0] = x2
    ar = (mask * nn(x2, b4[:, 2 * AC:3 * AC])).astype(BF)
    ad_ref[0, :, 2 * AC:3 * AC] = ar
    logits = nn(x2, b4[:, 4 * AC:5 * AC]) + nn(ar, rm[...])
    elane = lax.broadcasted_iota(jnp.int32, (LP, AC), 1)
    logits = jnp.where(elane < NE, logits, -1e30)
    e = jnp.exp(logits - jnp.max(logits, axis=-1, keepdims=True))
    probs = e * (1.0 / jnp.sum(e, axis=-1, keepdims=True))
    padded = jnp.concatenate([probs, jnp.zeros((SL - LP, AC), F32)], axis=0)
    pr_ref[0] = jnp.transpose(padded)[0:NE, :]


def attention_forward(block_in, sets, gains, wq, wk, wv, wo, b4, a2t, rm):
    n = block_in.shape[0]
    sq = whole((D, D))
    return pl.pallas_call(
        fwd_kernel,
        grid_spec=pltpu.PrefetchScalarGridSpec(
            num_scalar_prefetch=1,
            grid=(n,),
            in_specs=[per_image((1, LEN, D)), whole((8, D)), sq, sq, sq, sq, sq, whole((3 * D, AC)), whole((AC, AC))],
            out_specs=[
                per_image((1, LP, 3 * D)),
                per_image((1, LP, D)),
                per_image((1, LP, D)),
                per_image((1, LP, D)),
                per_image((1, LP, 3 * AC)),
                per_image((1, NE, SL)),
            ],
            scratch_shapes=[pltpu.VMEM((LP, D), F32)],
        ),
        out_shape=[
            jax.ShapeDtypeStruct((n, LP, 3 * D), BF),
            jax.ShapeDtypeStruct((n, LP, D), BF),
            jax.ShapeDtypeStruct((n, LP, D), F32),
            jax.ShapeDtypeStruct((n, LP, D), BF),
            jax.ShapeDtypeStruct((n, LP, 3 * AC), BF),
            jax.ShapeDtypeStruct((n, NE, SL), F32),
        ],
        compiler_params=params(1),
        cost_estimate=cost(28),
        name="attention_forward",
    )(sets, block_in, gains, wq, wk, wv, wo, b4, a2t, rm)


def window(base, first, limit):
    at = jnp.minimum(base + first // 16 * 16, limit - WIN)
    return pl.multiple_of(at, 16)


def fetch_blocks(at_start, b, sets):
    def copies(k):
        return [pltpu.make_async_copy(refs[k], buf.at[k], sems.at[k]) for refs, buf, sems in sets]

    @pl.when(at_start)
    def _():
        for k in range(GRP):
            for c in copies(k):
                c.start()

    for k in range(GRP):
        @pl.when(b == k)
        def _(k=k):
            for c in copies(k):
                c.wait()


def dispatch_kernel(offs, firsts, sets, slot_ref, gate_ref, *refs):
    x2_refs, cot_refs = refs[0:GRP], refs[GRP:2 * GRP]
    u1_ref, d2_ref, xa_ref, ga_ref, mk_ref, acc, cpad, x2_buf, cot_buf, x2_sem, cot_sem = refs[2 * GRP:]
    e = pl.program_id(0)
    b = pl.program_id(1)

    @pl.when(e == 0)
    def _():
        fetch_blocks(b == 0, b, ((x2_refs, x2_buf, x2_sem), (cot_refs, cot_buf, cot_sem)))

    @pl.when(b == 0)
    def _():
        xa_ref[...] = jnp.zeros_like(xa_ref)
        ga_ref[...] = jnp.zeros_like(ga_ref)
        mk_ref[...] = jnp.zeros_like(mk_ref)

    acc[...] = jnp.zeros_like(acc)
    cpad[...] = jnp.zeros_like(cpad)
    gcol = jnp.transpose(gate_ref[0, 0])
    rows = lax.broadcasted_iota(jnp.int32, (WIN, LP), 0)
    for i in range(IMG):
        first = firsts[(b * EL + e) * IMG + i]

        @pl.when(first < CAP)
        def _():
            at = window(0, first, CAP)
            here = pl.ds(at, WIN)
            pick = jnp.where(rows + at == slot_ref[0, 0, i:i + 1, 0:LP], 1.0, 0.0).astype(BF)
            cpad[0:LEN, :] = cot_buf[b, i].astype(F32)
            gg = (cpad[...] * gcol[0:LP, i:i + 1]).astype(BF)
            acc[here, 0:D] += nn(pick, x2_buf[b, i])
            acc[here, D:2 * D] += nn(pick, gg)
            acc[here, 2 * D:] += nn(pick, adapter_mask(LP, sets[b * IMG + i]).astype(BF))

    mk = acc[:, 2 * D:]
    xs = acc[:, 0:D].astype(BF)
    gs = acc[:, D:2 * D].astype(BF)
    at = pl.multiple_of(offs[e * (GRP + 1) + b], 16)
    here = pl.ds(at, CAP)
    xa_ref[0, here, 0:D] = xs
    xa_ref[0, here, D:DW] = (mk * nn(xs, u1_ref[0])).astype(BF)
    ga_ref[0, here, 0:D] = gs
    ga_ref[0, here, D:DW] = (mk * nn(gs, d2_ref[0])).astype(BF)
    mk_ref[0, here, :] = mk.astype(BF)


def dispatch(offs, firsts, sets, slots, gates, x2, cot, u1, d2):
    return pl.pallas_call(
        dispatch_kernel,
        grid_spec=pltpu.PrefetchScalarGridSpec(
            num_scalar_prefetch=3,
            grid=(EL, GRP),
            in_specs=[
                pl.BlockSpec((1, 1, 8, SL), lambda e, b, *_: (b, e, 0, 0)),
                pl.BlockSpec((1, 1, 8, SL), lambda e, b, *_: (b, e, 0, 0)),
            ] + [pl.BlockSpec(memory_space=pl.ANY)] * (2 * GRP) + [
                pl.BlockSpec((1, D, AC), lambda e, b, *_: (e, 0, 0)),
                pl.BlockSpec((1, D, AC), lambda e, b, *_: (e, 0, 0)),
            ],
            out_specs=[
                pl.BlockSpec((1, ROWS, DW), lambda e, b, *_: (e, 0, 0)),
                pl.BlockSpec((1, ROWS, DW), lambda e, b, *_: (e, 0, 0)),
                pl.BlockSpec((1, ROWS, AC), lambda e, b, *_: (e, 0, 0)),
            ],
            scratch_shapes=[
                pltpu.VMEM((CAP, 2 * D + AC), F32), pltpu.VMEM((LP, D), F32), pltpu.VMEM((GRP, IMG, LP, D), BF),
                pltpu.VMEM((GRP, IMG, LEN, D), BF), pltpu.SemaphoreType.DMA((GRP,)), pltpu.SemaphoreType.DMA((GRP,)),
            ],
        ),
        out_shape=[
            jax.ShapeDtypeStruct((EL, ROWS, DW), BF),
            jax.ShapeDtypeStruct((EL, ROWS, DW), BF),
            jax.ShapeDtypeStruct((EL, ROWS, AC), BF),
        ],
        compiler_params=params(2),
        cost_estimate=cost(1),
        name="dispatch",
    )(offs, firsts, sets, slots, gates, *x2, *cot, u1, d2)


def flip(v):
    return jnp.transpose(v.astype(F32)).astype(BF)


def gelu_parts(pre):
    c0 = math.sqrt(2.0 / math.pi)
    sq = pre * pre
    th = jnp.tanh(c0 * pre * (1.0 + 0.044715 * sq))
    half = 0.5 * (1.0 + th)
    slope = half + 0.5 * pre * (1.0 - th * th) * (c0 * (1.0 + 3 * 0.044715 * sq))
    return pre * half, slope


def fetch_weights(pieces, wbuf, sems, pairs):
    s = pl.program_id(0) * pairs + pl.program_id(1)
    hp = pieces[0].shape[1]

    def copy(t, half):
        e, p = divmod(t, pairs)
        src = pieces[2 * p + half].at[e]
        return pltpu.make_async_copy(src, wbuf.at[t % 2, pl.ds(half * hp, hp)], sems.at[t, half])

    @pl.when(s == 0)
    def _():
        copy(0, 0).start()
        copy(0, 1).start()

    for t in range(EL * pairs):
        @pl.when(s == t)
        def _(t=t):
            if t + 1 < EL * pairs:
                copy(t + 1, 0).start()
                copy(t + 1, 1).start()
            copy(t, 0).wait()
            copy(t, 1).wait()

    return s % 2


def expert_first_kernel(pairs, offs, xa_ref, ga_ref, *refs):
    pieces = refs[:2 * pairs]
    a1, a2, go_ref, at_ref, wbuf, sems = refs[2 * pairs:]
    e = pl.program_id(0)
    total = offs[e * (GRP + 1) + GRP]
    tiles = (total + (RT - 1)) // RT
    cur = fetch_weights(pieces, wbuf, sems, pairs)

    @pl.when(pl.program_id(1) == 0)
    def _():
        a1[...] = jnp.zeros_like(a1)
        a2[...] = jnp.zeros_like(a2)
        at_ref[0] = flip(xa_ref[0, :, D:DW])
        at_ref[1] = flip(ga_ref[0, :, D:DW])

    acc_u = jnp.zeros((AC, wbuf.shape[1]), F32)

    def step(t, carry):
        gu, gd = carry
        here = pl.ds(pl.multiple_of(t * RT, RT), RT)
        wu = wbuf[cur, :, 0:DW]
        wd = wbuf[cur, :, DW:2 * DW]
        pre = nt(xa_ref[0, here, :], wu)
        gact = nt(ga_ref[0, here, :], wd)
        act, slope = gelu_parts(pre)
        act = act.astype(BF)
        gp = (slope * gact).astype(BF)
        a1[0, here, :] += nn(act, wd)
        a2[0, here, :] += nn(gp, wu)
        return gu + nn(at_ref[0, :, here], gp), gd + nn(at_ref[1, :, here], act)

    gu, gd = lax.fori_loop(0, tiles, step, (acc_u, acc_u))
    go_ref[0, 0, 0] = jnp.transpose(gu).astype(BF)
    go_ref[0, 0, 1] = jnp.transpose(gd).astype(BF)


def expert_first(offs, xa, ga, pieces):
    pairs = len(pieces) // 2
    hp = pieces[0].shape[1]
    rows = pl.BlockSpec((1, ROWS, DW), lambda e, p, *_: (e, 0, 0))
    anyspace = pl.BlockSpec(memory_space=pl.ANY)
    return pl.pallas_call(
        functools.partial(expert_first_kernel, pairs),
        grid_spec=pltpu.PrefetchScalarGridSpec(
            num_scalar_prefetch=1,
            grid=(EL, pairs),
            in_specs=[rows, rows] + [anyspace] * len(pieces),
            out_specs=[rows, rows, pl.BlockSpec((1, 1, 2, 2 * hp, AC), lambda e, p, *_: (p, e, 0, 0, 0))],
            scratch_shapes=[pltpu.VMEM((2, AC, ROWS), BF), pltpu.VMEM((2, 2 * hp, 2 * DW), BF), pltpu.SemaphoreType.DMA((EL * pairs, 2))],
        ),
        out_shape=[
            jax.ShapeDtypeStruct((EL, ROWS, DW), F32),
            jax.ShapeDtypeStruct((EL, ROWS, DW), F32),
            jax.ShapeDtypeStruct((pairs, EL, 2, 2 * hp, AC), BF),
        ],
        compiler_params=params(2),
        cost_estimate=cost(56),
        name="expert_first",
    )(offs, xa, ga, *pieces)


def expert_last_kernel(offs, xa_ref, ga_ref, mk_ref, p1, p2, u1_ref, d2_ref, w0, w1, ob_ref, gb_ref, go_ref, gf_ref,
                       wbuf, sems):
    e = pl.program_id(0)
    total = offs[e * (GRP + 1) + GRP]
    tiles = (total + (RT - 1)) // RT
    cur = fetch_weights((w0, w1), wbuf, sems, 1)
    ob_ref[...] = jnp.zeros_like(ob_ref)
    gb_ref[...] = jnp.zeros_like(gb_ref)
    hb = wbuf.shape[1]

    def step(t, carry):
        gu, gd, gud, gdu = carry
        here = pl.ds(pl.multiple_of(t * RT, RT), RT)
        wu = wbuf[cur, :, 0:DW]
        wd = wbuf[cur, :, DW:2 * DW]
        x = xa_ref[0, here, :]
        g = ga_ref[0, here, :]
        pre = nt(x, wu)
        gact = nt(g, wd)
        act, slope = gelu_parts(pre)
        act = act.astype(BF)
        gp = (slope * gact).astype(BF)
        t1 = p1[0, here, :] + nn(act, wd)
        t2 = p2[0, here, :] + nn(gp, wu)
        mk = mk_ref[0, here, :].astype(F32)
        adt = (mk * t1[:, D:DW]).astype(BF)
        aut = (mk * t2[:, D:DW]).astype(BF)
        ob_ref[0, here, :] = (t1[:, 0:D] + nt(adt, d2_ref[0])).astype(BF)
        gb_ref[0, here, :] = (t2[:, 0:D] + nt(aut, u1_ref[0])).astype(BF)
        return (gu + nn(flip(x[:, D:DW]), gp), gd + nn(flip(g[:, D:DW]), act),
                gud + nn(flip(aut), x[:, 0:D]), gdu + nn(flip(adt), g[:, 0:D]))

    zero = jnp.zeros((AC, hb), F32)
    zed = jnp.zeros((AC, D), F32)
    gu, gd, gud, gdu = lax.fori_loop(0, tiles, step, (zero, zero, zed, zed))
    go_ref[0, 0] = jnp.transpose(gu).astype(BF)
    go_ref[0, 1] = jnp.transpose(gd).astype(BF)
    gf_ref[0, 0] = jnp.transpose(gud).astype(BF)
    gf_ref[0, 1] = jnp.transpose(gdu).astype(BF)


def expert_last(offs, xa, ga, mk, a1, a2, u1, d2, pieces):
    hp = pieces[0].shape[1]
    each = lambda *shape: pl.BlockSpec((1,) + shape, lambda e, p, *_: (e,) + (0,) * len(shape))
    anyspace = pl.BlockSpec(memory_space=pl.ANY)
    return pl.pallas_call(
        expert_last_kernel,
        grid_spec=pltpu.PrefetchScalarGridSpec(
            num_scalar_prefetch=1,
            grid=(EL, 1),
            in_specs=[each(ROWS, DW), each(ROWS, DW), each(ROWS, AC), each(ROWS, DW), each(ROWS, DW), each(D, AC), each(D, AC),
                      anyspace, anyspace],
            out_specs=[each(ROWS, D), each(ROWS, D), each(2, 2 * hp, AC), each(2, D, AC)],
            scratch_shapes=[pltpu.VMEM((2, 2 * hp, 2 * DW), BF), pltpu.SemaphoreType.DMA((EL, 2))],
        ),
        out_shape=[
            jax.ShapeDtypeStruct((EL, ROWS, D), BF),
            jax.ShapeDtypeStruct((EL, ROWS, D), BF),
            jax.ShapeDtypeStruct((EL, 2, 2 * hp, AC), BF),
            jax.ShapeDtypeStruct((EL, 2, D, AC), BF),
        ],
        compiler_params=params(2),
        cost_estimate=cost(34),
        name="expert_last",
    )(offs, xa, ga, mk, a1, a2, u1, d2, *pieces)


def combine_kernel(lo, n, offs, firsts, first_expert, ob, gb, slot_ref, gate_ref, *refs):
    b = pl.program_id(0)
    cot_refs, outs = refs[:GRP], refs[GRP:]
    y_ref, g_ref, cot_buf, cot_sem = outs[6:]
    fetch_blocks(b == 0, b, (([r.at[lo:lo + n] for r in cot_refs], cot_buf, cot_sem),))
    lanes = lax.broadcasted_iota(jnp.int32, (LP, WIN), 1)
    dlane = lax.broadcasted_iota(jnp.int32, (LP, AC), 1)
    scol = [jnp.transpose(slot_ref[0, e].astype(F32)) for e in range(EL)]
    gcol = [jnp.transpose(gate_ref[0, e]) for e in range(EL)]
    for i in range(n):
        y = jnp.zeros((LP, D), F32)
        g = jnp.zeros((LP, D), F32)
        dots = jnp.zeros((LP, AC), F32)
        cot = jnp.concatenate([cot_buf[b, i].astype(F32), jnp.zeros((LP - LEN, D), F32)], axis=0)
        for e in range(EL):
            first = jnp.minimum(firsts[(b * EL + e) * IMG + lo + i], CAP - 1)
            base = offs[e * (GRP + 1) + b]
            at = window(base, first, ROWS)
            here = pl.ds(at, WIN)
            slot = scol[e][0:LP, lo + i:lo + i + 1]
            pick = jnp.where(slot == (lanes + (at - base)).astype(F32), 1.0, 0.0).astype(BF)
            ye = nn(pick, ob[e, here, :])
            g = g + nn(pick, gb[e, here, :])
            y = y + gcol[e][0:LP, lo + i:lo + i + 1] * ye
            dot = jnp.sum(ye * cot, axis=-1, keepdims=True)
            dots = dots + jnp.where(dlane == first_expert[0] + e, dot, 0.0)
        y_ref[i] = y.astype(BF)
        g_ref[i, 0:LP] = g.astype(BF)
        full = jnp.transpose(jnp.concatenate([dots, jnp.zeros((SL - LP, AC), F32)], axis=0))[0:16, :]
        high = full.astype(BF)
        g_ref[i, LP:LG, 0:SL] = high
        g_ref[i, LP:LG, SL:2 * SL] = (full - high.astype(F32)).astype(BF)
        g_ref[i, LP:LG, 2 * SL:] = jnp.zeros((LG - LP, D - 2 * SL), BF)
    for v, mine, far, core in ((y_ref, outs[0], outs[1], outs[2]), (g_ref, outs[3], outs[4], outs[5])):
        for when, ref in ((0, mine), (1, far), (2, core), (3, core)):
            @pl.when(b == when)
            def _(ref=ref, v=v):
                if len(ref.shape) == 4:
                    ref[0] = v[...]
                else:
                    ref[...] = v[...]


def combine(lo, n, offs, firsts, first_expert, ob, gb, slots, gates, cot):
    block = lambda *shape: pl.BlockSpec((1,) + shape, lambda b, *_: (b,) + (0,) * len(shape))
    return pl.pallas_call(
        functools.partial(combine_kernel, lo, n),
        grid_spec=pltpu.PrefetchScalarGridSpec(
            num_scalar_prefetch=3,
            grid=(GRP,),
            in_specs=[whole((EL, ROWS, D)), whole((EL, ROWS, D)), block(EL, 8, SL), block(EL, 8, SL)] + [pl.BlockSpec(memory_space=pl.ANY)] * GRP,
            out_specs=[spec for rows in (LP, LG) for spec in (
                whole((n, rows, D)), whole((n, rows, D)), pl.BlockSpec((1, n, rows, D), lambda b, *_: (jnp.maximum(b - 2, 0), 0, 0, 0)))],
            scratch_shapes=[pltpu.VMEM((n, LP, D), BF), pltpu.VMEM((n, LG, D), BF), pltpu.VMEM((GRP, n, LEN, D), BF),
                            pltpu.SemaphoreType.DMA((GRP,))],
        ),
        out_shape=[jax.ShapeDtypeStruct(shape, BF) for rows in (LP, LG) for shape in ((n, rows, D), (n, rows, D), (2, n, rows, D))],
        compiler_params=params(1),
        cost_estimate=cost(6 * n),
        name="combine",
    )(offs, firsts, first_expert, ob, gb, slots, gates, *cot)


def bwd_kernel(lo, last, r, sets, live, order, x_ref, cot_ref, go_ref, gc_ref, gy_ref, pr_ref, mid_ref, qkv_ref, att_ref, x2_ref, ad_ref, g_ref,
               wq, wk, wv, wo, b4, a2t, rm, *refs):
    if last:
        pacc, _, ig_ref, mine_ref, other_ref, hid, gq, acc, flat = refs
    else:
        ig_ref, acc_ref, hid, gq, acc = refs
    i = pl.program_id(0) + lo
    mask = adapter_mask(LP, sets[i])
    alive = live[i].astype(F32)
    aq = ad_ref[0, :, 0:AC]
    ao = ad_ref[0, :, AC:2 * AC]
    ar = ad_ref[0, :, 2 * AC:3 * AC]

    @pl.when(i == lo)
    def _():
        acc[...] = pacc[...] if lo else jnp.zeros_like(acc)

    tr = flip
    gsum = go_ref[0].astype(F32) + gc_ref[0, 0].astype(F32) + gy_ref[0].astype(F32)
    dots = gsum[LP:LP + NE, 0:SL] + gsum[LP:LP + NE, SL:2 * SL]

    hid[...] = jnp.zeros((LP, D), F32)
    hid[0:LEN, :] = cot_ref[0].astype(F32) * alive
    gfin = hid[...]
    elane = lax.broadcasted_iota(jnp.int32, (LP, AC), 1)
    zrow = jnp.zeros((AC - NE, SL), F32)
    probs = jnp.transpose(jnp.concatenate([pr_ref[0], zrow], axis=0))[0:LP, :]
    gprobs = jnp.transpose(jnp.concatenate([dots, zrow], axis=0))[0:LP, :]
    gl = probs * (gprobs - jnp.sum(gprobs * probs, axis=-1, keepdims=True))
    gl = jnp.where(elane < NE, gl, 0.0).astype(BF)
    gar = (mask * nt(gl, rm[...])).astype(BF)
    gtwo = gsum[0:LP] + nt(gl, b4[:, 4 * AC:5 * AC]) + nt(gar, b4[:, 2 * AC:3 * AC])
    middle = mid_ref[0]
    unit2, inv2 = norm_parts(middle)
    gmid = gfin + norm_back(gtwo, unit2, inv2, g_ref[1:2, :])
    gbr = gmid.astype(BF)
    gao = (mask * nn(gbr, b4[:, 3 * AC:4 * AC])).astype(BF)
    gatt = (nt(gbr, wo[...]) + nt(gao, b4[:, AC:2 * AC])).astype(BF)
    gart = tr(gar)
    acc[:, 4 * D:5 * D] += nn(tr(gao), att_ref[0])
    acc[:, 5 * D:6 * D] += nn(tr(ao), gbr)
    acc[:, 6 * D:7 * D] += nn(gart, x2_ref[0])
    acc[:, 7 * D:] += nn(tr(ar), gl)

    lane = lax.broadcasted_iota(jnp.int32, (LP, 2 * HEAD), 1)
    keyok = lax.broadcasted_iota(jnp.int32, (LP, LP), 0) < LEN
    drow = lax.broadcasted_iota(jnp.int32, (2 * HEAD, LP), 0)
    scale = 1.0 / math.sqrt(HEAD)
    for h in range(HEADS // 2):
        at = h * 2 * HEAD
        q = qkv_ref[0, :, at:at + 2 * HEAD]
        k = qkv_ref[0, :, D + at:D + at + 2 * HEAD]
        v = qkv_ref[0, :, 2 * D + at:2 * D + at + 2 * HEAD]
        go = gatt[:, at:at + 2 * HEAD]
        kt = tr(k)
        dq, dk, dv = [], [], []
        for half in range(2):
            mine = (lane >= HEAD) if half else (lane < HEAD)
            s = nt(k, jnp.where(mine, q, jnp.zeros_like(q))) * scale
            s = jnp.where(keyok, s, -1e30)
            ex = jnp.exp(s - jnp.max(s, axis=0, keepdims=True))
            p = ex * (1.0 / jnp.sum(ex, axis=0, keepdims=True))
            dv.append(nn(p.astype(BF), go))
            dp = nt(v, jnp.where(mine, go, jnp.zeros_like(go)))
            gs = (p * (dp - jnp.sum(dp * p, axis=0, keepdims=True))).astype(BF)
            dk.append(nn(gs, q))
            dq.append(nn(kt, gs))
        dqt = jnp.where(drow < HEAD, dq[0], dq[1]) * scale
        gq[:, at:at + 2 * HEAD] = jnp.transpose(dqt).astype(BF)
        gq[:, D + at:D + at + 2 * HEAD] = (jnp.where(lane < HEAD, dk[0], dk[1]) * scale).astype(BF)
        gq[:, 2 * D + at:2 * D + at + 2 * HEAD] = jnp.where(lane < HEAD, dv[0], dv[1]).astype(BF)
    gqkv = gq[...]
    gaq = (mask * nn(gqkv, a2t[...])).astype(BF)
    hid[...] = jnp.zeros((LP, D), F32)
    hid[0:LEN, :] = x_ref[0].astype(F32)
    unit1, inv1 = norm_parts(hid[...])
    x1 = (unit1 * g_ref[0:1, :]).astype(BF)
    acc[:, 0:D] += nn(tr(gaq), x1)
    acc[:, D:4 * D] += nn(tr(aq), gqkv)
    gone = nt(gaq, b4[:, 0:AC])
    for j, w in enumerate((wq, wk, wv)):
        gone = gone + nt(gqkv[:, j * D:(j + 1) * D], w[...])
    ig = gmid + norm_back(gone, unit1, inv1, g_ref[0:1, :])
    ig_ref[0] = ig[0:LEN, :].astype(BF)

    @pl.when(pl.program_id(0) == pl.num_programs(0) - 1)
    def _():
        if not last:
            acc_ref[...] = acc[...]
            return
        for c in range(acc.shape[1] // AC):
            flat[c * AC:(c + 1) * AC, :] = jnp.transpose(acc[:, c * AC:(c + 1) * AC])
        half = mine_ref.shape[0]

        def place(p, carry):
            for ref, at in ((mine_ref, 0), (other_ref, half)):
                dev = order[at + p]
                row, base = 0, 0
                for w in (1, 3, 1, 1, 1):
                    here = pl.ds(pl.multiple_of(base + w * r * dev, 8), w * r)
                    ref[p, row:row + w * r, :] = flat[here, :].astype(BF)
                    row += w * r
                    base += w * D
                ref[p, row:row + NE, :] = flat[7 * D:7 * D + NE, :].astype(BF)
            return carry

        lax.fori_loop(0, half, place, 0)


def backward(lo, n, ndev, sets, live, order, block_in, cot, g, gc, gy, probs, mid, qkv, att, x2, ad, gains, wq, wk, wv, wo, b4, a2t,
             rm, prev):
    sq = whole((D, D))
    na = 7 * D + AC
    r = D // ndev
    last = lo > 0
    packed = (ndev // 2, 7 * r + NE, AC)

    def image(*shape):
        return pl.BlockSpec((1,) + shape, lambda i, *_: (i + lo,) + (0,) * len(shape))

    part = lambda *shape: pl.BlockSpec((1, 1) + shape, lambda i, *_: (0, i) + (0,) * len(shape))
    in_specs = [
        image(LEN, D), image(LEN, D), per_image((1, LG, D)), part(LG, D), per_image((1, LG, D)), image(NE, SL),
        image(LP, D), image(LP, 3 * D), image(LP, D), image(LP, D),
        image(LP, 3 * AC), whole((8, D)), sq, sq, sq, sq, sq, whole((3 * D, AC)), whole((AC, AC)),
    ]
    args = [block_in, cot, g, gc, gy, probs, mid, qkv, att, x2, ad, gains, wq, wk, wv, wo, b4, a2t, rm]
    scratch = [pltpu.VMEM((LP, D), F32), pltpu.VMEM((LP, 3 * D), BF), pltpu.VMEM((AC, na), F32)]
    alias = {}
    if last:
        in_specs += [whole((AC, na)), pl.BlockSpec(memory_space=pl.ANY)]
        args += [prev[1], prev[0]]
        alias = {3 + len(args) - 1: 0}
        scratch.append(pltpu.VMEM((na, AC), F32))
        tails = [packed, packed]
    else:
        tails = [(AC, na)]
    return pl.pallas_call(
        functools.partial(bwd_kernel, lo, last, r),
        grid_spec=pltpu.PrefetchScalarGridSpec(
            num_scalar_prefetch=3,
            grid=(n,),
            in_specs=in_specs,
            out_specs=[image(LEN, D)] + [whole(t) for t in tails],
            scratch_shapes=scratch,
        ),
        out_shape=[jax.ShapeDtypeStruct(block_in.shape, BF)] + [jax.ShapeDtypeStruct(t, BF if last else F32) for t in tails],
        input_output_aliases=alias,
        compiler_params=params(1),
        cost_estimate=cost(12 * n),
        name="backward",
    )(sets, live, order, *args)


def on_device(dpn, fsn, block_in, cotangent, image_live, image_set, expert_routes, expert_slots, gain_attn, gain_moe, w_qkv, w_out,
              w_router, w_up, w_down, qkv_first, qkv_second, out_first, out_second, router_first, router_second, up_first,
              up_second, down_first, down_second):
    ndev = dpn * fsn
    nx = 1 << ((fsn.bit_length() - 1) // 2)
    nz = fsn // nx
    ng = dpn // GRP
    r = D // ndev
    hs = w_up.shape[2]
    d = lax.axis_index("dp")
    q = d % GRP
    rings = [
        (nz, "fsdp", [(f, ((f // nx + 1) % nz) * nx + f % nx) for f in range(fsn)]),
        (nx, "fsdp", [(f, (f // nx) * nx + (f % nx + 1) % nx) for f in range(fsn)]),
        (ng, "dp", [(a, (a + GRP) % dpn) for a in range(dpn)]),
    ]

    def swap(v, bit):
        return lax.ppermute(v, "dp", [(a, a ^ bit) for a in range(dpn)])

    rel = [0, 2, 1, 3]

    tr = jnp.transpose
    small = jnp.concatenate(
        [
            qkv_first, out_first, router_first, tr(out_second),
            jnp.concatenate([w_router, gain_attn[:, None], gain_moe[:, None], jnp.zeros((r, AC - NE - 2), BF)], axis=1),
            jnp.zeros((r, AC), BF).at[0, 0:router_second.shape[0]].set(router_second),
        ],
        axis=1,
    )
    a2s = tr(qkv_second).reshape(3, r, AC)
    second = jnp.concatenate([a2s[0], a2s[1], a2s[2], jnp.zeros((r, 3 * AC), BF)], axis=1)
    front = jnp.stack([w_qkv[:, 0:D], w_qkv[:, D:2 * D], w_qkv[:, 2 * D:], w_out, small, second])
    front = lax.all_gather(front.reshape(6 * r, D), AXES, axis=0, tiled=True).reshape(ndev, 6, r, D)
    wq, wk, wv, wo, b4 = (front[:, j].reshape(D, D) for j in range(5))
    a2t = tr(front[:, 5, :, 0:3 * AC].reshape(ndev, r, 3, AC), (0, 2, 1, 3)).reshape(3 * D, AC)
    gains = jnp.concatenate(
        [b4[:, 4 * AC + NE].reshape(1, D), b4[:, 4 * AC + NE + 1].reshape(1, D), jnp.zeros((6, D), BF)], axis=0
    ).astype(F32)
    rm = front[:, 4, 0, 5 * AC:5 * AC + router_second.shape[0]].reshape(AC, NE)
    rm = jnp.pad(rm, ((0, 0), (0, AC - NE)))

    after = lambda v, *deps: lax.optimization_barrier((v,) + deps)[0]

    ef = jnp.concatenate([up_first, tr(down_second, (0, 2, 1))], axis=2).reshape(GRP, EL, r, 2 * AC)
    own = [lax.dynamic_index_in_dim(ef, q ^ j, 0, keepdims=False) for j in range(GRP)]
    sib_ef = swap(jnp.stack([own[1], own[3]]), 1)
    got_ef = swap(jnp.stack([own[2], sib_ef[1]]), 2)
    mine_ef = jnp.stack([own[0], sib_ef[0], got_ef[0], got_ef[1]])
    wpk = jnp.concatenate([tr(w_up, (0, 2, 1)), tr(up_second, (0, 2, 1)), tr(w_down, (0, 2, 1)), tr(down_first, (0, 2, 1))], axis=2)
    wpk = wpk.reshape(GRP, EL, hs, 2 * DW)
    own = [lax.dynamic_index_in_dim(wpk, q ^ j, 0, keepdims=False) for j in range(GRP)]
    sib = swap(jnp.stack([own[1], own[3]], axis=1), 1)
    near = jnp.stack([own[0], sib[:, 0]], axis=1).reshape(EL, 2 * hs, 2 * DW)
    send, _ = lax.optimization_barrier((jnp.stack([own[2], sib[:, 1]], axis=1), got_ef))
    got = swap(send, 2)
    far = got.reshape(EL, 2 * hs, 2 * DW)

    def hop(v, ring):
        return lax.ppermute(v, ring[1], ring[2])

    up = [[(u, ((u // nx + k) % nz) * nx + u % nx) for u in range(fsn)] for k in range(nz)]
    all_ef = jnp.concatenate([mine_ef] + [lax.ppermute(mine_ef, "fsdp", up[k]) for k in range(1, nz)])
    near, all_ef = lax.optimization_barrier((near, all_ef))
    for n, axis, perm in rings[1:]:
        rows = [all_ef]
        for _ in range(n - 1):
            rows.append(lax.ppermute(rows[-1], axis, perm))
        all_ef = jnp.concatenate(rows)
    near_x, all_ef = lax.optimization_barrier((near, all_ef))
    zn, xn, far = lax.optimization_barrier((hop(near, rings[0]), hop(near_x, rings[1]), far))
    z_row = [jnp.concatenate([near, far], axis=1), jnp.concatenate([zn, hop(far, rings[0])], axis=1)]
    x_row = [jnp.concatenate([xn, hop(far, rings[1])], axis=1)]
    z0, x0, block_in_late = lax.optimization_barrier((z_row[1], x_row[0], block_in))
    z_row[1], x_row[0] = z0, x0
    route = expert_routes.reshape(IMG, LEN, 2)
    slot = expert_slots.reshape(IMG, LEN, 2)
    ids = jnp.arange(NE, dtype=jnp.int32)[None, :, None, None]
    ok = (route[:, None] == ids) & (slot[:, None] >= 0) & (image_live[:, None, None, None] > 0)
    mine_slots = jnp.max(jnp.where(ok, slot[:, None], -1), axis=-1)
    mine_slots = jnp.pad(mine_slots, ((0, 8 - IMG), (0, 0), (0, SL - LEN)), constant_values=-1)
    mine_slots = tr(mine_slots, (1, 0, 2))

    def members(v):
        far = swap(v, 2)
        return [v, far, swap(v, 1), swap(far, 1)]

    def group(v):
        return jnp.stack(members(v))

    all_slots = lax.dynamic_slice_in_dim(group(mine_slots), q * EL, EL, axis=1)
    counts = jnp.max(all_slots, axis=(2, 3)) + 1
    steps = (counts + 15) // 16 * 16
    offs = jnp.concatenate([jnp.zeros((1, EL), jnp.int32), jnp.cumsum(steps, axis=0)], axis=0)
    offs = tr(offs).reshape(-1).astype(jnp.int32)
    firsts = jnp.min(jnp.where(all_slots >= 0, all_slots, CAP), axis=3)[:, :, 0:IMG].reshape(-1)
    all_sets = group(image_set).reshape(-1)
    cots = members(after(cotangent, got))

    f = lax.axis_index("fsdp")
    devs = jnp.arange(ndev, dtype=jnp.int32)
    dd, df = devs // fsn, devs % fsn
    gap = lambda mine, other, n: (mine - other) % n
    spot = (gap(d // GRP, dd // GRP, ng) * nx + gap(f % nx, df % nx, nx)) * nz + gap(f // nx, df // nx, nz)
    ef = jnp.take(all_ef, spot * GRP + ((dd % GRP) ^ q), axis=0)
    ef = tr(ef, (1, 0, 2, 3)).reshape(EL, D, 2 * AC)
    u1, d2 = ef[:, :, 0:AC], ef[:, :, AC:]

    offs, firsts, all_sets, block_in_late, *cots = lax.optimization_barrier((offs, firsts, all_sets, block_in_late, *cots))
    qkv, att, mid, x2, ad, probs = attention_forward(block_in_late, image_set, gains, wq, wk, wv, wo, b4, a2t, rm)
    for k in range(2, nz):
        z_row.append(hop(z_row[-1], rings[0]))
        x_row.append(hop(z_row[k - 1], rings[1]))
        if k == 2:
            z_row[k], x_row[k - 1], x2s = lax.optimization_barrier((z_row[k], x_row[k - 1], x2))
    x2s = members(x2s)
    gates = lax.dynamic_slice_in_dim(tr(group(jnp.pad(probs, ((0, 8 - IMG), (0, 0), (0, 0)))), (0, 2, 1, 3)), q * EL, EL, axis=1)

    xa, ga, mk = dispatch(offs, firsts, all_sets, all_slots, gates, x2s, cots, u1, d2)
    z_row[-1], x_row[-1], xa = lax.optimization_barrier((z_row[-1], x_row[-1], xa))
    x_row.append(hop(z_row[nz - 1], rings[1]))
    rows = [z_row, x_row]
    for _ in range(2, nx):
        rows.append([hop(v, rings[1]) for v in rows[-1]])
    held = [v for row in rows for v in row]
    rows = [held]
    for _ in range(1, ng):
        rows.append([hop(v, rings[2]) for v in rows[-1]])
    held = [v for row in rows for v in row]
    join = len(held) // 8
    pieces = [held[k] if join == 1 else jnp.concatenate(held[k * join:(k + 1) * join], axis=1) for k in range(8)]
    a1, a2, go = expert_first(offs, xa, ga, pieces[:6])
    go = [go[k] for k in range(3)]
    ob, gb, gl, gf = expert_last(offs, xa, ga, mk, a1, a2, u1, d2, pieces[6:])

    k = jnp.arange(ng * nx * nz, dtype=jnp.int32)
    kg, kx, kz = k // (nx * nz), k // nz % nx, k % nz
    column = (f // nx - kz) % nz * nx + (f % nx - kx) % nx
    rank = ((d // GRP - kg) % ng * GRP)[:, None] + (q ^ jnp.arange(GRP, dtype=jnp.int32))[None, :]
    spot = (rank * fsn + column[:, None]).reshape(-1)
    gf = jnp.take(gf.reshape(EL, 2, ndev, r, AC), spot, axis=2).reshape(EL, 2, ng * nx, nz * GRP * r, AC)
    simple = ng == 1 and nx == 2
    xback = [(v, u) for u, v in rings[1][2]]
    if simple:
        near_x = lax.ppermute(go[2], "fsdp", xback)
        near_x, ob = lax.optimization_barrier((near_x, ob))
        far_x = lax.ppermute(jnp.concatenate([gl, gf[:, :, 1]], axis=2), "fsdp", xback)

    fe = (q * EL).reshape(1)
    cut = 2
    parts = []
    for lo, n in ((0, cut), (cut, IMG - cut)):
        ym, yf, yp, gm, gfar, gp = combine(lo, n, offs, firsts, fe, ob, gb, all_slots, gates, cots)
        gc = swap(gp, 1)
        gs = (gfar.astype(F32) + gc[1].astype(F32)).astype(BF)
        gc, ob = lax.optimization_barrier((gc, ob))
        parts.append((lo, n, (ym, yf, yp), gm, gc, swap(gs, 2)))

    (lo, n, ya, ga1, gca, gya), (lo2, n2, yb, gb1, gcb, gyb) = parts
    spots = jnp.arange(ndev, dtype=jnp.int32)
    order = (q ^ jnp.array([0, 2, 1, 3], jnp.int32)[spots // fsn % GRP]) * fsn + (f + spots % fsn) % fsn
    order = (order if ng == 1 else spots).astype(jnp.int32)
    yca = swap(ya[2], 1)
    ycb = swap(yb[2], 1)
    add = lambda u, v: (u.astype(F32) + v.astype(F32)).astype(BF)
    ga1, gcb = lax.optimization_barrier((ga1, gcb))
    shared = (probs, mid, qkv, att, x2, ad, gains, wq, wk, wv, wo, b4, a2t, rm)
    first = backward(lo, n, ndev, image_set, image_live, order, block_in, cotangent, ga1, gca, gya, *shared, None)

    head, gyb, yca, ycb = lax.optimization_barrier((first[0], gyb, yca, ycb))
    ysend = jnp.concatenate([add(ya[1], yca[1]), add(yb[1], ycb[1])], axis=0)
    if simple:
        near_x, far_x, _ = lax.optimization_barrier((near_x, far_x, gyb))
        cut = GRP * hs
        s0 = add(go[0], near_x)
        s1 = add(go[1], far_x[:, :, 0:2 * cut])
        sf = add(gf[:, :, 0], far_x[:, :, 2 * cut:])
        hid = [s0[:, :, 0:cut], s0[:, :, cut:], s1[:, :, 0:cut], s1[:, :, cut:]]
        cols = [jnp.concatenate([hid[k], sf[:, :, k * GRP * r:(k + 1) * GRP * r]], axis=2) for k in range(nz)]
    else:
        cut = go[0].shape[2] * 4 // (ng * nx * nz)
        cols = []
        for k, v in enumerate(p for pair in go + [gl] for p in jnp.split(pair, pair.shape[2] // cut, axis=2)):
            at = k % nz * GRP * r
            cols.append(jnp.concatenate([v, gf[:, :, k // nz, at:at + GRP * r]], axis=2))
        for m, axis, perm in rings[2:0:-1]:
            back = [(v, u) for u, v in perm]
            part = len(cols) // m
            rows = [cols[k * part:(k + 1) * part] for k in range(m)]
            cols = rows[m - 1]
            for k in range(m - 2, -1, -1):
                cols = [add(lax.ppermute(v, axis, back), u) for v, u in zip(cols, rows[k])]
    down = [lax.ppermute(cols[k], "fsdp", [(u, ((u // nx - k) % nz) * nx + u % nx) for u in range(fsn)]) for k in range(1, nz)]
    yy = swap(ysend, 2)
    input_grad, mine, other = backward(lo2, n2, ndev, image_set, image_live, order, block_in, cotangent, gb1, gcb, gyb, *shared,
                                       (head, first[1]))
    mine, other, yy, *down = lax.optimization_barrier((mine, other, yy, *down))
    yya, yyb = yy[0:n], yy[n:]

    eg = (cols[0].astype(F32) + sum(v.astype(F32) for v in down)).astype(BF)
    eg = [jnp.concatenate([eg[:, :, j * hs:(j + 1) * hs], eg[:, :, GRP * hs + j * r:GRP * hs + (j + 1) * r]], axis=2) for j in range(GRP)]
    sib = swap(jnp.stack([eg[1], eg[3]]), 1)
    got = swap(jnp.stack([eg[2], sib[1]]), 2)
    got = jnp.concatenate([eg[0][None], sib[0:1], got], axis=0)
    at = jnp.stack([q ^ j for j in range(GRP)])
    eg = jnp.take(got, jnp.argsort(at), axis=0).reshape(NE, 2, hs + r, AC).astype(F32)
    ff = eg[:, :, hs:]
    eg = tr(eg[:, :, 0:hs], (1, 0, 3, 2))
    outs = []
    for at, m, y, yc, yy in ((lo, n, ya, yca, yya), (lo2, n2, yb, ycb, yyb)):
        total = mid[at:at + m] + y[0].astype(F32) + yc[0].astype(F32) + yy.astype(F32)
        outs.append(total[:, 0:LEN])
    block_out = (jnp.concatenate(outs, axis=0) * image_live.astype(F32)[:, None, None]).astype(BF)

    nrs = router_second.shape[0]
    if ng == 1:
        got = swap(other, 1)
        far = swap(add(mine[fsn:], got[fsn:]), 2)
        sm = add(add(mine[0:fsn], got[0:fsn]), far)
        total = sm[0].astype(F32)
        for k in range(1, fsn):
            perm = [(u, (u + k) % fsn) for u in range(fsn)]
            total = total + lax.ppermute(sm[k], "fsdp", perm).astype(F32)
        sm = total
    else:
        sm = jnp.concatenate([mine, other], axis=0)
        sm = lax.psum_scatter(sm, AXES, scatter_dimension=0, tiled=False).astype(F32)
    rs = tr(sm[7 * r:7 * r + NE]).reshape(-1)
    rs = lax.dynamic_slice_in_dim(rs, (d * fsn + f) * nrs, nrs)
    return (
        block_out,
        input_grad,
        sm[0:r],
        tr(sm[r:4 * r]),
        sm[4 * r:5 * r],
        tr(sm[5 * r:6 * r]),
        sm[6 * r:7 * r],
        rs,
        ff[:, 0],
        eg[0],
        eg[1],
        tr(ff[:, 1], (0, 2, 1)),
    )


def solution(mesh):
    dpn, fsn = mesh.shape["dp"], mesh.shape["fsdp"]
    both = ("dp", "fsdp")
    return jax.shard_map(
        functools.partial(on_device, dpn, fsn),
        mesh=mesh,
        in_specs=(
            P(both, None, None),
            P(both, None, None),
            P(both),
            P(both),
            P(both, None, None),
            P(both, None, None),
            P(both),
            P(both),
            P(both, None),
            P(both, None),
            P(both, None),
            P(None, None, both),
            P(None, None, both),
            P(both, None),
            P(None, both),
            P(both, None),
            P(None, both),
            P(both, None),
            P(both),
            P(None, both, None),
            P(None, None, both),
            P(None, None, both),
            P(None, None, both),
        ),
        out_specs=(
            P(both, None, None),
            P(both, None, None),
            P(both, None),
            P(None, both),
            P(both, None),
            P(None, both),
            P(both, None),
            P(both),
            P(None, both, None),
            P(None, None, both),
            P(None, None, both),
            P(None, None, both),
        ),
        check_vma=False,
    )
```

time: 922 us -> 566 us (0.61)
  waiting for transfers between devices: 487 us -> 156 us
  local copies, waits for them, and re-layouts: 99.8 us -> 44.7 us
  starting transfers between devices: 45.9 us -> 86.2 us
    ppermute x21 -> x25, waiting for transfers between devices: 205 us -> 79.4 us  [the longest x9 61.2 us: hop(): return lax.ppermute(v, ring[1], ring[2])]
    reduce_scatter x2 -> x0, waiting for transfers between devices: 118 us -> none  [the longest x1 118 us: on_device(): lax.psum_scatter(sm.astype(BF), AXES, scatter_dimension=0, tiled=False)]
    ppermute x22 -> x30, waiting for transfers between devices: 164 us -> 77 us  [swap(): return lax.ppermute(v, 'dp', [(a, a ^ bit) for a in range(dpn)])]
    ppermute x21 -> x25, starting transfers between devices: 32.2 us -> 62.2 us  [the longest x9 17.8 us: hop(): return lax.ppermute(v, ring[1], ring[2])]
    unnamed x79 -> x73, local copies, waits for them, and re-layouts: 37.7 us -> 11.6 us
    add x5 -> x7, other arithmetic: 12.6 us -> 1.47 us  [the longest x2 0.77 us: on_device(): mid[at:at + m] + y[0].astype(F32) + yc[0].astype(F32) + yy.astype(F32)]
    ppermute x22 -> x30, starting transfers between devices: 13.5 us -> 24 us  [swap(): return lax.ppermute(v, 'dp', [(a, a ^ bit) for a in range(dpn)])]
    slice x15 -> x14, local copies, waits for them, and re-layouts: 14.1 us -> 4.23 us  [the longest x2 3.04 us: on_device(): mid[at:at + m] + y[0].astype(F32) + yc[0].astype(F32) + yy.astype(F32)]
  transfers between devices with their start and end apart: 47 -> 56, of which waited for: 17 -> 28; matrix products, arithmetic and copies ran while one was open for 14% -> 10% of each run, Pallas kernels for 9% -> 33%
where the time goes in v2:
time: 566 us; the launch traced here: 554 us
  Pallas kernels  215 us (38%)
  waiting for transfers between devices  156 us (28%)
  starting transfers between devices  86.2 us (15%)
  local copies, waits for them, and re-layouts  44.7 us (8%)
  other arithmetic  36.7 us (6%)
  between operations  15.2 us (3%)
    ppermute x30, waiting for transfers between devices, swap(): return lax.ppermute(v, 'dp', [(a, a ^ bit) for a in range(dpn)])  77 us
    ppermute x9, waiting for transfers between devices, hop(): return lax.ppermute(v, ring[1], ring[2])  61.2 us
    pallas_call x2, Pallas kernels, backward(): pl.pallas_call(functools.partial(bwd_kernel, lo, last, r), grid_spec=pltp...  60.6 us
    pallas_call x1, Pallas kernels, expert_first(): pl.pallas_call(functools.partial(expert_first_kernel, pairs), grid_spec=p...  44.7 us
    pallas_call x2, Pallas kernels, combine(): pl.pallas_call(functools.partial(combine_kernel, lo, n), grid_spec=pltpu....  30.3 us
    pallas_call x1, Pallas kernels, expert_last(): pl.pallas_call(expert_last_kernel, grid_spec=pltpu.PrefetchScalarGridSpec...  29 us
    pallas_call x1, Pallas kernels, attention_forward(): pl.pallas_call(fwd_kernel, grid_spec=pltpu.PrefetchScalarGridSpec(num_sca...  27.4 us
    ppermute x30, starting transfers between devices, swap(): return lax.ppermute(v, 'dp', [(a, a ^ bit) for a in range(dpn)])  24 us
  transfers between devices with their start and end apart: 56, of which 28 were waited for; matrix products, arithmetic and copies ran while one was open for 10% of the time, Pallas kernels for 33%

profile of v2, /device:TPU:0, one launch (start us, length us, event | category | flops | bytes accessed | tf_op | source)
XLA Modules:
  0.0 554.5 jit_solution(9397376908477146228)
XLA Ops:
  35.6 5.0 collective-permute-done.10
  42.4 3.3 collective-permute-start.12
  45.7 8.9 %collective-permute-done.13 = bf16[16,2,24,256]{3,2,1,0:T(8,128)(2,1)S(1)} collective-permute-done((bf16[16,2,24,256]{3,2,1,0:T(8,128)(2,1)S(1)}, bf16[16,2,24,256]{3,2,1,0:T(8,128)(2,1)S(1)}, u32[]{:S(2)}, u32[]{:S(2)}) %collective-permute-start.13) | collective-permute-done | bytes 393248 | tf_op jit(solution)/shard_map/ppermute | solution.py:719
  57.2 8.8 %collective-permute-done.15 = bf16[2,2,96,1792]{3,2,1,0:T(8,128)(2,1)S(1)} collective-permute-done((bf16[2,2,96,1792]{3,2,1,0:T(8,128)(2,1)S(1)}, bf16[2,2,96,1792]{3,2,1,0:T(8,128)(2,1)S(1)}, u32[]{:S(2)}, u32[]{:S(2)}) %collective-permute-start.15) | collective-permute-done | bytes 1376288 | tf_op jit(solution)/shard_map/ppermute | solution.py:669
  67.5 27.0 %collective-permute-done.12 = bf16[2,192,1792]{2,1,0:T(8,128)(2,1)S(1)} collective-permute-done((bf16[2,192,1792]{2,1,0:T(8,128)(2,1)S(1)}, bf16[2,192,1792]{2,1,0:T(8,128)(2,1)S(1)}, u32[]{:S(2)}, u32[]{:S(2)}) %collective-permute-start.12) | collective-permute-done | bytes 1376288 | tf_op jit(solution)/shard_map/ppermute | solution.py:711
  94.5 4.5 collective-permute-done.14
  104.2 5.0 collective-permute-start.16
  117.8 3.2 collective-permute-done
  129.8 3.5 pad_maximum_fusion.2.refs_4_
  133.2 6.1 %collective-permute-done.16 = bf16[2,192,1792]{2,1,0:T(8,128)(2,1)} collective-permute-done((bf16[2,192,1792]{2,1,0:T(8,128)(2,1)S(1)}, bf16[2,192,1792]{2,1,0:T(8,128)(2,1)}, u32[]{:S(2)}, u32[]{:S(2)}) %collective-permute-start.16) | collective-permute-done | bytes 1376288 | tf_op jit(solution)/shard_map/ppermute | solution.py:711
  139.4 3.1 pad_maximum_fusion.1.refs_1_
  144.0 5.0 fusion.70
  154.9 27.4 %attention_forward.1 = (bf16[5,208,2304]{2,1,0:T(8,128)(2,1)}, bf16[5,208,768]{2,1,0:T(8,128)(2,1)}, f32[5,208,768]{2,1,0:T(8,128)}, bf16[5,208,768]{2,1,0:T(8,1...) custom-call(s32[5]{0:T(128)} %sets.5, bf16[5,197,768]{2,1,0:T(8,128)(2,1)} %x_ref.4, ...), custom_call_target="tpu_custom_call" | custom-call | flops 32199999488 | tf_op jit(solution)/shard_map/attention_forward/pallas_call | solution.py:135
  182.3 18.3 %collective-permute-done.21.refs_2_ = bf16[2,384,1792]{2,1,0:T(8,128)(2,1)} collective-permute-done((bf16[2,384,1792]{2,1,0:T(8,128)(2,1)}, bf16[2,384,1792]{2,1,0:T(8,128)(2,1)}, u32[]{:S(2)}, u32[]{:S(2)}) %collective-permute-start.21) | collective-permute-done | bytes 2752544 | tf_op jit(solution)/shard_map/ppermute | solution.py:711
  203.6 28.8 %collective-permute-done.28.refs_1_ = bf16[5,208,768]{2,1,0:T(8,128)(2,1)} collective-permute-done((bf16[5,208,768]{2,1,0:T(8,128)(2,1)}, bf16[5,208,768]{2,1,0:T(8,128)(2,1)}, u32[]{:S(2)}, u32[]{:S(2)}) %collective-permute-start.28) | collective-permute-done | bytes 1597472 | tf_op jit(solution)/shard_map/ppermute | solution.py:669
  234.9 3.3 collective-permute-done.25
  242.1 23.3 %dispatch.1 = (bf16[2,1536,896]{2,1,0:T(8,128)(2,1)}, bf16[2,1536,896]{2,1,0:T(8,128)(2,1)}, bf16[2,1536,128]{2,1,0:T(8,128)(2,1)}) custom-call(s32[10]{0:T(128)} %reshape.525.offs, s32[40]{0:T(128)} %reshape.526.firsts, s32[20]{0:T(128)} %reshape.527.sets, s32[4,2,8,256]{3,2,1,0:T(8,128)} %get-tuple-element.188.slot_ref, f32[4,2,8,256]{3,2,1,0:T(8,128)} %fusion.25.gate_ref, ...), custom_call_target="tpu_custom_call" | custom-call | flops 1150000000 | tf_op jit(solution)/shard_map/dispatch/pallas_call | solution.py:234
  267.7 44.7 %expert_first.1 = (f32[2,1536,896]{2,1,0:T(8,128)}, f32[2,1536,896]{2,1,0:T(8,128)}, bf16[3,2,2,768,128]{4,3,2,1,0:T(8,128)(2,1)}) custom-call(s32[10]{0:T(128)} %reshape.525.offs, bf16[2,1536,896]{2,1,0:T(8,128)(2,1)} %get-tuple-element.128.xa_ref, bf16[2,1536,896]{2,1,0:T(8,128)(2,1)} %get-tuple-element.129.ga_ref, ...), custom_call_target="tpu_custom_call" | custom-call | flops 64399998976 | tf_op jit(solution)/shard_map/expert_first/pallas_call | solution.py:347
  313.6 12.6 %collective-permute-start.31 = (bf16[2,2,768,128]{3,2,1,0:T(8,128)(2,1)S(1)}, bf16[2,2,768,128]{3,2,1,0:T(8,128)(2,1)S(1)}, u32[]{:S(2)}, u32[]{:S(2)}) collective-permute-start(bf16[2,2,768,128]{3,2,1,0:T(8,128)(2,1)S(1)} %slice_bitcast_fusion.3), channel_id=1, source_target_pairs={{1,0},{0,1},{3,2},{2,3},{5,4},{4,5},{7,6},{6,7},{9,8},{8,9},{11,10... | collective-permute-start | bytes 2359304 | tf_op jit(solution)/shard_map/ppermute | solution.py:796
  328.6 29.0 %expert_last.1 = (bf16[2,1536,768]{2,1,0:T(8,128)(2,1)}, bf16[2,1536,768]{2,1,0:T(8,128)(2,1)}, bf16[2,2,768,128]{3,2,1,0:T(8,128)(2,1)}, bf16[2,2,768,128]{3,2,1,0:T(8,128)(2,1)}) custom-call(s32[10]{0:T(128)} %reshape.525.offs, bf16[2,1536,896]{2,1,0:T(8,128)(2,1)} %get-tuple-element.128.xa_ref, bf16[2,1536,896]{2,1,0:T(8,128)(2,1)} %get-tuple-element.129.ga_ref, ...), custom_call_target="tpu_custom_call" | custom-call | flops 39099998208 | tf_op jit(solution)/shard_map/expert_last/pallas_call | solution.py:412
  357.7 13.6 %combine.2 = (bf16[2,208,768]{2,1,0:T(8,128)(2,1)}, bf16[2,208,768]{2,1,0:T(8,128)(2,1)}, bf16[2,2,208,768]{3,2,1,0:T(8,128)(2,1)}, bf16[2,224,768]{2,1,0:T(8,12...) custom-call(s32[10]{0:T(128)} %reshape.525.offs, s32[40]{0:T(128)} %reshape.526.firsts, ...), custom_call_target="tpu_custom_call" | custom-call | flops 13799999488 | tf_op jit(solution)/shard_map/combine/pallas_call | solution.py:479
  376.4 16.7 %combine.3 = (bf16[3,208,768]{2,1,0:T(8,128)(2,1)}, bf16[3,208,768]{2,1,0:T(8,128)(2,1)}, bf16[2,3,208,768]{3,2,1,0:T(8,128)(2,1)}, bf16[3,224,768]{2,1,0:T(8,12...) custom-call(s32[10]{0:T(128)} %reshape.525.offs, s32[40]{0:T(128)} %reshape.526.firsts, ...), custom_call_target="tpu_custom_call" | custom-call | flops 20700000256 | tf_op jit(solution)/shard_map/combine/pallas_call | solution.py:479
  402.8 3.5 collective-permute-start.35
  407.5 4.5 collective-permute-start.40
  414.7 7.9 %collective-permute-done.35.gy_ref = bf16[2,224,768]{2,1,0:T(8,128)(2,1)S(1)} collective-permute-done((bf16[2,224,768]{2,1,0:T(8,128)(2,1)S(1)}, bf16[2,224,768]{2,1,0:T(8,128)(2,1)S(1)}, u32[]{:S(2)}, u32[]{:S(2)}) %collective-permute-start.35) | collective-permute-done | bytes 688160 | tf_op jit(solution)/shard_map/ppermute | solution.py:669
  423.5 25.1 %backward.2 = (bf16[5,197,768]{2,1,0:T(8,128)(2,1)}, f32[128,5504]{1,0:T(8,128)}) custom-call(s32[5]{0:T(128)} %sets.5, s32[5]{0:T(128)} %live.3, s32[32]{0:T(128)} %fusion.43.order, bf16[5,197,768]{2,1,0:T(8,128)(2,1)} %x_ref.4, bf16[5,197,768]{2,1,0:T(8,128)(2,1)} %cot_ref.3, bf16[2,224,768]{2,1,0:T(8,128)(2,1)} %get-tuple-element.147.go_ref, ...), custom_call_target="tpu_custom_call" | custom-call | flops 27599998976 | tf_op jit(solution)/shard_map/backward/pallas_call | solution.py:634
  453.5 5.3 collective-permute-start.42
  464.2 35.5 %backward.3 = (bf16[5,197,768]{2,1,0:T(8,128)(2,1)}, bf16[16,176,128]{2,1,0:T(8,128)(2,1)}, bf16[16,176,128]{2,1,0:T(8,128)(2,1)}) custom-call(s32[5]{0:T(128)} %sets.5, s32[5]{0:T(128)} %live.3, s32[32]{0:T(128)} %fusion.43.order, bf16[5,197,768]{2,1,0:T(8,128)(2,1)} %x_ref.4, bf16[5,197,768]{2,1,0:T(8,128)(2,1)} %cot_ref.3, ...), custom_call_target="tpu_custom_call", output_to_operand_aliasing={{0}: (23, {})} | custom-call | flops 41400000512 | tf_op jit(solution)/shard_map/backward/pallas_call | solution.py:634
  510.7 4.1 collective-permute-done.54
  518.5 6.9 %collective-permute-done.45 = bf16[8,176,128]{2,1,0:T(8,128)(2,1)S(1)} collective-permute-done((bf16[8,176,128]{2,1,0:T(8,128)(2,1)S(1)}, bf16[8,176,128]{2,1,0:T(8,128)(2,1)S(1)}, u32[]{:S(2)}, u32[]{:S(2)}) %collective-permute-start.45) | collective-permute-done | bytes 360480 | tf_op jit(solution)/shard_map/ppermute | solution.py:669
  526.6 6.1 %collective-permute-start.46 = (bf16[176,128]{1,0:T(8,128)(2,1)S(1)}, bf16[176,128]{1,0:T(8,128)(2,1)S(1)}, u32[]{:S(2)}, u32[]{:S(2)}) collective-permute-start(bf16[176,128]{1,0:T(8,128)(2,1)S(1)} %get-tuple-element.224), channel_id=1, source_target_pairs={{0,1},{1,2},{2,3},{3,4},{4,5},{5,6},{6,7},{7,0},{8,9},{9,10},{10,1... | collective-permute-start | bytes 135176 | tf_op jit(solution)/shard_map/ppermute | solution.py:874
  534.3 3.3 collective-permute-start.49
  (302 shorter events, 136.0 us)
Async XLA Ops:
  7.2 136.8 %all-gather.2.cloned.1.call-start = ((), (), s32[]{:S(2)}) async-start(), calls=%async_computation | async-start | bytes 7299072 | tf_op jit(solution)/shard_map/all_gather | solution.py:685
  17.8 14.5 %collective-permute-start.6 = (bf16[2,2,96,1792]{3,2,1,0:T(8,128)(2,1)S(1)}, bf16[2,2,96,1792]{3,2,1,0:T(8,128)(2,1)S(1)}, u32[]{:S(2)}, u32[]{:S(2)}) collective-permute-start(bf16[2,2,96,1792]{3,2,1,0:T(8,128)(2,1)S(1)} %pad_maximum_fusion.5), channel_id=1, source_target_pairs={{0,8},{8,0},{16,24},{24,16},{1,9},{9,1},{17,25},{25,17},{2,10},{10... | collective-permute-start | bytes 4128776 | tf_op jit(solution)/shard_map/ppermute | solution.py:669
  28.4 12.2 %collective-permute-start.10 = (bf16[4,2,24,256]{3,2,1,0:T(8,128)(2,1)S(1)}, bf16[4,2,24,256]{3,2,1,0:T(8,128)(2,1)S(1)}, u32[]{:S(2)}, u32[]{:S(2)}) collective-permute-start(bf16[4,2,24,256]{3,2,1,0:T(8,128)(2,1)S(1)} %pad_maximum_fusion.17), channel_id=1, source_target_pairs={{0,4},{1,5},{2,6},{3,7},{4,0},{5,1},{6,2},{7,3},{8,12},{9,13},{10,... | collective-permute-start | bytes 294920 | tf_op jit(solution)/shard_map/ppermute | solution.py:714
  32.5 33.5 %collective-permute-start.15 = (bf16[2,2,96,1792]{3,2,1,0:T(8,128)(2,1)S(1)}, bf16[2,2,96,1792]{3,2,1,0:T(8,128)(2,1)S(1)}, u32[]{:S(2)}, u32[]{:S(2)}) collective-permute-start(bf16[2,2,96,1792]{3,2,1,0:T(8,128)(2,1)S(1)} %pad_maximum_fusion.7), channel_id=1, source_target_pairs={{0,16},{8,24},{16,0},{24,8},{1,17},{9,25},{17,1},{25,9},{2,18},{10... | collective-permute-start | bytes 4128776 | tf_op jit(solution)/shard_map/ppermute | solution.py:669
  40.8 13.8 %collective-permute-start.13 = (bf16[16,2,24,256]{3,2,1,0:T(8,128)(2,1)S(1)}, bf16[16,2,24,256]{3,2,1,0:T(8,128)(2,1)S(1)}, u32[]{:S(2)}, u32[]{:S(2)}) collective-permute-start(bf16[16,2,24,256]{3,2,1,0:T(8,128)(2,1)S(1)} %constant_dynamic-update-slice_fusion), channel_id=1, source_target_pairs={{0,1},{1,0},{2,3},{3,2},{4,5},{5,4},{6,7},{7,6},{8,9},{9,8},{10,11... | collective-permute-start | bytes 1179656 | tf_op jit(solution)/shard_map/ppermute | solution.py:719
  42.4 52.1 %collective-permute-start.12 = (bf16[2,192,1792]{2,1,0:T(8,128)(2,1)S(1)}, bf16[2,192,1792]{2,1,0:T(8,128)(2,1)S(1)}, u32[]{:S(2)}, u32[]{:S(2)}) collective-permute-start(bf16[2,192,1792]{2,1,0:T(8,128)(2,1)S(1)} %bitcast.181), channel_id=1, source_target_pairs={{0,2},{1,3},{2,4},{3,5},{4,6},{5,7},{6,0},{7,1},{8,10},{9,11},{10,... | collective-permute-start | bytes 4128776 | tf_op jit(solution)/shard_map/ppermute | solution.py:711
  54.6 44.4 %collective-permute-start.14 = (bf16[2,192,1792]{2,1,0:T(8,128)(2,1)S(1)}, bf16[2,192,1792]{2,1,0:T(8,128)(2,1)S(1)}, u32[]{:S(2)}, u32[]{:S(2)}) collective-permute-start(bf16[2,192,1792]{2,1,0:T(8,128)(2,1)S(1)} %bitcast.182), channel_id=1, source_target_pairs={{0,1},{1,0},{2,3},{3,2},{4,5},{5,4},{6,7},{7,6},{8,9},{9,8},{10,11... | collective-permute-start | bytes 4128776 | tf_op jit(solution)/shard_map/ppermute | solution.py:711
  66.0 45.8 %collective-permute-start.18 = (bf16[5,197,768]{2,1,0:T(8,128)(2,1)}, bf16[5,197,768]{2,1,0:T(8,128)(2,1)}, u32[]{:S(2)}, u32[]{:S(2)}) collective-permute-start(bf16[5,197,768]{2,1,0:T(8,128)(2,1)} %cot_ref.3), channel_id=1, source_target_pairs={{0,16},{8,24},{16,0},{24,8},{1,17},{9,25},{17,1},{25,9},{2,18},{10... | collective-permute-start | bytes 4538888 | tf_op jit(solution)/shard_map/ppermute | solution.py:669
  100.1 29.6 %collective-permute-start.17 = (bf16[2,192,1792]{2,1,0:T(8,128)(2,1)S(1)}, bf16[2,192,1792]{2,1,0:T(8,128)(2,1)}, u32[]{:S(2)}, u32[]{:S(2)}) collective-permute-start(bf16[2,192,1792]{2,1,0:T(8,128)(2,1)S(1)} %bitcast.192), channel_id=1, source_target_pairs={{0,1},{1,0},{2,3},{3,2},{4,5},{5,4},{6,7},{7,6},{8,9},{9,8},{10,11... | collective-permute-start | bytes 4128776 | tf_op jit(solution)/shard_map/ppermute | solution.py:711
  104.2 35.2 %collective-permute-start.16 = (bf16[2,192,1792]{2,1,0:T(8,128)(2,1)S(1)}, bf16[2,192,1792]{2,1,0:T(8,128)(2,1)}, u32[]{:S(2)}, u32[]{:S(2)}) collective-permute-start(bf16[2,192,1792]{2,1,0:T(8,128)(2,1)S(1)} %bitcast.193), channel_id=1, source_target_pairs={{0,2},{1,3},{2,4},{3,5},{4,6},{5,7},{6,0},{7,1},{8,10},{9,11},{10,... | collective-permute-start | bytes 4128776 | tf_op jit(solution)/shard_map/ppermute | solution.py:711
  109.2 34.7 %collective-permute-start.19 = (bf16[5,197,768]{2,1,0:T(8,128)(2,1)}, bf16[5,197,768]{2,1,0:T(8,128)(2,1)}, u32[]{:S(2)}, u32[]{:S(2)}) collective-permute-start(bf16[5,197,768]{2,1,0:T(8,128)(2,1)} %cot_ref.3), channel_id=1, source_target_pairs={{0,8},{8,0},{16,24},{24,16},{1,9},{9,1},{17,25},{25,17},{2,10},{10... | collective-permute-start | bytes 4538888 | tf_op jit(solution)/shard_map/ppermute | solution.py:669
  111.8 32.1 %collective-permute-start.20 = (bf16[5,197,768]{2,1,0:T(8,128)(2,1)}, bf16[5,197,768]{2,1,0:T(8,128)(2,1)}, u32[]{:S(2)}, u32[]{:S(2)}) collective-permute-start(bf16[5,197,768]{2,1,0:T(8,128)(2,1)} %collective-permute-done.18.refs_5_.refs_1_), channel_id=1, source_target_pairs={{0,8},{8,0},{16,24},{24,16},{1,9},{9,1},{17,25},{25,17},{2,10},{10... | collective-permute-start | bytes 4538888 | tf_op jit(solution)/shard_map/ppermute | solution.py:669
  142.4 58.2 %collective-permute-start.21 = (bf16[2,384,1792]{2,1,0:T(8,128)(2,1)}, bf16[2,384,1792]{2,1,0:T(8,128)(2,1)}, u32[]{:S(2)}, u32[]{:S(2)}) collective-permute-start(bf16[2,384,1792]{2,1,0:T(8,128)(2,1)} %pad_maximum_fusion.1.refs_1_), channel_id=1, source_target_pairs={{0,2},{1,3},{2,4},{3,5},{4,6},{5,7},{6,0},{7,1},{8,10},{9,11},{10,... | collective-permute-start | bytes 8257544 | tf_op jit(solution)/shard_map/ppermute | solution.py:711
  143.3 58.9 %collective-permute-start.22 = (bf16[2,384,1792]{2,1,0:T(8,128)(2,1)}, bf16[2,384,1792]{2,1,0:T(8,128)(2,1)}, u32[]{:S(2)}, u32[]{:S(2)}) collective-permute-start(bf16[2,384,1792]{2,1,0:T(8,128)(2,1)} %pad_maximum_fusion.1.refs_1_), channel_id=1, source_target_pairs={{0,1},{1,0},{2,3},{3,2},{4,5},{5,4},{6,7},{7,6},{8,9},{9,8},{10,11... | collective-permute-start | bytes 8257544 | tf_op jit(solution)/shard_map/ppermute | solution.py:711
  202.1 30.2 %collective-permute-start.28 = (bf16[5,208,768]{2,1,0:T(8,128)(2,1)}, bf16[5,208,768]{2,1,0:T(8,128)(2,1)}, u32[]{:S(2)}, u32[]{:S(2)}) collective-permute-start(bf16[5,208,768]{2,1,0:T(8,128)(2,1)} %get-tuple-element.121.refs_0_.x2_ref), channel_id=1, source_target_pairs={{0,16},{8,24},{16,0},{24,8},{1,17},{9,25},{17,1},{25,9},{2,18},{10... | collective-permute-start | bytes 4792328 | tf_op jit(solution)/shard_map/ppermute | solution.py:669
  202.6 62.8 %collective-permute-start.23 = (bf16[2,384,1792]{2,1,0:T(8,128)(2,1)}, bf16[2,384,1792]{2,1,0:T(8,128)(2,1)}, u32[]{:S(2)}, u32[]{:S(2)}) collective-permute-start(bf16[2,384,1792]{2,1,0:T(8,128)(2,1)} %collective-permute-done.21.refs_2_), channel_id=1, source_target_pairs={{0,2},{1,3},{2,4},{3,5},{4,6},{5,7},{6,0},{7,1},{8,10},{9,11},{10,... | collective-permute-start | bytes 8257544 | tf_op jit(solution)/shard_map/ppermute | solution.py:711
  202.9 62.5 %collective-permute-start.24 = (bf16[2,384,1792]{2,1,0:T(8,128)(2,1)}, bf16[2,384,1792]{2,1,0:T(8,128)(2,1)}, u32[]{:S(2)}, u32[]{:S(2)}) collective-permute-start(bf16[2,384,1792]{2,1,0:T(8,128)(2,1)} %collective-permute-done.21.refs_2_), channel_id=1, source_target_pairs={{0,1},{1,0},{2,3},{3,2},{4,5},{5,4},{6,7},{7,6},{8,9},{9,8},{10,11... | collective-permute-start | bytes 8257544 | tf_op jit(solution)/shard_map/ppermute | solution.py:711
  203.6 38.5 %collective-permute-start.29 = (bf16[5,208,768]{2,1,0:T(8,128)(2,1)}, bf16[5,208,768]{2,1,0:T(8,128)(2,1)}, u32[]{:S(2)}, u32[]{:S(2)}) collective-permute-start(bf16[5,208,768]{2,1,0:T(8,128)(2,1)} %get-tuple-element.121.refs_0_.x2_ref), channel_id=1, source_target_pairs={{0,8},{8,0},{16,24},{24,16},{1,9},{9,1},{17,25},{25,17},{2,10},{10... | collective-permute-start | bytes 4792328 | tf_op jit(solution)/shard_map/ppermute | solution.py:669
  265.4 61.6 %collective-permute-start.32 = (bf16[2,384,1792]{2,1,0:T(8,128)(2,1)}, bf16[2,384,1792]{2,1,0:T(8,128)(2,1)S(1)}, u32[]{:S(2)}, u32[]{:S(2)}) collective-permute-start(bf16[2,384,1792]{2,1,0:T(8,128)(2,1)} %collective-permute-done.23.refs_3_), channel_id=1, source_target_pairs={{0,1},{1,0},{2,3},{3,2},{4,5},{5,4},{6,7},{7,6},{8,9},{9,8},{10,11... | collective-permute-start | bytes 8257544 | tf_op jit(solution)/shard_map/ppermute | solution.py:711
  313.6 44.1 %collective-permute-start.31 = (bf16[2,2,768,128]{3,2,1,0:T(8,128)(2,1)S(1)}, bf16[2,2,768,128]{3,2,1,0:T(8,128)(2,1)S(1)}, u32[]{:S(2)}, u32[]{:S(2)}) collective-permute-start(bf16[2,2,768,128]{3,2,1,0:T(8,128)(2,1)S(1)} %slice_bitcast_fusion.3), channel_id=1, source_target_pairs={{1,0},{0,1},{3,2},{2,3},{5,4},{4,5},{7,6},{6,7},{9,8},{8,9},{11,10... | collective-permute-start | bytes 2359304 | tf_op jit(solution)/shard_map/ppermute | solution.py:796
  393.1 19.4 %collective-permute-start.34 = (bf16[2,3,224,768]{3,2,1,0:T(8,128)(2,1)}, bf16[2,3,224,768]{3,2,1,0:T(8,128)(2,1)}, u32[]{:S(2)}, u32[]{:S(2)}) collective-permute-start(bf16[2,3,224,768]{3,2,1,0:T(8,128)(2,1)} %get-tuple-element.145), channel_id=1, source_target_pairs={{0,8},{8,0},{16,24},{24,16},{1,9},{9,1},{17,25},{25,17},{2,10},{10... | collective-permute-start | bytes 6193160 | tf_op jit(solution)/shard_map/ppermute | solution.py:669
  402.8 19.8 %collective-permute-start.35 = (bf16[2,224,768]{2,1,0:T(8,128)(2,1)S(1)}, bf16[2,224,768]{2,1,0:T(8,128)(2,1)S(1)}, u32[]{:S(2)}, u32[]{:S(2)}) collective-permute-start(bf16[2,224,768]{2,1,0:T(8,128)(2,1)S(1)} %fusion.7), channel_id=1, source_target_pairs={{0,16},{8,24},{16,0},{24,8},{1,17},{9,25},{17,1},{25,9},{2,18},{10... | collective-permute-start | bytes 2064392 | tf_op jit(solution)/shard_map/ppermute | solution.py:669
  407.5 41.1 %collective-permute-start.40 = (bf16[2,2,1152,128]{3,2,1,0:T(8,128)(2,1)}, bf16[2,2,1152,128]{3,2,1,0:T(8,128)(2,1)}, u32[]{:S(2)}, u32[]{:S(2)}) collective-permute-start(bf16[2,2,1152,128]{3,2,1,0:T(8,128)(2,1)} %pad_maximum_fusion.8), channel_id=1, source_target_pairs={{1,0},{0,1},{3,2},{2,3},{5,4},{4,5},{7,6},{6,7},{9,8},{8,9},{11,10... | collective-permute-start | bytes 3538952 | tf_op jit(solution)/shard_map/ppermute | solution.py:798
  411.9 36.6 %collective-permute-start.37 = (bf16[2,2,208,768]{3,2,1,0:T(8,128)(2,1)}, bf16[2,2,208,768]{3,2,1,0:T(8,128)(2,1)}, u32[]{:S(2)}, u32[]{:S(2)}) collective-permute-start(bf16[2,2,208,768]{3,2,1,0:T(8,128)(2,1)} %get-tuple-element.155), channel_id=1, source_target_pairs={{0,8},{8,0},{16,24},{24,16},{1,9},{9,1},{17,25},{25,17},{2,10},{10... | collective-permute-start | bytes 3833864 | tf_op jit(solution)/shard_map/ppermute | solution.py:669
  411.9 36.6 %collective-permute-start.38 = (bf16[2,3,208,768]{3,2,1,0:T(8,128)(2,1)}, bf16[2,3,208,768]{3,2,1,0:T(8,128)(2,1)}, u32[]{:S(2)}, u32[]{:S(2)}) collective-permute-start(bf16[2,3,208,768]{3,2,1,0:T(8,128)(2,1)} %get-tuple-element.156), channel_id=1, source_target_pairs={{0,8},{8,0},{16,24},{24,16},{1,9},{9,1},{17,25},{25,17},{2,10},{10... | collective-permute-start | bytes 5750792 | tf_op jit(solution)/shard_map/ppermute | solution.py:669
  413.9 34.6 %collective-permute-start.36 = (bf16[3,224,768]{2,1,0:T(8,128)(2,1)S(1)}, bf16[3,224,768]{2,1,0:T(8,128)(2,1)}, u32[]{:S(2)}, u32[]{:S(2)}) collective-permute-start(bf16[3,224,768]{2,1,0:T(8,128)(2,1)S(1)} %fusion.1), channel_id=1, source_target_pairs={{0,16},{8,24},{16,0},{24,8},{1,17},{9,25},{17,1},{25,9},{2,18},{10... | collective-permute-start | bytes 3096584 | tf_op jit(solution)/shard_map/ppermute | solution.py:669
  452.7 49.4 %collective-permute-start.43 = (bf16[2,2,480,128]{3,2,1,0:T(8,128)(2,1)}, bf16[2,2,480,128]{3,2,1,0:T(8,128)(2,1)}, u32[]{:S(2)}, u32[]{:S(2)}) collective-permute-start(bf16[2,2,480,128]{3,2,1,0:T(8,128)(2,1)} %pad_maximum_fusion.12), channel_id=1, source_target_pairs={{0,2},{1,3},{2,4},{3,5},{4,6},{5,7},{6,0},{7,1},{8,10},{9,11},{10,... | collective-permute-start | bytes 1474568 | tf_op jit(solution)/shard_map/ppermute | solution.py:844
  453.5 48.6 %collective-permute-start.42 = (bf16[2,2,480,128]{3,2,1,0:T(8,128)(2,1)}, bf16[2,2,480,128]{3,2,1,0:T(8,128)(2,1)}, u32[]{:S(2)}, u32[]{:S(2)}) collective-permute-start(bf16[2,2,480,128]{3,2,1,0:T(8,128)(2,1)} %pad_maximum_fusion.11), channel_id=1, source_target_pairs={{0,4},{1,5},{2,6},{3,7},{4,0},{5,1},{6,2},{7,3},{8,12},{9,13},{10,... | collective-permute-start | bytes 1474568 | tf_op jit(solution)/shard_map/ppermute | solution.py:844
  459.7 42.4 %collective-permute-start.41 = (bf16[2,2,480,128]{3,2,1,0:T(8,128)(2,1)}, bf16[2,2,480,128]{3,2,1,0:T(8,128)(2,1)}, u32[]{:S(2)}, u32[]{:S(2)}) collective-permute-start(bf16[2,2,480,128]{3,2,1,0:T(8,128)(2,1)} %pad_maximum_fusion.10), channel_id=1, source_target_pairs={{0,6},{1,7},{2,0},{3,1},{4,2},{5,3},{6,4},{7,5},{8,14},{9,15},{10,... | collective-permute-start | bytes 1474568 | tf_op jit(solution)/shard_map/ppermute | solution.py:844
  463.8 38.4 %collective-permute-start.39 = (bf16[5,208,768]{2,1,0:T(8,128)(2,1)}, bf16[5,208,768]{2,1,0:T(8,128)(2,1)S(1)}, u32[]{:S(2)}, u32[]{:S(2)}) collective-permute-start(bf16[5,208,768]{2,1,0:T(8,128)(2,1)} %pad_maximum_fusion.4), channel_id=1, source_target_pairs={{0,16},{8,24},{16,0},{24,8},{1,17},{9,25},{17,1},{25,9},{2,18},{10... | collective-permute-start | bytes 4792328 | tf_op jit(solution)/shard_map/ppermute | solution.py:669
  504.6 10.9 %collective-permute-start.44 = (bf16[16,176,128]{2,1,0:T(8,128)(2,1)}, bf16[16,176,128]{2,1,0:T(8,128)(2,1)}, u32[]{:S(2)}, u32[]{:S(2)}) collective-permute-start(bf16[16,176,128]{2,1,0:T(8,128)(2,1)} %get-tuple-element.177), channel_id=1, source_target_pairs={{0,8},{8,0},{16,24},{24,16},{1,9},{9,1},{17,25},{25,17},{2,10},{10... | collective-permute-start | bytes 2162696 | tf_op jit(solution)/shard_map/ppermute | solution.py:669
  526.6 13.5 %collective-permute-start.46 = (bf16[176,128]{1,0:T(8,128)(2,1)S(1)}, bf16[176,128]{1,0:T(8,128)(2,1)S(1)}, u32[]{:S(2)}, u32[]{:S(2)}) collective-permute-start(bf16[176,128]{1,0:T(8,128)(2,1)S(1)} %get-tuple-element.224), channel_id=1, source_target_pairs={{0,1},{1,2},{2,3},{3,4},{4,5},{5,6},{6,7},{7,0},{8,9},{9,10},{10,1... | collective-permute-start | bytes 135176 | tf_op jit(solution)/shard_map/ppermute | solution.py:874
  (57 other events, 640.0 us)
Sparse Core Ops, SparseCore 0:
  15.7 105.7 all-gather.1
